TPU v7x, 512 devices: a whole 4x8x8 slice. The times are simulated.
512 devices in a mesh: dp: 32 (over z, x), seq: 16 (over y, core).
Axes of the slice: x: 4, y: 8, z: 8, core: 2. Of those that a mesh axis runs over, the one named last changes fastest.
Arguments:
- tokens: bfloat16 [32, 8192, 2048], P('dp', 'seq'), may hold values from -60 to 60
- in_gain: float32 [2048], replicated, may hold values from 0.1 to 1.9
- in_weight: bfloat16 [2048, 2304], P('dp'), may hold values from -0.125 to 0.125
- conv_weight: float32 [4, 2304], replicated, may hold values from -5 to 5
- conv_bias: float32 [2304], replicated, may hold values from -3 to 3
- log_decay: float32 [32, 32, 8192], P('dp', None, 'seq'), may hold values from -0.9 to 0
- skip: float32 [32], replicated, may hold values from 0.05 to 1
- out_gain: float32 [2048], replicated, may hold values from 0.1 to 1.9
- scan_order: int32 [512], replicated, may hold values from 0 to 511, each once
Outputs:
- regrouped: bfloat16 [32, 8192, 2048], P('dp', 'seq')
Inputs may be any that keep to these rules, and one draw needn't show every extreme that they name: Each of the 512 positions appears once; the q-th position of a frame in the next layer's scan is scan_order[q].
All inputs are finite; a program needn't handle non-finite values.
Results may differ from a plain program's by a relative error of at most 0.008.
Values may be sent and summed in bfloat16 or wider, within the bound.
No kernel may reach another device: no remote copies, remote signals or barrier semaphores. Data moves between devices by JAX's collectives and lax.ppermute only.
A program may use at most 128 MiB of HBM per device.

v0:
```python
import jax
import jax.numpy as jnp
from jax import lax
from jax.sharding import PartitionSpec as P

HALF_HEADS = 32
HEADDIM = 64
STATE = 128
GROUP = 128
POSITIONS = 512


def passed_along(block, axis, distance):
    devices = range(lax.axis_size(axis))
    route = [(i - distance, i) for i in devices if i - distance in devices]
    return lax.ppermute(block, axis, route)


def entering_2(part, axis, combine, identity):
    place = lax.axis_index(axis)
    gathered = jax.tree.map(lambda a: lax.all_gather(a, axis), part)
    state = jax.tree.map(lambda a, e: jnp.zeros_like(a) + jnp.asarray(e, a.dtype), part, identity)

    def one(step, state):
        return combine(
            state, jax.tree.map(lambda a: lax.dynamic_index_in_dim(a, step, 0, False), gathered)
        )

    return lax.fori_loop(0, place, one, state)


def project(operand, in_weight):
    whole_weight = lax.all_gather(in_weight, "dp", axis=0, tiled=True)
    return jnp.dot(operand, whole_weight, preferred_element_type=jnp.float32).astype(jnp.bfloat16)


def combine_states(earlier, later):
    return (earlier[0] * later[0], later[0][:, None, None] * earlier[1] + later[1])


def on_device(
    tokens, in_gain, in_weight, conv_weight, conv_bias, log_decay, skip, out_gain, scan_order
):
    own_tokens = tokens[0]
    token_count = own_tokens.shape[0]
    tap_count = conv_weight.shape[0]
    margin = tap_count - 1
    widened = own_tokens.astype(jnp.float32)
    inverse = lax.rsqrt(jnp.mean(widened * widened, axis=1, keepdims=True) + 1e-05)
    normed = (widened * inverse * in_gain[None, :]).astype(jnp.bfloat16)
    projected = project(normed, in_weight)
    earlier_rows = passed_along(projected[token_count - margin :], "seq", 1)
    extended = jnp.concatenate([earlier_rows, projected], axis=0)
    mixed_pre = conv_bias[None, :] + conv_weight[0][None, :] * extended[0:token_count].astype(
        jnp.float32
    )
    for offset in range(1, tap_count):
        mixed_pre = mixed_pre + conv_weight[offset][None, :] * extended[
            offset : offset + token_count
        ].astype(jnp.float32)
    mixed = jax.nn.silu(mixed_pre).astype(jnp.bfloat16)
    inner_width = HALF_HEADS * HEADDIM
    x_heads = mixed[:, :inner_width].reshape(token_count, HALF_HEADS, HEADDIM)
    b_vectors = mixed[:, inner_width : inner_width + STATE]
    c_vectors = mixed[:, inner_width + STATE :]
    own_decay = log_decay[0]
    block_count = token_count // GROUP
    places = jnp.arange(GROUP)
    causal = places[None, :] <= places[:, None]
    intra_parts = []
    block_states = []
    closings = []
    cumulatives = []
    device_state = jnp.zeros((HALF_HEADS, HEADDIM, STATE), jnp.float32)
    device_decay = jnp.ones((HALF_HEADS,), jnp.float32)
    for block_index in range(block_count):
        first_row = block_index * GROUP
        end_row = first_row + GROUP
        x_block = x_heads[first_row:end_row]
        b_block = b_vectors[first_row:end_row]
        c_block = c_vectors[first_row:end_row]
        decay_block = own_decay[:, first_row:end_row]
        cumulative = jnp.cumsum(decay_block, axis=1)
        step_size = -decay_block
        scores = lax.dot_general(
            c_block, b_block, (((1,), (1,)), ((), ())), preferred_element_type=jnp.float32
        )
        log_gap = cumulative[:, :, None] - cumulative[:, None, :]
        decay_mask = jnp.exp(jnp.where(causal[None], log_gap, -1e30))
        weights = (scores[None] * decay_mask * step_size[:, None, :]).astype(jnp.bfloat16)
        intra_parts.append(
            jnp.einsum("hts,shp->thp", weights, x_block, preferred_element_type=jnp.float32)
        )
        closing = cumulative[:, -1:]
        scaled = (
            (jnp.exp(closing - cumulative) * step_size).T[:, :, None] * x_block.astype(jnp.float32)
        ).astype(jnp.bfloat16)
        block_state = jnp.einsum("shp,sn->hpn", scaled, b_block, preferred_element_type=jnp.float32)
        fading = jnp.exp(closing[:, 0])
        device_state = fading[:, None, None] * device_state + block_state
        device_decay = device_decay * fading
        block_states.append(block_state)
        closings.append(fading)
        cumulatives.append(cumulative)
    carried = entering_2(
        (device_decay, device_state),
        "seq",
        combine_states,
        (jnp.ones_like(device_decay), jnp.zeros_like(device_state)),
    )
    entering = carried[1]
    outputs = []
    for block_index in range(block_count):
        first_row = block_index * GROUP
        c_block = c_vectors[first_row : first_row + GROUP]
        inter = jnp.einsum(
            "tn,hpn->thp",
            c_block,
            entering.astype(jnp.bfloat16),
            preferred_element_type=jnp.float32,
        )
        inter = inter * jnp.exp(cumulatives[block_index]).T[:, :, None]
        outputs.append(intra_parts[block_index] + inter)
        entering = closings[block_index][:, None, None] * entering + block_states[block_index]
    ssm_out = jnp.concatenate(outputs, axis=0) + skip[None, :, None] * x_heads.astype(jnp.float32)
    head_scale = lax.rsqrt(jnp.mean(ssm_out * ssm_out, axis=2, keepdims=True) + 1e-05)
    normalized = (ssm_out * head_scale * out_gain.reshape(HALF_HEADS, HEADDIM)[None]).astype(
        jnp.bfloat16
    )
    frames_here = token_count // POSITIONS
    framed = normalized.reshape(frames_here, POSITIONS, inner_width)
    picked = jnp.take(framed, scan_order, axis=1).transpose(1, 0, 2)
    seq_count = lax.axis_size("seq")
    outgoing = picked.reshape(seq_count, POSITIONS // seq_count, frames_here, inner_width)
    arrived = lax.all_to_all(outgoing, "seq", split_axis=0, concat_axis=2, tiled=True)
    return arrived.reshape(1, token_count, inner_width)


def solution(mesh):
    in_specs = (
        P("dp", "seq", None),
        P(),
        P("dp", None),
        P(),
        P(),
        P("dp", None, "seq"),
        P(),
        P(),
        P(),
    )
    out_specs = P("dp", "seq", None)
    return jax.shard_map(
        on_device, mesh=mesh, in_specs=in_specs, out_specs=out_specs, check_vma=False
    )
```

profile of v0, /device:TPU:1, one launch (start us, length us, event | category | flops | bytes accessed | tf_op | source)
XLA Modules:
  0.0 378.1 jit_solution(2298110102641624891)
XLA Ops:
  6.5 0.7 all-gather.5.cloned.1.call-update
  7.3 0.8 fusion.86
  9.2 0.7 slice_reduce_fusion
  10.5 2.1 fusion
  12.6 0.7 slice_negate_fusion.3
  13.3 111.3 %all-gather.5.cloned.1.call-done = bf16[2048,2304]{1,0:T(8,128)(2,1)} async-done(((bf16[64,2304]{1,0:T(8,128)(2,1)}), bf16[2048,2304]{1,0:T(8,128)(2,1)}) %all-gather.5.cloned.1.call-update) | async-done | bytes 9437200 | tf_op jit(solution)/shard_map/all_gather | solution.py:33
  124.6 9.1 %convolution_convert_fusion = bf16[512,2304]{1,0:T(8,128)(2,1)S(1)} fusion(bf16[2048,2304]{1,0:T(8,128)(2,1)} %all-gather.5.cloned.1.call-done, bf16[1,512,2048]{2,1,0:T(8,128)(2,1)S(1)} %copy-done.15, f32[2048]{0:T(1024)S(1)} %copy-done.41, f32[512]{0:T(512)S(1)} %add_rsqrt_fusion.1), kind=kOutput, calls=%fused_computation.6 | convolution fusion | flops 4837212160 | bytes 13903872 | tf_op jit(solution)/shard_map/dot_general | solution.py:34
  133.8 4.4 %collective-permute-start = (bf16[3,2304]{1,0:T(4,128)(2,1)S(1)}, bf16[3,2304]{1,0:T(4,128)(2,1)S(1)}, u32[]{:S(2)}, u32[]{:S(2)}) collective-permute-start(bf16[3,2304]{1,0:T(4,128)(2,1)S(1)} %slice.152), channel_id=1, source_target_pairs={{0,1},{1,2},{2,3},{3,4},{4,5},{5,6},{6,7},{7,8},{8,9},{9,10},{10,1... | collective-permute-start | bytes 41480 | tf_op jit(solution)/shard_map/ppermute | solution.py:16
  140.0 3.4 multiply_convert_fusion
  143.4 1.5 fusion.85
  144.9 2.0 copy.46
  146.9 1.0 copy.47
  148.2 1.3 copy.49
  149.6 1.3 fusion.42
  150.9 1.7 fusion.43
  153.0 0.7 copy-done.12
  154.1 1.4 convolution_add_fusion
  155.5 1.3 dynamic-slice
  157.4 0.8 dynamic-update-slice
  158.2 24.8 %all-reduce = f32[512]{0:T(512)S(1)} all-reduce(f32[512]{0:T(512)S(1)} %dynamic-update-slice), channel_id=2, replica_groups=mesh['dp'=32,'seq'=16] {'seq'}, use_global_device_ids=true, to_apply=%add | all-reduce | flops 512 | bytes 4096
  183.6 0.7 mul.419
  185.1 0.7 compare_and_fusion
  188.3 2.5 slice_convert_fusion
  190.8 5.4 %copy.54 = f32[512,2048]{0,1:T(8,128)} copy(f32[512,2048]{1,0:T(8,128)} %slice_convert_fusion) | data formatting | bytes 8388608 | tf_op jit(solution)/shard_map/convert_element_type | solution.py:125
  196.8 3.0 convolution_bitcast_fusion.3
  199.8 1.9 convolution_bitcast_fusion.2
  201.7 1.9 convolution_bitcast_fusion.1
  203.6 1.9 convolution_bitcast_fusion
  205.5 45.8 %all-gather.7.cloned.1.call-done = f32[512,64,128]{2,1,0:T(8,128)} async-done(((f32[32,64,128]{2,1,0:T(8,128)}), f32[512,64,128]{2,1,0:T(8,128)}) %all-gather.7.cloned.1.call-update) | async-done | bytes 16777232 | tf_op jit(solution)/shard_map/all_gather | solution.py:21
  251.4 2.3 while.12
  252.1 1.4 bitcast_add_fusion.2
  253.8 1.9 multiply_add_fusion
  256.0 0.9 copy-done.2
  256.9 0.7 copy-done.17
  258.4 1.2 copy-done.11
  260.3 0.9 copy-done.3
  261.2 1.0 fusion.7
  262.2 2.5 mul.426
  264.7 5.5 %copy.55 = f32[512,2048]{1,0:T(8,128)} copy(f32[512,2048]{0,1:T(8,128)} %bitcast.90) | data formatting | bytes 8388608 | tf_op jit(solution)/shard_map/mul | solution.py:127
  270.2 1.3 copy.50
  271.6 1.3 copy.51
  272.9 1.3 copy.52
  274.2 1.3 copy.53
  275.6 4.3 %fusion.5 = bf16[512,2048]{1,0:T(8,128)(2,1)S(1)} fusion(f32[512,2048]{1,0:T(8,128)} %copy.55, f32[128,2048]{1,0:T(8,128)} %copy.53, f32[128,2048]{1,0:T(8,128)} %copy.52, f32[128,2048]{1,0:T(8,128)} %copy.51, f32[128,2048]{1,0:T(8,128)S(1)} %copy-done.13, f32[2048]{0:T(1024)S(1)} %copy-done.31, f32[2048]{0:T(1024)S(1)} %copy-done.23, ...), kind=kLoop, calls=%fused_computation.13 | loop fusion | flops 9437184 | bytes 12599296 | tf_op jit(solution)/shard_map/convert_element_type | solution.py:127
  279.9 3.3 gather_fusion
  283.2 1.8 broadcast_select_fusion
  285.1 83.7 %all_to_all.15 = bf16[16,32,1,2048]{3,1,2,0:T(8,128)(2,1)S(1)} all-to-all(bf16[16,32,1,2048]{3,1,2,0:T(8,128)(2,1)S(1)} %broadcast_select_fusion), channel_id=1, replica_groups=mesh['dp'=32,'seq'=16] {'seq'}, dimensions={0} | all-to-all | bytes 4194304 | tf_op jit(solution)/shard_map/all_to_all | solution.py:135
  368.8 2.5 copy.57
  (114 shorter events, 11.5 us)
Async XLA Ops:
  6.5 6.1 %copy-start.20 = (f32[1,32,512]{2,1,0:T(8,128)S(1)}, f32[1,32,512]{2,1,0:T(8,128)}, u32[]{:S(2)}) copy-start(f32[1,32,512]{2,1,0:T(8,128)} %param.16) | copy-start | bytes 196612
  6.5 118.1 %copy-start.15 = (bf16[1,512,2048]{2,1,0:T(8,128)(2,1)S(1)}, bf16[1,512,2048]{2,1,0:T(8,128)(2,1)}, u32[]{:S(2)}) copy-start(bf16[1,512,2048]{2,1,0:T(8,128)(2,1)} %param.11) | copy-start | bytes 6291460
  6.5 118.1 %copy-start.41 = (f32[2048]{0:T(1024)S(1)}, f32[2048]{0:T(1024)}, u32[]{:S(2)}) copy-start(f32[2048]{0:T(1024)} %param.12) | copy-start | bytes 24580
  6.5 118.1 %all-gather.5.cloned.1.call-start = ((), (), s32[]{:S(2)}) async-start(), calls=%async_computation.1 | async-start | bytes 9732096 | tf_op jit(solution)/shard_map/all_gather | solution.py:33
  7.3 244.0 %all-gather.7.cloned.1.call-start = ((), (), s32[]{:S(2)}) async-start(), calls=%async_computation.2 | async-start | bytes 17825792 | tf_op jit(solution)/shard_map/all_gather | solution.py:21
  13.3 124.8 %copy-start.22 = (f32[4,2304]{1,0:T(4,128)S(1)}, f32[4,2304]{1,0:T(4,128)}, u32[]{:S(2)}) copy-start(f32[4,2304]{1,0:T(4,128)} %param.14) | copy-start | bytes 110596
  13.3 126.7 %copy-start.29 = (f32[2304]{0:T(1024)S(1)}, f32[2304]{0:T(1024)}, u32[]{:S(2)}) copy-start(f32[2304]{0:T(1024)} %param.15) | copy-start | bytes 27652
  133.8 6.2 %collective-permute-start = (bf16[3,2304]{1,0:T(4,128)(2,1)S(1)}, bf16[3,2304]{1,0:T(4,128)(2,1)S(1)}, u32[]{:S(2)}, u32[]{:S(2)}) collective-permute-start(bf16[3,2304]{1,0:T(4,128)(2,1)S(1)} %slice.152), channel_id=1, source_target_pairs={{0,1},{1,2},{2,3},{3,4},{4,5},{5,6},{6,7},{7,8},{8,9},{9,10},{10,1... | collective-permute-start | bytes 41480 | tf_op jit(solution)/shard_map/ppermute | solution.py:16
  143.3 115.0 %copy-start = (bf16[512,2304]{1,0:T(8,128)(2,1)}, bf16[512,2304]{1,0:T(8,128)(2,1)S(1)}, u32[]{:S(2)}) copy-start(bf16[512,2304]{1,0:T(8,128)(2,1)S(1)} %multiply_convert_fusion) | copy-start | bytes 7077892
  149.5 3.1 copy-start.21
  149.5 4.5 %copy-start.34 = (f32[32]{0:T(128)S(1)}, f32[32]{0:T(128)}, u32[]{:S(2)}) copy-start(f32[32]{0:T(128)} %exp.131) | copy-start | bytes 388
  149.5 4.5 %copy-start.36 = (f32[32]{0:T(128)S(1)}, f32[32]{0:T(128)}, u32[]{:S(2)}) copy-start(f32[32]{0:T(128)} %exp.132) | copy-start | bytes 388
  149.6 4.5 %copy-start.39 = (f32[32]{0:T(128)S(1)}, f32[32]{0:T(128)}, u32[]{:S(2)}) copy-start(f32[32]{0:T(128)} %get-tuple-element.90) | copy-start | bytes 388
  149.6 4.5 %copy-start.40 = (f32[32]{0:T(128)S(1)}, f32[32]{0:T(128)}, u32[]{:S(2)}) copy-start(f32[32]{0:T(128)} %exp.130) | copy-start | bytes 388
  150.9 2.1 copy-start.1
  152.7 1.0 copy-start.12
  153.0 1.1 copy-start.10
  190.8 6.0 %copy-start.27 = (f32[32,128]{1,0:T(8,128)S(1)}, f32[32,128]{1,0:T(8,128)}, u32[]{:S(2)}) copy-start(f32[32,128]{1,0:T(8,128)} %get-tuple-element.73) | copy-start | bytes 49156
  196.2 3.6 copy-start.14
  196.2 3.6 copy-start.26
  196.2 3.6 copy-start.28
  199.8 2.0 copy-start.25
  201.7 1.9 copy-start.24
  251.4 2.4 copy-start.33
  251.4 2.4 copy-start.37
  253.8 1.9 copy-start.16
  255.7 1.2 copy-start.2
  255.7 1.9 copy-start.17
  256.0 4.3 %copy-start.4 = (f32[128,32,64]{0,2,1:T(8,128)}, f32[128,32,64]{0,2,1:T(8,128)S(1)}, u32[]{:S(2)}) copy-start(f32[128,32,64]{0,2,1:T(8,128)S(1)} %fusion.17) | copy-start | bytes 3145732
  256.0 2.0 copy-start.19
  258.0 2.3 copy-start.6
  258.0 1.6 copy-start.11
  258.0 1.9 copy-start.18
  258.0 1.9 copy-start.35
  258.3 2.9 copy-start.3
  258.3 2.8 copy-start.38
  261.2 1.0 copy-start.8
  264.7 5.5 %copy-start.5 = (f32[128,32,64]{0,2,1:T(8,128)S(1)}, f32[128,32,64]{0,2,1:T(8,128)}, u32[]{:S(2)}) copy-start(f32[128,32,64]{0,2,1:T(8,128)} %copy-done.4) | copy-start | bytes 3145732
  270.2 1.4 copy-start.7
  271.6 2.7 copy-start.9
  272.9 2.6 copy-start.23
  272.9 2.6 copy-start.31
  274.2 1.3 copy-start.13
  275.6 4.3 %copy-start.30 = (s32[1024]{0:T(1024)S(1)}, s32[1024]{0:T(1024)}, u32[]{:S(2)}) copy-start(s32[1024]{0:T(1024)} %pad_clamp_fusion) | copy-start | bytes 12292
  279.9 3.3 copy-start.32
Sparse Core Ops, SparseCore 0:
  10.5 114.0 all-gather.4
  155.6 95.6 all-gather.6
where the time goes:
time: 380 us; the launch traced here: 378 us
  waiting for transfers between devices  158 us (42%)
  blocking collectives  108 us (28%)
  local copies, waits for them, and re-layouts  44 us (12%)
  matrix products  24.4 us (6%)
  other arithmetic  24.2 us (6%)
  between operations  14.5 us (4%)
  starting transfers between devices  4.43 us (1%)
    all_gather x1, waiting for transfers between devices, project(): whole_weight = lax.all_gather(in_weight, 'dp', axis=0, tiled=True)  111 us
    all_to_all x1, blocking collectives, on_device(): lax.all_to_all(outgoing, 'seq', split_axis=0, concat_axis=2, tiled=True)  83.7 us
    all_gather x1, waiting for transfers between devices, entering_2(): gathered = jax.tree.map(lambda a: lax.all_gather(a, axis), part)  45.8 us
    unnamed x1, blocking collectives  24.8 us
    dot_general x1, matrix products, project(): jnp.dot(operand, whole_weight, preferred_element_type=jnp.float32)  9.08 us
    dot_general x4, matrix products, on_device(): jnp.einsum('hts,shp->thp', weights, x_block, preferred_element_type=jnp.f...  8.69 us
    mul x2, local copies, waits for them, and re-layouts, on_device(): ssm_out * head_scale * out_gain.reshape(HALF_HEADS, HEADDIM)[None]  8.02 us
  transfers between devices with their start and end apart: 3, of which 2 were waited for; matrix products, arithmetic and copies ran while one was open for 9% of the time, Pallas kernels for 0%

commit v1 on v0

v1 whole, which is shorter than its diff:
```python
import jax
import jax.numpy as jnp
from jax import lax
from jax.experimental import pallas as pl
from jax.experimental.pallas import tpu as pltpu
from jax.sharding import PartitionSpec as P

HEADDIM = 64
STATE = 128
GROUP = 128
POSITIONS = 512
ROWS = 1024
PAD = 16
BLOCKS = ROWS // GROUP
OWN = 1024
COLS = 256
CHUNKS = 1
CHUNK = OWN // CHUNKS
EPS = 1e-05

Z, X, Y = 8, 4, 8
bf16 = jnp.bfloat16
f32 = jnp.float32


def place(z, x, y, core):
    return (z * X + x) * (2 * Y) + 2 * y + core


def far_groups():
    return [
        [place(2 * k + dz, x, y, c) for k in range(Z // 2)]
        for dz in range(2)
        for x in range(X)
        for y in range(Y)
        for c in range(2)
    ]


def near_groups():
    return [
        [place(2 * zp + dz, x, 2 * yp + dy, c) for dz in range(2) for x in range(X) for dy in range(2)]
        for zp in range(Z // 2)
        for yp in range(Y // 2)
        for c in range(2)
    ]


def spread(block, groups):
    count = len(groups[0])
    return lax.all_to_all(
        jnp.broadcast_to(block[None], (count,) + block.shape),
        ("dp", "seq"), 0, 0, axis_index_groups=groups, tiled=True,
    )


def params():
    return pltpu.CompilerParams(vmem_limit_bytes=58 * 1024 * 1024)


def whole(shape):
    return pl.BlockSpec(shape, lambda *_: (0,) * len(shape))


def project_and_mix(normed, w, taps, bias, w_all, p_all):
    for k in range(4):
        w_all[512 * k : 512 * k + 512, :] = w[:, 32 * k : 32 * k + 32, :].reshape(512, COLS)
    p_all[...] = (
        jnp.dot(normed[...], w_all[...], preferred_element_type=f32).astype(bf16).astype(f32)
    )


def mixed_rows(start, taps, bias, p_all):
    rows = p_all[pl.ds(pl.multiple_of(start + 8, 8), GROUP + 8), :]
    pre = bias[...] + taps[0:1, :] * rows[5 : 5 + GROUP]
    for k in range(1, 4):
        pre = pre + taps[k : k + 1, :] * rows[5 + k : 5 + k + GROUP]
    return (pre / (1.0 + jnp.exp(-pre))).astype(bf16)


def bc_body(normed, w, taps, bias, b_out, c_out, scores, w_all, p_all):
    project_and_mix(normed, w, taps, bias, w_all, p_all)

    def one(j, carry):
        start = pl.multiple_of(j * GROUP, GROUP)
        mixed = mixed_rows(start, taps, bias, p_all)
        b, c = mixed[:, :STATE], mixed[:, STATE:]
        b_out[pl.ds(start, GROUP), :] = b
        c_out[pl.ds(start, GROUP), :] = c
        scores[pl.ds(start, GROUP), :] = lax.dot_general(
            c, b, (((1,), (1,)), ((), ())), preferred_element_type=f32
        )
        return carry

    lax.fori_loop(0, BLOCKS, one, 0)


def bc_kernel(normed, w, taps, bias):
    return pl.pallas_call(
        bc_body,
        out_shape=(
            jax.ShapeDtypeStruct((ROWS, STATE), bf16),
            jax.ShapeDtypeStruct((ROWS, STATE), bf16),
            jax.ShapeDtypeStruct((ROWS, GROUP), f32),
        ),
        grid=(1,),
        in_specs=[
            whole(normed.shape),
            pl.BlockSpec((16, 128, COLS), lambda i: (0, 0, 0)),
            whole(taps.shape),
            whole(bias.shape),
        ],
        out_specs=(whole((ROWS, STATE)), whole((ROWS, STATE)), whole((ROWS, GROUP))),
        scratch_shapes=[pltpu.VMEM((2048, COLS), bf16), pltpu.VMEM((PAD + ROWS, COLS), f32)],
        compiler_params=params(),
        name="bc",
    )(normed, w, taps, bias)


def heads_body(
    normed, w, taps, bias, b_all, c_all, scores_all, cum_r, step_r, cum_c, step_c, skip,
    local, state, w_all, p_all,
):
    project_and_mix(normed, w, taps, bias, w_all, p_all)
    state[...] = jnp.zeros_like(state)
    row = lax.broadcasted_iota(jnp.int32, (GROUP, GROUP), 0)
    lane = lax.broadcasted_iota(jnp.int32, (GROUP, GROUP), 1)
    causal = lane <= row
    first = lane < HEADDIM

    def one(j, carry):
        start = pl.multiple_of(j * GROUP, GROUP)
        here = pl.ds(start, GROUP)
        mixed = mixed_rows(start, taps, bias, p_all)
        b = b_all[here, :]
        c = c_all[here, :]
        scores = scores_all[here, :]
        for pair in range(COLS // 128):
            wide = slice(128 * pair, 128 * pair + 128)
            x = mixed[:, wide].astype(f32)
            cums, steps, weights = [], [], []
            for h in (2 * pair, 2 * pair + 1):
                cum = jnp.broadcast_to(cum_c[0, here, h : h + 1], (GROUP, GROUP))
                gap = cum - cum_r[0, h : h + 1, here]
                decay = jnp.exp(jnp.where(causal, gap, -1e30))
                weights.append((scores * decay * step_r[0, h : h + 1, here]).astype(bf16))
                cums.append(cum)
                steps.append(jnp.broadcast_to(step_c[0, here, h : h + 1], (GROUP, GROUP)))
            both = jnp.concatenate(weights, axis=1)
            apart = jnp.concatenate(
                [jnp.where(first, x, 0.0).astype(bf16), jnp.where(first, 0.0, x).astype(bf16)], axis=0
            )
            intra = jnp.dot(both, apart, preferred_element_type=f32)
            cum = jnp.where(first, cums[0], cums[1])
            step = jnp.where(first, steps[0], steps[1])
            closing = cum[GROUP - 1 : GROUP, :]
            scaled = (jnp.exp(closing - cum) * step * x).astype(bf16)
            block_state = lax.dot_general(
                b, scaled, (((0,), (0,)), ((), ())), preferred_element_type=f32
            )
            entering = state[pair]
            inter = jnp.exp(cum) * jnp.dot(c, entering.astype(bf16), preferred_element_type=f32)
            local[here, wide] = intra + inter + skip[:, wide] * x
            state[pair] = jnp.exp(closing) * entering + block_state
        return carry

    lax.fori_loop(0, BLOCKS, one, 0)


def heads_kernel(normed, w, first_step, taps, bias, b_all, c_all, scores, cum_r, step_r, cum_c, step_c, skip):
    steps = taps.shape[1] // COLS
    heads = COLS // HEADDIM
    return pl.pallas_call(
        heads_body,
        out_shape=(
            jax.ShapeDtypeStruct((ROWS, steps * COLS), f32),
            jax.ShapeDtypeStruct((steps * COLS // 128, STATE, 128), f32),
        ),
        grid=(steps,),
        in_specs=[
            whole(normed.shape),
            pl.BlockSpec((16, 128, COLS), lambda i: (0, 0, i + first_step)),
            pl.BlockSpec((4, COLS), lambda i: (0, i)),
            pl.BlockSpec((1, COLS), lambda i: (0, i)),
            whole(b_all.shape),
            whole(c_all.shape),
            whole(scores.shape),
            pl.BlockSpec((1, heads, ROWS), lambda i: (i, 0, 0)),
            pl.BlockSpec((1, heads, ROWS), lambda i: (i, 0, 0)),
            pl.BlockSpec((1, ROWS, heads), lambda i: (i, 0, 0)),
            pl.BlockSpec((1, ROWS, heads), lambda i: (i, 0, 0)),
            pl.BlockSpec((1, COLS), lambda i: (0, i)),
        ],
        out_specs=(
            pl.BlockSpec((ROWS, COLS), lambda i: (0, i)),
            pl.BlockSpec((COLS // 128, STATE, 128), lambda i: (i, 0, 0)),
        ),
        scratch_shapes=[pltpu.VMEM((2048, COLS), bf16), pltpu.VMEM((PAD + ROWS, COLS), f32)],
        compiler_params=params(),
        name="heads",
    )(normed, w, taps, bias, b_all, c_all, scores, cum_r, step_r, cum_c, step_c, skip)


def chain_body(parts, out):
    entering = jnp.zeros(out.shape[1:], f32)
    for y in range(Y):
        out[y] = entering.astype(bf16)
        fade = parts[y, STATE : STATE + 1, :].astype(f32) + parts[y, STATE + 1 : STATE + 2, :].astype(f32)
        entering = fade * entering + parts[y, :STATE, :].astype(f32)


def chain_kernel(parts):
    return pl.pallas_call(
        chain_body,
        out_shape=jax.ShapeDtypeStruct((Y, STATE, parts.shape[2]), bf16),
        compiler_params=params(),
        name="chain",
    )(parts)


def finish_body(local, c_all, entering, cum, gain, order, out):
    lane = lax.broadcasted_iota(jnp.int32, (GROUP, GROUP), 1)
    row = lax.broadcasted_iota(jnp.int32, (GROUP, GROUP), 0)
    same_head = jnp.where((lane < HEADDIM) == (row < HEADDIM), 1.0 / HEADDIM, 0.0).astype(bf16)
    position = lax.broadcasted_iota(jnp.int32, (POSITIONS, POSITIONS), 1)
    pick = jnp.where(position == order[...], 1.0, 0.0).astype(bf16)
    first = lax.broadcasted_iota(jnp.int32, (1, 128), 1) < HEADDIM
    for frame in range(ROWS // POSITIONS):
        here = slice(frame * POSITIONS, (frame + 1) * POSITIONS)
        parts = []
        for pair in range(COLS // 128):
            wide = slice(128 * pair, 128 * pair + 128)
            inter = jnp.dot(c_all[here, :], entering[pair], preferred_element_type=f32)
            fade = jnp.exp(
                jnp.where(first, cum[0, here, 2 * pair : 2 * pair + 1], cum[0, here, 2 * pair + 1 : 2 * pair + 2])
            )
            ssm = local[here, wide] + fade * inter
            square = ssm * ssm
            high = square.astype(bf16)
            low = (square - high.astype(f32)).astype(bf16)
            mean = jnp.dot(high, same_head, preferred_element_type=f32) + jnp.dot(
                low, same_head, preferred_element_type=f32
            )
            parts.append((ssm * lax.rsqrt(mean + EPS) * gain[:, wide]).astype(bf16))
        normalized = jnp.concatenate(parts, axis=1)
        picked = jnp.dot(pick, normalized, preferred_element_type=f32).astype(bf16)
        out[:, frame] = picked.reshape(2 * Y, POSITIONS // (2 * Y), COLS)


def finish_kernel(local, c_all, entering, cum, gain, order):
    steps = local.shape[1] // COLS
    heads = COLS // HEADDIM
    piece = POSITIONS // (2 * Y)
    return pl.pallas_call(
        finish_body,
        out_shape=jax.ShapeDtypeStruct((2 * Y, 2, piece, local.shape[1]), bf16),
        grid=(steps,),
        in_specs=[
            pl.BlockSpec((ROWS, COLS), lambda i: (0, i)),
            whole(c_all.shape),
            pl.BlockSpec((COLS // 128, STATE, 128), lambda i: (i, 0, 0)),
            pl.BlockSpec((1, ROWS, heads), lambda i: (i, 0, 0)),
            pl.BlockSpec((1, COLS), lambda i: (0, i)),
            whole(order.shape),
        ],
        out_specs=pl.BlockSpec((2 * Y, 2, piece, COLS), lambda i: (0, 0, 0, i)),
        compiler_params=params(),
        name="finish",
    )(local, c_all, entering, cum, gain, order)


def regroup_body(*refs):
    *parts, out = refs
    row = lax.broadcasted_iota(jnp.int32, (POSITIONS, POSITIONS), 0)
    col = lax.broadcasted_iota(jnp.int32, (POSITIONS, POSITIONS), 1)
    piece = POSITIONS // (2 * Y)
    pick = jnp.where(col == (row % (2 * Y)) * piece + row // (2 * Y), 1.0, 0.0).astype(bf16)
    for g, part in enumerate(parts):
        for c in range(2):
            rows = part[:, c].reshape(POSITIONS, CHUNK)
            picked = jnp.dot(pick, rows, preferred_element_type=f32).astype(bf16)
            out[:, c * OWN + g * CHUNK : c * OWN + (g + 1) * CHUNK] = picked


def regroup_kernel(parts):
    return pl.pallas_call(
        regroup_body,
        out_shape=jax.ShapeDtypeStruct((POSITIONS, 2 * OWN), bf16),
        compiler_params=params(),
        name="regroup",
    )(*parts)


def on_device(
    tokens, in_gain, in_weight, conv_weight, conv_bias, log_decay, skip, out_gain, scan_order
):
    seq = lax.axis_index("seq")
    core = seq % 2
    y = seq // 2
    swap = [(i, i ^ 1) for i in range(2 * Y)]
    onward = [(i, i + 2) for i in range(2 * Y - 2)]
    head_count = OWN // HEADDIM

    def own_part(a):
        return lax.dynamic_slice_in_dim(a, core * OWN, OWN, a.ndim - 1)

    weight = jnp.concatenate([in_weight[:, 2 * OWN :], own_part(in_weight)], axis=1)
    half = lax.dynamic_slice_in_dim(weight, (y % 2) * 32, 32, 0)
    far = spread(half, far_groups()).reshape(128, 2 * STATE + OWN)
    cuts = [0] + [2 * STATE + (g + 1) * CHUNK for g in range(CHUNKS)]
    chunks = [spread(far[:, a:b], near_groups()) for a, b in zip(cuts, cuts[1:])]

    own = tokens[0]
    sibling = lax.ppermute(own, "seq", swap)
    tail = jnp.where(core == 1, own[POSITIONS - PAD :], sibling[POSITIONS - PAD :])
    tail = lax.ppermute(tail, "seq", onward)
    even = jnp.where(core == 0, own, sibling)
    odd = jnp.where(core == 0, sibling, own)
    widened = jnp.concatenate([tail, even, odd], axis=0).astype(f32)
    inverse = lax.rsqrt(jnp.mean(widened * widened, axis=1, keepdims=True) + EPS)
    normed = (widened * inverse * in_gain[None, :]).astype(bf16)

    def own_heads(which):
        return lax.dynamic_slice_in_dim(log_decay[0], which * head_count, head_count, 0)

    mine = own_heads(core)
    other = lax.ppermute(own_heads(1 - core), "seq", swap)
    decay = jnp.concatenate(
        [jnp.where(core == 0, mine, other), jnp.where(core == 0, other, mine)], axis=1
    )
    blocked = decay.reshape(head_count, BLOCKS, GROUP)
    cumulative = jnp.cumsum(blocked, axis=2)
    closings = cumulative[:, :, -1]
    before = jnp.concatenate(
        [jnp.zeros((head_count, 1), f32), jnp.cumsum(closings, axis=1)], axis=1
    )
    from_start = (cumulative + before[:, :BLOCKS, None]).reshape(head_count, ROWS)
    fade = jnp.exp(before[:, BLOCKS])
    heads = COLS // HEADDIM

    def by_step(a):
        return a.reshape(head_count // heads, heads, ROWS)

    cum_r = by_step(cumulative)
    step_r = by_step(-decay)
    cum_c = cum_r.transpose(0, 2, 1)
    step_c = step_r.transpose(0, 2, 1)
    whole_c = by_step(from_start).transpose(0, 2, 1)

    own_taps, own_bias = own_part(conv_weight[:, : 2 * OWN]), own_part(conv_bias[None, : 2 * OWN])
    own_skip = jnp.repeat(
        lax.dynamic_slice_in_dim(skip, core * head_count, head_count, 0), HEADDIM
    )[None, :]
    own_gain = own_part(out_gain[None, :])
    fade_rows = jnp.repeat(fade, HEADDIM).reshape(OWN // 128, 1, 128)
    fade_high = fade_rows.astype(bf16)
    fade_low = (fade_rows - fade_high.astype(f32)).astype(bf16)
    order = scan_order[:, None]

    b_all, c_all, scores = bc_kernel(
        normed, chunks[0], conv_weight[:, 2 * OWN :], conv_bias[None, 2 * OWN :]
    )
    same_core = [list(range(c, 2 * Y, 2)) for c in range(2)]
    arrived = []
    for g in range(CHUNKS):
        wide = slice(g * CHUNK, (g + 1) * CHUNK)
        steps = slice(g * CHUNK // COLS, (g + 1) * CHUNK // COLS)
        pairs = slice(g * CHUNK // 128, (g + 1) * CHUNK // 128)
        local, state = heads_kernel(
            normed, chunks[g], 1 if g == 0 else 0, own_taps[:, wide], own_bias[:, wide],
            b_all, c_all, scores, cum_r[steps], step_r[steps], cum_c[steps], step_c[steps],
            own_skip[:, wide],
        )
        count = CHUNK // 128
        sent = jnp.concatenate(
            [
                state.astype(bf16),
                fade_high[pairs],
                fade_low[pairs],
                jnp.zeros((count, 14, 128), bf16),
            ],
            axis=1,
        )
        per = 128 * count // Y
        if per != 128:
            sent = sent.reshape(count, STATE + 16, 128 // per, per).transpose(0, 2, 1, 3)
            sent = sent.reshape(Y, STATE + 16, per)
        parts = lax.all_to_all(sent, "seq", 0, 0, axis_index_groups=same_core, tiled=True)
        entering = lax.all_to_all(
            chain_kernel(parts), "seq", 0, 0, axis_index_groups=same_core, tiled=True
        )
        if per != 128:
            entering = entering.reshape(count, 128 // per, STATE, per).transpose(0, 2, 1, 3)
            entering = entering.reshape(count, STATE, 128)
        outgoing = finish_kernel(
            local, c_all, entering, whole_c[steps], own_gain[:, wide], order
        )
        back = lax.all_to_all(outgoing, "seq", 0, 0, tiled=True)
        arrived.append(back.reshape(Y, 2, 2, POSITIONS // (2 * Y), CHUNK))
    return regroup_kernel(arrived)[None]


def solution(mesh):
    in_specs = (
        P("dp", "seq", None),
        P(),
        P("dp", None),
        P(),
        P(),
        P("dp", None, "seq"),
        P(),
        P(),
        P(),
    )
    out_specs = P("dp", "seq", None)
    return jax.shard_map(
        on_device, mesh=mesh, in_specs=in_specs, out_specs=out_specs, check_vma=False
    )
```

time: 380 us -> 247 us (0.65)
  waiting for transfers between devices: 158 us -> 46.9 us
  Pallas kernels: 0 us -> 46.2 us
  local copies, waits for them, and re-layouts: 44 us -> 16.7 us
  matrix products: 24.4 us -> 0 us
  starting transfers between devices: 4.43 us -> 20.9 us
  between operations: 14.5 us -> 0.32 us
  blocking collectives: 108 us -> 98.6 us
  other arithmetic: 24.2 us -> 16.5 us
    all_gather x2 -> x0, waiting for transfers between devices: 157 us -> none  [the longest x1 111 us: project(): whole_weight = lax.all_gather(in_weight, 'dp', axis=0, tiled=True)]
    pallas_call x0 -> x5, Pallas kernels: none -> 46.2 us  [the longest x1 24.1 us: heads_kernel(): pl.pallas_call(heads_body, out_shape=(jax.ShapeDtypeStruct((ROWS, steps *...]
    ppermute x1 -> x3, waiting for transfers between devices: 0.01 us -> 41.3 us  [the longest x1 41.3 us: on_device(): tail = lax.ppermute(tail, 'seq', onward)]
    unnamed x1 -> x0, blocking collectives: 24.8 us -> none
    dot_general x17 -> x0, matrix products: 24.4 us -> none  [the longest x1 9.08 us: project(): jnp.dot(operand, whole_weight, preferred_element_type=jnp.float32)]
    all_to_all x1 -> x3, blocking collectives: 83.7 us -> 98.6 us  [the longest x1 62 us: on_device(): back = lax.all_to_all(outgoing, 'seq', 0, 0, tiled=True)]
    all_to_all x0 -> x2, starting transfers between devices: none -> 11.5 us  [the longest x1 8.06 us: spread(): lax.all_to_all(jnp.broadcast_to(block[None], (count,) + block.shape), ('d...]
    mul x5 -> x0, local copies, waits for them, and re-layouts: 10.1 us -> none  [the longest x2 8.02 us: on_device(): ssm_out * head_scale * out_gain.reshape(HALF_HEADS, HEADDIM)[None]]
  transfers between devices with their start and end apart: 3 -> 5, of which waited for: 2 -> 2; matrix products, arithmetic and copies ran while one was open for 9% -> 11% of each run, Pallas kernels for 0% -> 0%
where the time goes in v1:
time: 247 us; the launch traced here: 246 us
  blocking collectives  98.6 us (40%)
  waiting for transfers between devices  46.9 us (19%)
  Pallas kernels  46.2 us (19%)
  starting transfers between devices  20.9 us (8%)
  local copies, waits for them, and re-layouts  16.7 us (7%)
  other arithmetic  16.5 us (7%)
    all_to_all x1, blocking collectives, on_device(): back = lax.all_to_all(outgoing, 'seq', 0, 0, tiled=True)  62 us
    ppermute x1, waiting for transfers between devices, on_device(): tail = lax.ppermute(tail, 'seq', onward)  41.3 us
    pallas_call x1, Pallas kernels, heads_kernel(): pl.pallas_call(heads_body, out_shape=(jax.ShapeDtypeStruct((ROWS, steps *...  24.1 us
    all_to_all x1, blocking collectives, spread(): lax.all_to_all(jnp.broadcast_to(block[None], (count,) + block.shape), ('d...  20.3 us
    all_to_all x1, blocking collectives, on_device(): lax.all_to_all(sent, 'seq', 0, 0, axis_index_groups=same_core, tiled=True)  16.2 us
    pallas_call x1, Pallas kernels, finish_kernel(): pl.pallas_call(finish_body, out_shape=jax.ShapeDtypeStruct((2 * Y, 2, pie...  9.38 us
    all_to_all x1, starting transfers between devices, spread(): lax.all_to_all(jnp.broadcast_to(block[None], (count,) + block.shape), ('d...  8.06 us
    convert_element_type x1, other arithmetic, on_device(): normed = (widened * inverse * in_gain[None, :]).astype(bf16)  6.93 us
  transfers between devices with their start and end apart: 5, of which 2 were waited for; matrix products, arithmetic and copies ran while one was open for 11% of the time, Pallas kernels for 0%

profile of v1, /device:TPU:1, one launch (start us, length us, event | category | flops | bytes accessed | tf_op | source)
XLA Modules:
  0.0 246.1 jit_solution(9193414691460194518)
XLA Ops:
  0.0 0.8 slice.36
  0.8 0.9 constant_dynamic-slice_fusion.1
  1.7 20.3 %all_to_all.25 = bf16[4,32,1280]{2,1,0:T(8,128)(2,1)S(1)} all-to-all(bf16[4,32,1280]{2,1,0:T(8,128)(2,1)S(1)} %broadcast_in_dim.38), channel_id=1, replica_groups={{0,128,256,384},{1,129,257,385},{2,130,258,386},{3,131,259,387},{4,132,..., dimensions={0} | all-to-all | bytes 655360 | tf_op jit(solution)/shard_map/all_to_all | solution.py:51
  22.1 2.8 %broadcast_in_dim.40 = bf16[16,128,1280]{2,1,0:T(8,128)(2,1)} broadcast(bf16[128,1280]{1,0:T(8,128)(2,1)S(1)} %bitcast.29), dimensions={1,2} | broadcast | bytes 5570560 | tf_op jit(solution)/shard_map/broadcast_in_dim | solution.py:52
  24.9 0.0 copy-start.7
  24.9 0.0 copy-start.11
  24.9 8.1 %all-to-all-start.1 = ((bf16[16,128,1280]{2,1,0:T(8,128)(2,1)}), bf16[16,128,1280]{2,1,0:T(8,128)(2,1)}, u32[]{:S(2)}, u32[]{:S(2)}) async-start(bf16[16,128,1280]{2,1,0:T(8,128)(2,1)} %broadcast_in_dim.40), calls=%async_computation.1 | async-start | bytes 10485760 | tf_op jit(solution)/shard_map/all_to_all | solution.py:51
  33.0 4.0 %collective-permute-start = (bf16[512,2048]{1,0:T(8,128)(2,1)S(1)}, bf16[512,2048]{1,0:T(8,128)(2,1)}, u32[]{:S(2)}, u32[]{:S(2)}) collective-permute-start(bf16[512,2048]{1,0:T(8,128)(2,1)S(1)} %bitcast.28), channel_id=1, source_target_pairs={{0,1},{1,0},{2,3},{3,2},{4,5},{5,4},{6,7},{7,6},{8,9},{9,8},{10,11... | collective-permute-start | bytes 6291464 | tf_op jit(solution)/shard_map/ppermute | solution.py:314
  37.1 1.9 collective-permute-start.2
  39.1 0.6 constant_dynamic-slice_fusion.taps
  39.7 0.6 slice.39.taps
  40.3 0.6 slice.40
  40.9 0.1 dynamic_slice.36
  40.9 0.1 broadcast_in_dim.42
  41.0 0.7 broadcast_in_dim_reshape.4.skip
  41.7 0.6 dynamic-slice.8
  42.3 0.1 pad.4.clone
  42.5 4.5 %reduce_window_sum.22 = f32[16,8,128]{2,1,0:T(8,128)S(1)} reduce-window(f32[16,8,128]{2,1,0:T(8,128)S(1)} %bitcast.30, f32[]{:T(128)} %constant.53.clone.1), window={size=1x1x128 pad=0_0x0_0x127_0}, to_apply=%region_1.2 | reduce-window | flops 2080768 | bytes 131076 | tf_op jit(solution)/shard_map/jit(cumsum)/reduce_window_sum | solution.py:332
  47.0 0.1 slice.45
  47.1 2.0 copy.31
  49.1 2.0 copy.32
  51.1 0.1 copy.33
  51.2 0.1 exp.8
  51.3 0.1 broadcast_in_dim.43
  51.4 0.1 broadcast_in_dim.44
  51.5 0.9 slice_select_fusion
  52.4 3.5 %collective-permute-start.1 = (bf16[16,2048]{1,0:T(8,128)(2,1)S(1)}, bf16[16,2048]{1,0:T(8,128)(2,1)S(1)}, u32[]{:S(2)}, u32[]{:S(2)}) collective-permute-start(bf16[16,2048]{1,0:T(8,128)(2,1)S(1)} %slice_select_fusion), channel_id=1, source_target_pairs={{0,2},{1,3},{2,4},{3,5},{4,6},{5,7},{6,8},{7,9},{8,10},{9,11},{10,... | collective-permute-start | bytes 196616 | tf_op jit(solution)/shard_map/ppermute | solution.py:316
  55.9 1.9 broadcast_select_fusion.1
  57.8 41.3 %collective-permute-done.1 = bf16[16,2048]{1,0:T(8,128)(2,1)S(1)} collective-permute-done((bf16[16,2048]{1,0:T(8,128)(2,1)S(1)}, bf16[16,2048]{1,0:T(8,128)(2,1)S(1)}, u32[]{:S(2)}, u32[]{:S(2)}) %collective-permute-start.1) | collective-permute-done | bytes 65568 | tf_op jit(solution)/shard_map/ppermute | solution.py:316
  99.1 1.0 fusion
  100.1 6.9 %fusion.2.normed = bf16[1040,2048]{1,0:T(8,128)(2,1)} fusion(f32[2048]{0:T(1024)S(1)} %copy-done.8, f32[1040]{0:T(1024)S(1)} %add_rsqrt_fusion, bf16[512,2048]{1,0:T(8,128)(2,1)S(1)} %get-tuple-element.16, bf16[512,2048]{1,0:T(8,128)(2,1)S(1)} %get-tuple-element.15, bf16[16,2048]{1,0:T(8,128)(2,1)S(1)} %collective-permute-done.1), kind=kLoop, calls=%fused_computation.4 | loop fusion | flops 19169280 | bytes 8532032 | tf_op jit(solution)/shard_map/convert_element_type | solution.py:321
  107.1 6.8 %bc.1 = (bf16[1024,128]{1,0:T(8,128)(2,1)}, bf16[1024,128]{1,0:T(8,128)(2,1)}, f32[1024,128]{1,0:T(8,128)}) custom-call(bf16[1040,2048]{1,0:T(8,128)(2,1)} %fusion.2.normed, bf16[16,128,1280]{2,1,0:T(8,128)(2,1)} %all-to-all-done.1.w, f32[4,256]{1,0:T(4,128)} %slice.39.taps, f32[1,256]{1,0:T(1,128)} %bitcast.34), custom_call_target="tpu_custom_call" | custom-call | tf_op jit(solution)/shard_map/bc/pallas_call | solution.py:99
  113.9 24.1 %heads.1 = (f32[1024,1024]{1,0:T(8,128)}, f32[8,128,128]{2,1,0:T(8,128)}) custom-call(bf16[1040,2048]{1,0:T(8,128)(2,1)} %fusion.2.normed, bf16[16,128,1280]{2,1,0:T(8,128)(2,1)} %all-to-all-done.1.w, f32[4,1024]{1,0:T(4,128)} %constant_dynamic-slice_fusion.taps, f32[1,1024]{1,0:T(1,128)} %bitcast.33, bf16[1024,128]{1,0:T(8,128)(2,1)} %get-tuple-element.10.b_all, ...), custom_call_target="tpu_custom_call" | custom-call | tf_op jit(solution)/shard_map/heads/pallas_call | solution.py:173
  138.0 1.1 convert_element_type.48
  139.1 0.1 maximum_maximum_fusion
  139.2 16.2 %all_to_all.26.parts = bf16[8,144,128]{2,1,0:T(8,128)(2,1)} all-to-all(bf16[8,144,128]{2,1,0:T(8,128)(2,1)S(1)} %maximum_maximum_fusion), channel_id=1, replica_groups={{0,2,4,6,8,10,12,14},{1,3,5,7,9,11,13,15},{16,18,20,22,24,26,28,30},{17..., dimensions={0} | all-to-all | bytes 589824 | tf_op jit(solution)/shard_map/all_to_all | solution.py:388
  155.4 1.7 chain.1
  157.1 3.4 %all-to-all-start.3 = ((bf16[8,128,128]{2,1,0:T(8,128)(2,1)}), bf16[8,128,128]{2,1,0:T(8,128)(2,1)S(1)}, u32[]{:S(2)}, u32[]{:S(2)}) async-start(bf16[8,128,128]{2,1,0:T(8,128)(2,1)} %chain.1), calls=%async_computation.3 | async-start | bytes 524288 | tf_op jit(solution)/shard_map/all_to_all | solution.py:389
  160.6 0.6 dynamic-slice.9
  161.2 0.9 copy.36.order
  162.1 0.1 copy.34
  162.1 0.1 add.59
  162.3 2.0 copy.35
  164.3 5.6 %all-to-all-done.3.entering = bf16[8,128,128]{2,1,0:T(8,128)(2,1)S(1)} async-done(((bf16[8,128,128]{2,1,0:T(8,128)(2,1)}), bf16[8,128,128]{2,1,0:T(8,128)(2,1)S(1)}, u32[]{:S(2)}, u32[]{:S(2)}) %all-to-all-start.3) | async-done | bytes 262176 | tf_op jit(solution)/shard_map/all_to_all | solution.py:389
  169.8 0.7 copy-done.3
  170.5 9.4 %finish.1 = bf16[16,2,32,1024]{3,2,1,0:T(8,128)(2,1)} custom-call(f32[1024,1024]{1,0:T(8,128)} %get-tuple-element.13.local, bf16[1024,128]{1,0:T(8,128)(2,1)} %get-tuple-element.11.c_all, bf16[8,128,128]{2,1,0:T(8,128)(2,1)} %copy-done.3, f32[4,1024,4]{2,1,0:T(8,128)} %bitcast.27, f32[1,1024]{1,0:T(1,128)} %bitcast.31, s32[512,1]{1,0:T(8,128)} %copy.36.order), custom_call_target="tpu_custom_call" | custom-call | tf_op jit(solution)/shard_map/finish/pallas_call | solution.py:254
  179.9 62.0 %all_to_all.27 = bf16[16,2,32,1024]{3,2,1,0:T(8,128)(2,1)} all-to-all(bf16[16,2,32,1024]{3,2,1,0:T(8,128)(2,1)} %finish.1), channel_id=1, replica_groups=mesh['dp'=32,'seq'=16] {'seq'}, dimensions={0} | all-to-all | bytes 4194304 | tf_op jit(solution)/shard_map/all_to_all | solution.py:398
  242.0 4.2 %regroup.1 = bf16[512,2048]{1,0:T(8,128)(2,1)} custom-call(bf16[8,2,2,32,1024]{4,3,2,1,0:T(8,128)(2,1)} %bitcast.24), custom_call_target="tpu_custom_call" | custom-call | tf_op jit(solution)/shard_map/regroup/pallas_call | solution.py:286
  (46 shorter events, 0.3 us)
Async XLA Ops:
  24.9 8.1 %copy-start = (bf16[1,512,2048]{2,1,0:T(8,128)(2,1)S(1)}, bf16[1,512,2048]{2,1,0:T(8,128)(2,1)}, u32[]{:S(2)}) copy-start(bf16[1,512,2048]{2,1,0:T(8,128)(2,1)} %param.9) | copy-start | bytes 6291460
  24.9 12.2 %copy-start.6 = (f32[1,32,512]{2,1,0:T(8,128)S(1)}, f32[1,32,512]{2,1,0:T(8,128)}, u32[]{:S(2)}) copy-start(f32[1,32,512]{2,1,0:T(8,128)} %param.14) | copy-start | bytes 196612
  24.9 14.1 %slice-start = ((f32[4,2304]{1,0:T(4,128)}), f32[4,2048]{1,0:T(4,128)S(1)}, s32[]{:S(2)}) async-start(f32[4,2304]{1,0:T(4,128)} %param.12), calls=%async_computation.5 | async-start | bytes 65536 | tf_op jit(solution)/shard_map/slice | solution.py:350
  24.9 14.8 %copy-start.5 = (f32[4,2304]{1,0:T(4,128)S(1)}, f32[4,2304]{1,0:T(4,128)}, u32[]{:S(2)}) copy-start(f32[4,2304]{1,0:T(4,128)} %param.12) | copy-start | bytes 110596
  24.9 15.4 %copy-start.7 = (f32[2304]{0:T(1024)S(1)}, f32[2304]{0:T(1024)}, u32[]{:S(2)}) copy-start(f32[2304]{0:T(1024)} %param.13) | copy-start | bytes 27652
  24.9 15.9 %copy-start.11 = (f32[32]{0:T(128)S(1)}, f32[32]{0:T(128)}, u32[]{:S(2)}) copy-start(f32[32]{0:T(128)} %param.15) | copy-start | bytes 388
  24.9 16.8 %slice-start.1 = ((f32[2304]{0:T(1024)}), f32[2048]{0:T(1024)S(1)}, s32[]{:S(2)}) async-start(f32[2304]{0:T(1024)} %param.13), calls=%async_computation.6 | async-start | bytes 16384 | tf_op jit(solution)/shard_map/slice | solution.py:350
  24.9 82.1 %all-to-all-start.1 = ((bf16[16,128,1280]{2,1,0:T(8,128)(2,1)}), bf16[16,128,1280]{2,1,0:T(8,128)(2,1)}, u32[]{:S(2)}, u32[]{:S(2)}) async-start(bf16[16,128,1280]{2,1,0:T(8,128)(2,1)} %broadcast_in_dim.40), calls=%async_computation.1 | async-start | bytes 10485760 | tf_op jit(solution)/shard_map/all_to_all | solution.py:51
  33.0 18.5 %collective-permute-start = (bf16[512,2048]{1,0:T(8,128)(2,1)S(1)}, bf16[512,2048]{1,0:T(8,128)(2,1)}, u32[]{:S(2)}, u32[]{:S(2)}) collective-permute-start(bf16[512,2048]{1,0:T(8,128)(2,1)S(1)} %bitcast.28), channel_id=1, source_target_pairs={{0,1},{1,0},{2,3},{3,2},{4,5},{5,4},{6,7},{7,6},{8,9},{9,8},{10,11... | collective-permute-start | bytes 6291464 | tf_op jit(solution)/shard_map/ppermute | solution.py:314
  37.1 5.3 %collective-permute-start.2 = (f32[16,512]{1,0:T(8,128)S(1)}, f32[16,512]{1,0:T(8,128)S(1)}, u32[]{:S(2)}, u32[]{:S(2)}) collective-permute-start(f32[16,512]{1,0:T(8,128)S(1)} %dynamic-slice_bitcast_fusion), channel_id=1, source_target_pairs={{0,1},{1,0},{2,3},{3,2},{4,5},{5,4},{6,7},{7,6},{8,9},{9,8},{10,11... | collective-permute-start | bytes 98312 | tf_op jit(solution)/shard_map/ppermute | solution.py:327
  47.0 10.8 %copy-start.1 = (f32[4,4,1024]{2,1,0:T(4,128)}, f32[4,4,1024]{2,1,0:T(4,128)S(1)}, u32[]{:S(2)}) copy-start(f32[4,4,1024]{2,1,0:T(4,128)S(1)} %reshape.91.cum_r) | copy-start | bytes 196612
  49.1 8.7 %copy-start.4 = (f32[4,4,1024]{2,1,0:T(4,128)}, f32[4,4,1024]{2,1,0:T(4,128)S(1)}, u32[]{:S(2)}) copy-start(f32[4,4,1024]{2,1,0:T(4,128)S(1)} %maximum_negate_fusion.step_r) | copy-start | bytes 196612
  52.4 47.8 %copy-start.8 = (f32[2048]{0:T(1024)S(1)}, f32[2048]{0:T(1024)}, u32[]{:S(2)}) copy-start(f32[2048]{0:T(1024)} %param.10) | copy-start | bytes 24580
  52.4 46.7 %collective-permute-start.1 = (bf16[16,2048]{1,0:T(8,128)(2,1)S(1)}, bf16[16,2048]{1,0:T(8,128)(2,1)S(1)}, u32[]{:S(2)}, u32[]{:S(2)}) collective-permute-start(bf16[16,2048]{1,0:T(8,128)(2,1)S(1)} %slice_select_fusion), channel_id=1, source_target_pairs={{0,2},{1,3},{2,4},{3,5},{4,6},{5,7},{6,8},{7,9},{8,10},{9,11},{10,... | collective-permute-start | bytes 196616 | tf_op jit(solution)/shard_map/ppermute | solution.py:316
  113.9 46.7 %copy-start.10 = (f32[2048]{0:T(1024)S(1)}, f32[2048]{0:T(1024)}, u32[]{:S(2)}) copy-start(f32[2048]{0:T(1024)} %param.16) | copy-start | bytes 24580
  113.9 47.3 %copy-start.9 = (s32[512]{0:T(512)S(1)}, s32[512]{0:T(512)}, u32[]{:S(2)}) copy-start(s32[512]{0:T(512)} %param.17) | copy-start | bytes 6148
  113.9 48.4 %copy-start.2 = (f32[4,4,1024]{2,1,0:T(4,128)S(1)}, f32[4,4,1024]{2,1,0:T(4,128)}, u32[]{:S(2)}) copy-start(f32[4,4,1024]{2,1,0:T(4,128)} %copy-done.1) | copy-start | bytes 196612
  157.1 12.7 %all-to-all-start.3 = ((bf16[8,128,128]{2,1,0:T(8,128)(2,1)}), bf16[8,128,128]{2,1,0:T(8,128)(2,1)S(1)}, u32[]{:S(2)}, u32[]{:S(2)}) async-start(bf16[8,128,128]{2,1,0:T(8,128)(2,1)} %chain.1), calls=%async_computation.3 | async-start | bytes 524288 | tf_op jit(solution)/shard_map/all_to_all | solution.py:389
  169.8 0.7 copy-start.3

commit v2 on v1

--- a/solution.py
+++ b/solution.py
@@ -14,7 +14,7 @@
 BLOCKS = ROWS // GROUP
 OWN = 1024
 COLS = 256
-CHUNKS = 1
+CHUNKS = 2
 CHUNK = OWN // CHUNKS
 EPS = 1e-05
 
@@ -39,9 +39,9 @@
 
 def near_groups():
     return [
-        [place(2 * zp + dz, x, 2 * yp + dy, c) for dz in range(2) for x in range(X) for dy in range(2)]
+        [place(2 * zp + dz, x, y, c) for dz in range(2) for x in range(X)]
         for zp in range(Z // 2)
-        for yp in range(Y // 2)
+        for y in range(Y)
         for c in range(2)
     ]
 
@@ -64,7 +64,7 @@
 
 def project_and_mix(normed, w, taps, bias, w_all, p_all):
     for k in range(4):
-        w_all[512 * k : 512 * k + 512, :] = w[:, 32 * k : 32 * k + 32, :].reshape(512, COLS)
+        w_all[512 * k : 512 * k + 512, :] = w[:, 64 * k : 64 * k + 64, :].reshape(512, COLS)
     p_all[...] = (
         jnp.dot(normed[...], w_all[...], preferred_element_type=f32).astype(bf16).astype(f32)
     )
@@ -106,7 +106,7 @@
         grid=(1,),
         in_specs=[
             whole(normed.shape),
-            pl.BlockSpec((16, 128, COLS), lambda i: (0, 0, 0)),
+            pl.BlockSpec((8, 256, COLS), lambda i: (0, 0, 0)),
             whole(taps.shape),
             whole(bias.shape),
         ],
@@ -118,8 +118,8 @@
 
 
 def heads_body(
-    normed, w, taps, bias, b_all, c_all, scores_all, cum_r, step_r, cum_c, step_c, skip,
-    local, state, w_all, p_all,
+    normed, w, taps, bias, b_all, c_all, scores_all, cum_r, step_r, cum_c, step_c, skip, fades,
+    local, sent, w_all, p_all, state,
 ):
     project_and_mix(normed, w, taps, bias, w_all, p_all)
     state[...] = jnp.zeros_like(state)
@@ -165,21 +165,31 @@
         return carry
 
     lax.fori_loop(0, BLOCKS, one, 0)
-
-
-def heads_kernel(normed, w, first_step, taps, bias, b_all, c_all, scores, cum_r, step_r, cum_c, step_c, skip):
+    pairs = COLS // 128
+    slab = STATE // Y
+    fade_row = sent.shape[1] - PAD
+    for y in range(Y):
+        for pair in range(pairs):
+            at = pl.multiple_of((pl.program_id(0) * pairs + pair) * slab, slab)
+            sent[y, pl.ds(at, slab), :] = state[pair, slab * y : slab * y + slab, :].astype(bf16)
+        sent[y, fade_row:, :] = fades[...]
+
+
+def heads_kernel(
+    normed, w, first_step, taps, bias, b_all, c_all, scores, cum_r, step_r, cum_c, step_c, skip, fades
+):
     steps = taps.shape[1] // COLS
     heads = COLS // HEADDIM
     return pl.pallas_call(
         heads_body,
         out_shape=(
             jax.ShapeDtypeStruct((ROWS, steps * COLS), f32),
-            jax.ShapeDtypeStruct((steps * COLS // 128, STATE, 128), f32),
+            jax.ShapeDtypeStruct((Y, steps * COLS // 128 * (STATE // Y) + PAD, 128), bf16),
         ),
         grid=(steps,),
         in_specs=[
             whole(normed.shape),
-            pl.BlockSpec((16, 128, COLS), lambda i: (0, 0, i + first_step)),
+            pl.BlockSpec((8, 256, COLS), lambda i: (0, 0, i + first_step)),
             pl.BlockSpec((4, COLS), lambda i: (0, i)),
             pl.BlockSpec((1, COLS), lambda i: (0, i)),
             whole(b_all.shape),
@@ -190,29 +200,42 @@
             pl.BlockSpec((1, ROWS, heads), lambda i: (i, 0, 0)),
             pl.BlockSpec((1, ROWS, heads), lambda i: (i, 0, 0)),
             pl.BlockSpec((1, COLS), lambda i: (0, i)),
+            whole(fades.shape),
         ],
         out_specs=(
             pl.BlockSpec((ROWS, COLS), lambda i: (0, i)),
-            pl.BlockSpec((COLS // 128, STATE, 128), lambda i: (i, 0, 0)),
+            whole((Y, steps * COLS // 128 * (STATE // Y) + PAD, 128)),
         ),
-        scratch_shapes=[pltpu.VMEM((2048, COLS), bf16), pltpu.VMEM((PAD + ROWS, COLS), f32)],
+        scratch_shapes=[
+            pltpu.VMEM((2048, COLS), bf16),
+            pltpu.VMEM((PAD + ROWS, COLS), f32),
+            pltpu.VMEM((COLS // 128, STATE, 128), f32),
+        ],
         compiler_params=params(),
         name="heads",
-    )(normed, w, taps, bias, b_all, c_all, scores, cum_r, step_r, cum_c, step_c, skip)
+    )(normed, w, taps, bias, b_all, c_all, scores, cum_r, step_r, cum_c, step_c, skip, fades)
 
 
 def chain_body(parts, out):
-    entering = jnp.zeros(out.shape[1:], f32)
-    for y in range(Y):
-        out[y] = entering.astype(bf16)
-        fade = parts[y, STATE : STATE + 1, :].astype(f32) + parts[y, STATE + 1 : STATE + 2, :].astype(f32)
-        entering = fade * entering + parts[y, :STATE, :].astype(f32)
+    slab = STATE // Y
+    pairs = CHUNK // 128
+    for g in range(CHUNKS):
+        base = g * (pairs * slab + PAD)
+        for pair in range(pairs):
+            rows = slice(base + pair * slab, base + pair * slab + slab)
+            to = slice((g * pairs + pair) * slab, (g * pairs + pair + 1) * slab)
+            entering = jnp.zeros((slab, 128), f32)
+            for y in range(Y):
+                out[y, to, :] = entering.astype(bf16)
+                fades = parts[y, base + pairs * slab : base + pairs * slab + PAD, :].astype(f32)
+                fade = fades[pair : pair + 1] + fades[pairs + pair : pairs + pair + 1]
+                entering = fade * entering + parts[y, rows, :].astype(f32)
 
 
 def chain_kernel(parts):
     return pl.pallas_call(
         chain_body,
-        out_shape=jax.ShapeDtypeStruct((Y, STATE, parts.shape[2]), bf16),
+        out_shape=jax.ShapeDtypeStruct((Y, parts.shape[1] - CHUNKS * PAD, 128), bf16),
         compiler_params=params(),
         name="chain",
     )(parts)
@@ -230,7 +253,8 @@
         parts = []
         for pair in range(COLS // 128):
             wide = slice(128 * pair, 128 * pair + 128)
-            inter = jnp.dot(c_all[here, :], entering[pair], preferred_element_type=f32)
+            state = entering[:, pair * (STATE // Y) : (pair + 1) * (STATE // Y), :].reshape(STATE, 128)
+            inter = jnp.dot(c_all[here, :], state, preferred_element_type=f32)
             fade = jnp.exp(
                 jnp.where(first, cum[0, here, 2 * pair : 2 * pair + 1], cum[0, here, 2 * pair + 1 : 2 * pair + 2])
             )
@@ -247,7 +271,7 @@
         out[:, frame] = picked.reshape(2 * Y, POSITIONS // (2 * Y), COLS)
 
 
-def finish_kernel(local, c_all, entering, cum, gain, order):
+def finish_kernel(local, c_all, entering, g, cum, gain, order):
     steps = local.shape[1] // COLS
     heads = COLS // HEADDIM
     piece = POSITIONS // (2 * Y)
@@ -258,7 +282,7 @@
         in_specs=[
             pl.BlockSpec((ROWS, COLS), lambda i: (0, i)),
             whole(c_all.shape),
-            pl.BlockSpec((COLS // 128, STATE, 128), lambda i: (i, 0, 0)),
+            pl.BlockSpec((Y, COLS // 128 * (STATE // Y), 128), lambda i: (0, g * steps + i, 0)),
             pl.BlockSpec((1, ROWS, heads), lambda i: (i, 0, 0)),
             pl.BlockSpec((1, COLS), lambda i: (0, i)),
             whole(order.shape),
@@ -269,26 +293,29 @@
     )(local, c_all, entering, cum, gain, order)
 
 
-def regroup_body(*refs):
-    *parts, out = refs
+def regroup_body(part, *refs):
+    out = refs[-1]
     row = lax.broadcasted_iota(jnp.int32, (POSITIONS, POSITIONS), 0)
     col = lax.broadcasted_iota(jnp.int32, (POSITIONS, POSITIONS), 1)
     piece = POSITIONS // (2 * Y)
     pick = jnp.where(col == (row % (2 * Y)) * piece + row // (2 * Y), 1.0, 0.0).astype(bf16)
-    for g, part in enumerate(parts):
-        for c in range(2):
-            rows = part[:, c].reshape(POSITIONS, CHUNK)
-            picked = jnp.dot(pick, rows, preferred_element_type=f32).astype(bf16)
-            out[:, c * OWN + g * CHUNK : c * OWN + (g + 1) * CHUNK] = picked
-
-
-def regroup_kernel(parts):
+    rows = part[...].reshape(POSITIONS, CHUNK)
+    out[...] = jnp.dot(pick, rows, preferred_element_type=f32).astype(bf16)
+
+
+def regroup_kernel(part, out, g):
+    earlier = [] if out is None else [out]
     return pl.pallas_call(
         regroup_body,
         out_shape=jax.ShapeDtypeStruct((POSITIONS, 2 * OWN), bf16),
+        grid=(2,),
+        in_specs=[pl.BlockSpec((Y, None, 2, POSITIONS // (2 * Y), CHUNK), lambda c: (0, c, 0, 0, 0))]
+        + [pl.BlockSpec(memory_space=pl.ANY) for _ in earlier],
+        out_specs=pl.BlockSpec((POSITIONS, CHUNK), lambda c: (0, c * CHUNKS + g)),
+        input_output_aliases={1: 0} if earlier else {},
         compiler_params=params(),
         name="regroup",
-    )(*parts)
+    )(part, *earlier)
 
 
 def on_device(
@@ -296,7 +323,6 @@
 ):
     seq = lax.axis_index("seq")
     core = seq % 2
-    y = seq // 2
     swap = [(i, i ^ 1) for i in range(2 * Y)]
     onward = [(i, i + 2) for i in range(2 * Y - 2)]
     head_count = OWN // HEADDIM
@@ -305,10 +331,10 @@
         return lax.dynamic_slice_in_dim(a, core * OWN, OWN, a.ndim - 1)
 
     weight = jnp.concatenate([in_weight[:, 2 * OWN :], own_part(in_weight)], axis=1)
-    half = lax.dynamic_slice_in_dim(weight, (y % 2) * 32, 32, 0)
-    far = spread(half, far_groups()).reshape(128, 2 * STATE + OWN)
+    far = spread(weight, far_groups()).reshape(256, 2 * STATE + OWN)
     cuts = [0] + [2 * STATE + (g + 1) * CHUNK for g in range(CHUNKS)]
-    chunks = [spread(far[:, a:b], near_groups()) for a, b in zip(cuts, cuts[1:])]
+    far_chunks = [far[:, a:b] for a, b in zip(cuts, cuts[1:])]
+    chunks = [spread(far_chunks[0], near_groups())]
 
     own = tokens[0]
     sibling = lax.ppermute(own, "seq", swap)
@@ -316,9 +342,14 @@
     tail = lax.ppermute(tail, "seq", onward)
     even = jnp.where(core == 0, own, sibling)
     odd = jnp.where(core == 0, sibling, own)
-    widened = jnp.concatenate([tail, even, odd], axis=0).astype(f32)
-    inverse = lax.rsqrt(jnp.mean(widened * widened, axis=1, keepdims=True) + EPS)
-    normed = (widened * inverse * in_gain[None, :]).astype(bf16)
+
+    def norm(rows):
+        widened = rows.astype(f32)
+        inverse = lax.rsqrt(jnp.mean(widened * widened, axis=1, keepdims=True) + EPS)
+        return (widened * inverse * in_gain[None, :]).astype(bf16)
+
+    normed = jnp.concatenate([jnp.zeros((PAD, 2048), bf16), norm(jnp.concatenate([even, odd], axis=0))], axis=0)
+    tail = norm(tail)
 
     def own_heads(which):
         return lax.dynamic_slice_in_dim(log_decay[0], which * head_count, head_count, 0)
@@ -352,52 +383,59 @@
         lax.dynamic_slice_in_dim(skip, core * head_count, head_count, 0), HEADDIM
     )[None, :]
     own_gain = own_part(out_gain[None, :])
-    fade_rows = jnp.repeat(fade, HEADDIM).reshape(OWN // 128, 1, 128)
+    fade_rows = jnp.repeat(fade, HEADDIM).reshape(OWN // 128, 128)
     fade_high = fade_rows.astype(bf16)
     fade_low = (fade_rows - fade_high.astype(f32)).astype(bf16)
     order = scan_order[:, None]
+    fade_parts = []
+    for g in range(CHUNKS):
+        pairs = slice(g * CHUNK // 128, (g + 1) * CHUNK // 128)
+        fades = jnp.concatenate([fade_high[pairs], fade_low[pairs]], axis=0)
+        fade_parts.append(jnp.pad(fades, ((0, PAD - fades.shape[0]), (0, 0))))
+
+    (
+        normed, tail, cum_r, step_r, cum_c, step_c, whole_c, own_taps, own_bias, own_skip, own_gain,
+        order, fade_parts, far_chunks,
+    ) = lax.optimization_barrier(
+        (
+            normed, tail, cum_r, step_r, cum_c, step_c, whole_c, own_taps, own_bias, own_skip,
+            own_gain, order, fade_parts, far_chunks,
+        )
+    )
+    normed = lax.dynamic_update_slice(normed, tail, (0, 0))
+    chunks += [spread(a, near_groups()) for a in far_chunks[1:]]
 
     b_all, c_all, scores = bc_kernel(
         normed, chunks[0], conv_weight[:, 2 * OWN :], conv_bias[None, 2 * OWN :]
     )
     same_core = [list(range(c, 2 * Y, 2)) for c in range(2)]
-    arrived = []
+    locals_, sents = [], []
     for g in range(CHUNKS):
         wide = slice(g * CHUNK, (g + 1) * CHUNK)
         steps = slice(g * CHUNK // COLS, (g + 1) * CHUNK // COLS)
-        pairs = slice(g * CHUNK // 128, (g + 1) * CHUNK // 128)
-        local, state = heads_kernel(
+        local, sent = heads_kernel(
             normed, chunks[g], 1 if g == 0 else 0, own_taps[:, wide], own_bias[:, wide],
             b_all, c_all, scores, cum_r[steps], step_r[steps], cum_c[steps], step_c[steps],
-            own_skip[:, wide],
+            own_skip[:, wide], fade_parts[g],
         )
-        count = CHUNK // 128
-        sent = jnp.concatenate(
-            [
-                state.astype(bf16),
-                fade_high[pairs],
-                fade_low[pairs],
-                jnp.zeros((count, 14, 128), bf16),
-            ],
-            axis=1,
-        )
-        per = 128 * count // Y
-        if per != 128:
-            sent = sent.reshape(count, STATE + 16, 128 // per, per).transpose(0, 2, 1, 3)
-            sent = sent.reshape(Y, STATE + 16, per)
-        parts = lax.all_to_all(sent, "seq", 0, 0, axis_index_groups=same_core, tiled=True)
-        entering = lax.all_to_all(
-            chain_kernel(parts), "seq", 0, 0, axis_index_groups=same_core, tiled=True
-        )
-        if per != 128:
-            entering = entering.reshape(count, 128 // per, STATE, per).transpose(0, 2, 1, 3)
-            entering = entering.reshape(count, STATE, 128)
+        locals_.append(local)
+        sents.append(sent)
+    parts = lax.all_to_all(
+        jnp.concatenate(sents, axis=1), "seq", 0, 0, axis_index_groups=same_core, tiled=True
+    )
+    entering = lax.all_to_all(
+        chain_kernel(parts), "seq", 0, 0, axis_index_groups=same_core, tiled=True
+    )
+    out = None
+    for g in range(CHUNKS):
+        wide = slice(g * CHUNK, (g + 1) * CHUNK)
+        steps = slice(g * CHUNK // COLS, (g + 1) * CHUNK // COLS)
         outgoing = finish_kernel(
-            local, c_all, entering, whole_c[steps], own_gain[:, wide], order
+            locals_[g], c_all, entering, g, whole_c[steps], own_gain[:, wide], order
         )
         back = lax.all_to_all(outgoing, "seq", 0, 0, tiled=True)
-        arrived.append(back.reshape(Y, 2, 2, POSITIONS // (2 * Y), CHUNK))
-    return regroup_kernel(arrived)[None]
+        out = regroup_kernel(back.reshape(Y, 2, 2, POSITIONS // (2 * Y), CHUNK), out, g)
+    return out[None]
 
 
 def solution(mesh):

time: 247 us -> 250 us (1.012)
  blocking collectives: 98.6 us -> 26.1 us
  starting transfers between devices: 20.9 us -> 42.7 us
  local copies, waits for them, and re-layouts: 16.7 us -> 37.8 us
  waiting for transfers between devices: 46.9 us -> 66 us
  Pallas kernels: 46.2 us -> 54.1 us
  other arithmetic: 16.5 us -> 21.3 us
    all_to_all x2 -> x0, blocking collectives: 78.3 us -> none  [the longest x1 62 us: on_device(): back = lax.all_to_all(outgoing, 'seq', 0, 0, tiled=True)]
    all_to_all x0 -> x3, waiting for transfers between devices: none -> 58.1 us  [the longest x2 47.3 us: on_device(): back = lax.all_to_all(outgoing, 'seq', 0, 0, tiled=True)]
    ppermute x1, waiting for transfers between devices: 41.3 us -> 0.01 us  [on_device(): tail = lax.ppermute(tail, 'seq', onward)]
    all_to_all x0 -> x3, starting transfers between devices: none -> 16.6 us  [the longest x2 10.7 us: on_device(): back = lax.all_to_all(outgoing, 'seq', 0, 0, tiled=True)]
    slice x0 -> x14, local copies, waits for them, and re-layouts: none -> 14.4 us  [the longest x3 5.9 us: on_device(): step_r[steps]]
    all_to_all x1, blocking collectives: 20.3 us -> 26.1 us  [spread(): lax.all_to_all(jnp.broadcast_to(block[None], (count,) + block.shape), ('d...]
    all_to_all x1 -> x2, starting transfers between devices: 8.06 us -> 13.7 us  [spread(): lax.all_to_all(jnp.broadcast_to(block[None], (count,) + block.shape), ('d...]
    pallas_call x1 -> x2, Pallas kernels: 24.1 us -> 28.4 us  [heads_kernel(): pl.pallas_call(heads_body, out_shape=(jax.ShapeDtypeStruct((ROWS, steps *...]
  transfers between devices with their start and end apart: 5 -> 9, of which waited for: 2 -> 5; matrix products, arithmetic and copies ran while one was open for 11% -> 19% of each run, Pallas kernels for 0% -> 12%
where the time goes in v2:
time: 250 us; the launch traced here: 248 us
  waiting for transfers between devices  66 us (26%)
  Pallas kernels  54.1 us (22%)
  starting transfers between devices  42.7 us (17%)
  local copies, waits for them, and re-layouts  37.8 us (15%)
  blocking collectives  26.1 us (10%)
  other arithmetic  21.3 us (9%)
    all_to_all x2, waiting for transfers between devices, on_device(): back = lax.all_to_all(outgoing, 'seq', 0, 0, tiled=True)  47.3 us
    pallas_call x2, Pallas kernels, heads_kernel(): pl.pallas_call(heads_body, out_shape=(jax.ShapeDtypeStruct((ROWS, steps *...  28.4 us
    all_to_all x1, blocking collectives, spread(): lax.all_to_all(jnp.broadcast_to(block[None], (count,) + block.shape), ('d...  26.1 us
    all_to_all x2, starting transfers between devices, spread(): lax.all_to_all(jnp.broadcast_to(block[None], (count,) + block.shape), ('d...  13.7 us
    pallas_call x2, Pallas kernels, finish_kernel(): pl.pallas_call(finish_body, out_shape=jax.ShapeDtypeStruct((2 * Y, 2, pie...  11.7 us
    all_to_all x1, waiting for transfers between devices, on_device(): lax.all_to_all(jnp.concatenate(sents, axis=1), 'seq', 0, 0, axis_index_gr...  10.7 us
    all_to_all x2, starting transfers between devices, on_device(): back = lax.all_to_all(outgoing, 'seq', 0, 0, tiled=True)  10.7 us
    all_to_all x1, waiting for transfers between devices, on_device(): lax.all_to_all(chain_kernel(parts), 'seq', 0, 0, axis_index_groups=same_c...  7.23 us
  transfers between devices with their start and end apart: 9, of which 5 were waited for; matrix products, arithmetic and copies ran while one was open for 19% of the time, Pallas kernels for 12%

profile of v2, /device:TPU:1, one launch (start us, length us, event | category | flops | bytes accessed | tf_op | source)
XLA Modules:
  0.0 248.4 jit_solution(15651703123018094104)
XLA Ops:
  0.0 0.8 slice.117
  0.8 0.9 constant_dynamic-slice_fusion
  1.8 26.1 %all_to_all.35 = bf16[4,64,1280]{2,1,0:T(8,128)(2,1)S(1)} all-to-all(bf16[4,64,1280]{2,1,0:T(8,128)(2,1)S(1)} %broadcast_in_dim.22), channel_id=1, replica_groups={{0,128,256,384},{1,129,257,385},{2,130,258,386},{3,131,259,387},{4,132,..., dimensions={0} | all-to-all | bytes 1310720 | tf_op jit(solution)/shard_map/all_to_all | solution.py:51
  27.8 0.8 copy-done.6
  28.7 1.8 broadcast_in_dim.24
  30.6 8.3 %all-to-all-start.2 = ((bf16[8,256,768]{2,1,0:T(8,128)(2,1)}), bf16[8,256,768]{2,1,0:T(8,128)(2,1)S(1)}, u32[]{:S(2)}, u32[]{:S(2)}) async-start(bf16[8,256,768]{2,1,0:T(8,128)(2,1)} %broadcast_in_dim.24), calls=%async_computation.2 | async-start | bytes 6291456 | tf_op jit(solution)/shard_map/all_to_all | solution.py:51
  38.9 3.9 %collective-permute-start = (bf16[512,2048]{1,0:T(8,128)(2,1)}, bf16[512,2048]{1,0:T(8,128)(2,1)}, u32[]{:S(2)}, u32[]{:S(2)}) collective-permute-start(bf16[512,2048]{1,0:T(8,128)(2,1)} %bitcast.32), channel_id=1, source_target_pairs={{0,1},{1,0},{2,3},{3,2},{4,5},{5,4},{6,7},{7,6},{8,9},{9,8},{10,11... | collective-permute-start | bytes 6291464 | tf_op jit(solution)/shard_map/ppermute | solution.py:340
  42.8 1.9 collective-permute-start.2
  46.9 4.5 %reduce_window_sum.22 = f32[16,8,128]{2,1,0:T(8,128)S(1)} reduce-window(f32[16,8,128]{2,1,0:T(8,128)S(1)} %bitcast.33, f32[]{:T(128)} %constant.42.clone.1), window={size=1x1x128 pad=0_0x0_0x127_0}, to_apply=%region_2.3 | reduce-window | flops 2080768 | bytes 131076 | tf_op jit(solution)/shard_map/jit(cumsum)/reduce_window_sum | solution.py:363
  51.6 2.0 copy.38
  54.2 2.0 copy.39
  56.2 2.0 copy.42
  59.5 4.0 %negate_bitcast_fusion = (f32[4,1024,4]{2,1,0:T(8,128)}, f32[4,4,1024]{1,2,0:T(8,128)}) fusion(f32[4,4,1024]{1,2,0:T(8,128)} %copy.38), kind=kLoop, calls=%fused_computation.36 | loop fusion | flops 16384 | bytes 196608 | tf_op jit(solution)/shard_map/transpose | solution.py:378
  63.4 1.0 slice.143
  64.4 0.9 slice_select_fusion
  65.3 3.2 %collective-permute-start.1 = (bf16[16,2048]{1,0:T(8,128)(2,1)S(1)}, bf16[16,2048]{1,0:T(8,128)(2,1)S(1)}, u32[]{:S(2)}, u32[]{:S(2)}) collective-permute-start(bf16[16,2048]{1,0:T(8,128)(2,1)S(1)} %slice_select_fusion), channel_id=1, source_target_pairs={{0,2},{1,3},{2,4},{3,5},{4,6},{5,7},{6,8},{7,9},{8,10},{9,11},{10,... | collective-permute-start | bytes 196616 | tf_op jit(solution)/shard_map/ppermute | solution.py:342
  68.5 2.1 broadcast_select_fusion.1
  70.6 1.0 fusion
  71.6 5.5 %fusion.2 = bf16[1024,2048]{1,0:T(8,128)(2,1)S(1)} fusion(f32[2048]{0:T(1024)S(1)} %copy-done.13, f32[1024]{0:T(1024)S(1)} %add_rsqrt_fusion, bf16[512,2048]{1,0:T(8,128)(2,1)S(1)} %get-tuple-element.52, bf16[512,2048]{1,0:T(8,128)(2,1)S(1)} %get-tuple-element.51), kind=kLoop, calls=%fused_computation.4 | loop fusion | flops 14680064 | bytes 8400896 | tf_op jit(solution)/shard_map/convert_element_type | solution.py:349
  77.1 2.5 %concatenate.32 = bf16[1040,2048]{1,0:T(8,128)(2,1)} pad(bf16[1024,2048]{1,0:T(8,128)(2,1)S(1)} %fusion.2, bf16[]{:T(256)} %constant.45.clone.1), padding=16_0x0_0 | pad | bytes 8454146 | tf_op jit(solution)/shard_map/concatenate | solution.py:351
  79.9 1.7 broadcast_in_dim.23
  82.2 5.4 %all-to-all-start.1 = ((bf16[8,256,512]{2,1,0:T(8,128)(2,1)}), bf16[8,256,512]{2,1,0:T(8,128)(2,1)}, u32[]{:S(2)}, u32[]{:S(2)}) async-start(bf16[8,256,512]{2,1,0:T(8,128)(2,1)} %broadcast_in_dim.23), calls=%async_computation.1 | async-start | bytes 4194304 | tf_op jit(solution)/shard_map/all_to_all | solution.py:51
  88.8 2.7 %fusion.15 = (f32[2,4,1024]{1,2,0:T(8,128)}, f32[2,4,1024]{1,2,0:T(8,128)S(1)}) fusion(f32[4,4,1024]{1,2,0:T(8,128)} %get-tuple-element.36), kind=kLoop, calls=%fused_computation.40 | loop fusion | bytes 131072 | tf_op jit(solution)/shard_map/slice | solution.py:418
  91.5 2.3 copy.44.step_r
  93.8 0.9 copy.43.step_r
  97.8 1.5 fusion.13
  99.3 0.9 copy-done.3
  100.1 1.5 fusion.14
  101.6 6.8 %bc.1 = (bf16[1024,128]{1,0:T(8,128)(2,1)}, bf16[1024,128]{1,0:T(8,128)(2,1)}, f32[1024,128]{1,0:T(8,128)}) custom-call(bf16[1040,2048]{1,0:T(8,128)(2,1)} %constant_dynamic-update-slice_fusion.normed, bf16[8,256,768]{2,1,0:T(8,128)(2,1)} %copy-done, f32[4,256]{1,0:T(4,128)} %slice.122.taps, f32[1,256]{1,0:T(1,128)} %bitcast.37), custom_call_target="tpu_custom_call" | custom-call | tf_op jit(solution)/shard_map/bc/pallas_call | solution.py:99
  108.4 14.3 %heads.3 = (f32[1024,512]{1,0:T(8,128)}, bf16[8,80,128]{2,1,0:T(8,128)(2,1)}) custom-call(bf16[1040,2048]{1,0:T(8,128)(2,1)} %constant_dynamic-update-slice_fusion.normed, bf16[8,256,768]{2,1,0:T(8,128)(2,1)} %copy-done, f32[4,512]{1,0:T(4,128)} %get-tuple-element.67.taps, f32[1,512]{1,0:T(1,128)} %get-tuple-element.73.bias, ...), custom_call_target="tpu_custom_call" | custom-call | tf_op jit(solution)/shard_map/heads/pallas_call | solution.py:183
  122.7 14.2 %heads.2 = (f32[1024,512]{1,0:T(8,128)}, bf16[8,80,128]{2,1,0:T(8,128)(2,1)}) custom-call(bf16[1040,2048]{1,0:T(8,128)(2,1)} %constant_dynamic-update-slice_fusion.normed, bf16[8,256,512]{2,1,0:T(8,128)(2,1)} %all-to-all-done.1.w, f32[4,512]{1,0:T(4,128)} %get-tuple-element.68.taps, f32[1,512]{1,0:T(1,128)} %get-tuple-element.74.bias, ...), custom_call_target="tpu_custom_call" | custom-call | tf_op jit(solution)/shard_map/heads/pallas_call | solution.py:183
  136.9 1.8 pad_maximum_fusion.1
  138.8 5.9 %all-to-all-start.3 = ((bf16[8,160,128]{2,1,0:T(8,128)(2,1)}), bf16[8,160,128]{2,1,0:T(8,128)(2,1)S(1)}, u32[]{:S(2)}, u32[]{:S(2)}) async-start(bf16[8,160,128]{2,1,0:T(8,128)(2,1)} %pad_maximum_fusion.1), calls=%async_computation.3 | async-start | bytes 655360 | tf_op jit(solution)/shard_map/all_to_all | solution.py:423
  144.7 0.9 copy.45.order
  145.6 10.7 %all-to-all-done.3.parts = bf16[8,160,128]{2,1,0:T(8,128)(2,1)S(1)} async-done(((bf16[8,160,128]{2,1,0:T(8,128)(2,1)}), bf16[8,160,128]{2,1,0:T(8,128)(2,1)S(1)}, u32[]{:S(2)}, u32[]{:S(2)}) %all-to-all-start.3) | async-done | bytes 327712 | tf_op jit(solution)/shard_map/all_to_all | solution.py:423
  157.0 1.7 chain.1
  158.8 3.4 %all-to-all-start.4 = ((bf16[8,128,128]{2,1,0:T(8,128)(2,1)}), bf16[8,128,128]{2,1,0:T(8,128)(2,1)S(1)}, u32[]{:S(2)}, u32[]{:S(2)}) async-start(bf16[8,128,128]{2,1,0:T(8,128)(2,1)} %chain.1), calls=%async_computation.4 | async-start | bytes 524288 | tf_op jit(solution)/shard_map/all_to_all | solution.py:426
  162.8 1.5 fusion.12
  164.3 7.2 %all-to-all-done.4.entering = bf16[8,128,128]{2,1,0:T(8,128)(2,1)S(1)} async-done(((bf16[8,128,128]{2,1,0:T(8,128)(2,1)}), bf16[8,128,128]{2,1,0:T(8,128)(2,1)S(1)}, u32[]{:S(2)}, u32[]{:S(2)}) %all-to-all-start.4) | async-done | bytes 262176 | tf_op jit(solution)/shard_map/all_to_all | solution.py:426
  172.2 5.9 %finish.3 = bf16[16,2,32,512]{3,2,1,0:T(8,128)(2,1)} custom-call(f32[1024,512]{1,0:T(8,128)} %get-tuple-element.48.local, bf16[1024,128]{1,0:T(8,128)(2,1)} %get-tuple-element.33.c_all, bf16[8,128,128]{2,1,0:T(8,128)(2,1)} %copy-done.7, f32[2,1024,4]{2,1,0:T(8,128)} %get-tuple-element.53.cum, f32[1,512]{1,0:T(1,128)} %get-tuple-element.69.gain, ...), custom_call_target="tpu_custom_call" | custom-call | tf_op jit(solution)/shard_map/finish/pallas_call | solution.py:278
  178.1 7.1 %all-to-all-start.6 = ((bf16[16,2,32,512]{3,2,1,0:T(8,128)(2,1)}), bf16[16,2,32,512]{3,2,1,0:T(8,128)(2,1)S(1)}, u32[]{:S(2)}, u32[]{:S(2)}) async-start(bf16[16,2,32,512]{3,2,1,0:T(8,128)(2,1)} %finish.3), calls=%async_computation.6 | async-start | bytes 2097152 | tf_op jit(solution)/shard_map/all_to_all | solution.py:436
  185.2 5.8 %finish.2 = bf16[16,2,32,512]{3,2,1,0:T(8,128)(2,1)} custom-call(f32[1024,512]{1,0:T(8,128)} %get-tuple-element.41.local, bf16[1024,128]{1,0:T(8,128)(2,1)} %get-tuple-element.33.c_all, bf16[8,128,128]{2,1,0:T(8,128)(2,1)} %copy-done.7, f32[2,1024,4]{2,1,0:T(8,128)} %get-tuple-element.54.cum, f32[1,512]{1,0:T(1,128)} %get-tuple-element.70.gain, ...), custom_call_target="tpu_custom_call" | custom-call | tf_op jit(solution)/shard_map/finish/pallas_call | solution.py:278
  191.0 22.2 %all-to-all-done.6 = bf16[16,2,32,512]{3,2,1,0:T(8,128)(2,1)S(1)} async-done(((bf16[16,2,32,512]{3,2,1,0:T(8,128)(2,1)}), bf16[16,2,32,512]{3,2,1,0:T(8,128)(2,1)S(1)}, u32[]{:S(2)}, u32[]{:S(2)}) %all-to-all-start.6) | async-done | bytes 1048608 | tf_op jit(solution)/shard_map/all_to_all | solution.py:436
  213.3 3.6 %all-to-all-start.5 = ((bf16[16,2,32,512]{3,2,1,0:T(8,128)(2,1)}), bf16[16,2,32,512]{3,2,1,0:T(8,128)(2,1)S(1)}, u32[]{:S(2)}, u32[]{:S(2)}) async-start(bf16[16,2,32,512]{3,2,1,0:T(8,128)(2,1)} %finish.2), calls=%async_computation.5 | async-start | bytes 2097152 | tf_op jit(solution)/shard_map/all_to_all | solution.py:436
  216.8 2.8 %regroup.2.refs_0_ = bf16[512,2048]{1,0:T(8,128)(2,1)} custom-call(bf16[8,2,2,32,512]{4,3,2,1,0:T(8,128)(2,1)} %bitcast.28), custom_call_target="tpu_custom_call" | custom-call | tf_op jit(solution)/shard_map/regroup/pallas_call | solution.py:308
  219.6 25.1 %all-to-all-done.5 = bf16[16,2,32,512]{3,2,1,0:T(8,128)(2,1)S(1)} async-done(((bf16[16,2,32,512]{3,2,1,0:T(8,128)(2,1)}), bf16[16,2,32,512]{3,2,1,0:T(8,128)(2,1)S(1)}, u32[]{:S(2)}, u32[]{:S(2)}) %all-to-all-start.5) | async-done | bytes 1048608 | tf_op jit(solution)/shard_map/all_to_all | solution.py:436
  244.7 1.0 copy-done.5
  245.7 2.7 %regroup.3 = bf16[512,2048]{1,0:T(8,128)(2,1)} custom-call(bf16[8,2,2,32,512]{4,3,2,1,0:T(8,128)(2,1)} %bitcast.29, bf16[512,2048]{1,0:T(8,128)(2,1)} %regroup.2.refs_0_), custom_call_target="tpu_custom_call", output_to_operand_aliasing={{}: (1, {})} | custom-call | tf_op jit(solution)/shard_map/regroup/pallas_call | solution.py:308
  (90 shorter events, 11.4 us)
Async XLA Ops:
  27.8 0.8 copy-start.6
  30.6 12.2 %copy-start.12 = (f32[1,32,512]{2,1,0:T(8,128)S(1)}, f32[1,32,512]{2,1,0:T(8,128)}, u32[]{:S(2)}) copy-start(f32[1,32,512]{2,1,0:T(8,128)} %param.14) | copy-start | bytes 196612
  30.6 14.1 %slice-start = ((f32[4,2304]{1,0:T(4,128)}), f32[4,2048]{1,0:T(4,128)S(1)}, s32[]{:S(2)}) async-start(f32[4,2304]{1,0:T(4,128)} %param.12), calls=%async_computation.7 | async-start | bytes 65536 | tf_op jit(solution)/shard_map/slice | solution.py:381
  30.6 14.2 %copy-start.18 = (f32[32]{0:T(128)S(1)}, f32[32]{0:T(128)}, u32[]{:S(2)}) copy-start(f32[32]{0:T(128)} %param.15) | copy-start | bytes 388
  30.6 15.0 %slice-start.1 = ((f32[2304]{0:T(1024)}), f32[2048]{0:T(1024)S(1)}, s32[]{:S(2)}) async-start(f32[2304]{0:T(1024)} %param.13), calls=%async_computation.8 | async-start | bytes 16384 | tf_op jit(solution)/shard_map/slice | solution.py:381
  30.6 49.3 %all-to-all-start.2 = ((bf16[8,256,768]{2,1,0:T(8,128)(2,1)}), bf16[8,256,768]{2,1,0:T(8,128)(2,1)S(1)}, u32[]{:S(2)}, u32[]{:S(2)}) async-start(bf16[8,256,768]{2,1,0:T(8,128)(2,1)} %broadcast_in_dim.24), calls=%async_computation.2 | async-start | bytes 6291456 | tf_op jit(solution)/shard_map/all_to_all | solution.py:51
  38.9 25.6 %collective-permute-start = (bf16[512,2048]{1,0:T(8,128)(2,1)}, bf16[512,2048]{1,0:T(8,128)(2,1)}, u32[]{:S(2)}, u32[]{:S(2)}) collective-permute-start(bf16[512,2048]{1,0:T(8,128)(2,1)} %bitcast.32), channel_id=1, source_target_pairs={{0,1},{1,0},{2,3},{3,2},{4,5},{5,4},{6,7},{7,6},{8,9},{9,8},{10,11... | collective-permute-start | bytes 6291464 | tf_op jit(solution)/shard_map/ppermute | solution.py:340
  42.8 4.1 %collective-permute-start.2 = (f32[16,512]{1,0:T(8,128)S(1)}, f32[16,512]{1,0:T(8,128)S(1)}, u32[]{:S(2)}, u32[]{:S(2)}) collective-permute-start(f32[16,512]{1,0:T(8,128)S(1)} %dynamic-slice_bitcast_fusion), channel_id=1, source_target_pairs={{0,1},{1,0},{2,3},{3,2},{4,5},{5,4},{6,7},{7,6},{8,9},{9,8},{10,11... | collective-permute-start | bytes 98312 | tf_op jit(solution)/shard_map/ppermute | solution.py:358
  59.5 5.0 %copy-start.8 = (bf16[1,512,2048]{2,1,0:T(8,128)(2,1)S(1)}, bf16[1,512,2048]{2,1,0:T(8,128)(2,1)}, u32[]{:S(2)}) copy-start(bf16[1,512,2048]{2,1,0:T(8,128)(2,1)} %param.9) | copy-start | bytes 6291460
  65.3 14.3 %collective-permute-start.1 = (bf16[16,2048]{1,0:T(8,128)(2,1)S(1)}, bf16[16,2048]{1,0:T(8,128)(2,1)S(1)}, u32[]{:S(2)}, u32[]{:S(2)}) collective-permute-start(bf16[16,2048]{1,0:T(8,128)(2,1)S(1)} %slice_select_fusion), channel_id=1, source_target_pairs={{0,2},{1,3},{2,4},{3,5},{4,6},{5,7},{6,8},{7,9},{8,10},{9,11},{10,... | collective-permute-start | bytes 196616 | tf_op jit(solution)/shard_map/ppermute | solution.py:342
  70.6 1.0 copy-start.13
  79.9 2.3 copy-start
  81.6 6.0 %copy-start.11 = (f32[4,2304]{1,0:T(4,128)S(1)}, f32[4,2304]{1,0:T(4,128)}, u32[]{:S(2)}) copy-start(f32[4,2304]{1,0:T(4,128)} %param.12) | copy-start | bytes 110596
  81.6 6.6 %copy-start.14 = (f32[2304]{0:T(1024)S(1)}, f32[2304]{0:T(1024)}, u32[]{:S(2)}) copy-start(f32[2304]{0:T(1024)} %param.13) | copy-start | bytes 27652
  82.2 40.5 %all-to-all-start.1 = ((bf16[8,256,512]{2,1,0:T(8,128)(2,1)}), bf16[8,256,512]{2,1,0:T(8,128)(2,1)}, u32[]{:S(2)}, u32[]{:S(2)}) async-start(bf16[8,256,512]{2,1,0:T(8,128)(2,1)} %broadcast_in_dim.23), calls=%async_computation.1 | async-start | bytes 4194304 | tf_op jit(solution)/shard_map/all_to_all | solution.py:51
  91.5 3.3 %copy-start.15 = (f32[1,1024]{1,0:T(1,128)S(1)}, f32[1,1024]{1,0:T(1,128)}, u32[]{:S(2)}) copy-start(f32[1,1024]{1,0:T(1,128)} %broadcast_in_dim_reshape.3) | copy-start | bytes 12292
  91.5 3.9 %copy-start.16 = (f32[1024]{0:T(1024)S(1)}, f32[1024]{0:T(1024)}, u32[]{:S(2)}) copy-start(f32[1024]{0:T(1024)} %dynamic-slice.8) | copy-start | bytes 12292
  91.5 6.3 %copy-start.1 = (f32[4,1024,4]{2,1,0:T(8,128)S(1)}, f32[4,1024,4]{2,1,0:T(8,128)}, u32[]{:S(2)}) copy-start(f32[4,1024,4]{2,1,0:T(8,128)} %get-tuple-element.38) | copy-start | bytes 196612
  97.8 2.3 copy-start.3
  122.7 14.2 %copy-start.10 = (bf16[8,80,128]{2,1,0:T(8,128)(2,1)S(1)}, bf16[8,80,128]{2,1,0:T(8,128)(2,1)}, u32[]{:S(2)}) copy-start(bf16[8,80,128]{2,1,0:T(8,128)(2,1)} %get-tuple-element.43) | copy-start | bytes 491524
  122.7 22.0 %copy-start.17 = (s32[512]{0:T(512)S(1)}, s32[512]{0:T(512)}, u32[]{:S(2)}) copy-start(s32[512]{0:T(512)} %param.17) | copy-start | bytes 6148
  136.9 25.3 %dynamic-slice-start = ((f32[2048]{0:T(1024)}, s32[]{:T(128)}), f32[1024]{0:T(1024)S(1)}, s32[]{:S(2)}) async-start(f32[2048]{0:T(1024)} %param.16, s32[]{:T(128)} %select_n.65), calls=%async_computation.9 | async-start | bytes 8704 | tf_op jit(solution)/shard_map/dynamic-slice.3
  136.9 25.9 %copy-start.2 = (f32[4,4,1024]{1,2,0:T(8,128)S(1)}, f32[4,4,1024]{1,2,0:T(8,128)}, u32[]{:S(2)}) copy-start(f32[4,4,1024]{1,2,0:T(8,128)} %copy.42) | copy-start | bytes 196612
  138.8 17.6 %all-to-all-start.3 = ((bf16[8,160,128]{2,1,0:T(8,128)(2,1)}), bf16[8,160,128]{2,1,0:T(8,128)(2,1)S(1)}, u32[]{:S(2)}, u32[]{:S(2)}) async-start(bf16[8,160,128]{2,1,0:T(8,128)(2,1)} %pad_maximum_fusion.1), calls=%async_computation.3 | async-start | bytes 655360 | tf_op jit(solution)/shard_map/all_to_all | solution.py:423
  156.3 0.7 copy-start.9
  158.8 12.7 %all-to-all-start.4 = ((bf16[8,128,128]{2,1,0:T(8,128)(2,1)}), bf16[8,128,128]{2,1,0:T(8,128)(2,1)S(1)}, u32[]{:S(2)}, u32[]{:S(2)}) async-start(bf16[8,128,128]{2,1,0:T(8,128)(2,1)} %chain.1), calls=%async_computation.4 | async-start | bytes 524288 | tf_op jit(solution)/shard_map/all_to_all | solution.py:426
  171.5 0.7 copy-start.7
  178.1 35.2 %all-to-all-start.6 = ((bf16[16,2,32,512]{3,2,1,0:T(8,128)(2,1)}), bf16[16,2,32,512]{3,2,1,0:T(8,128)(2,1)S(1)}, u32[]{:S(2)}, u32[]{:S(2)}) async-start(bf16[16,2,32,512]{3,2,1,0:T(8,128)(2,1)} %finish.3), calls=%async_computation.6 | async-start | bytes 2097152 | tf_op jit(solution)/shard_map/all_to_all | solution.py:436
  213.3 3.6 %copy-start.4 = (bf16[16,2,32,512]{3,2,1,0:T(8,128)(2,1)}, bf16[16,2,32,512]{3,2,1,0:T(8,128)(2,1)S(1)}, u32[]{:S(2)}) copy-start(bf16[16,2,32,512]{3,2,1,0:T(8,128)(2,1)S(1)} %all-to-all-done.6) | copy-start | bytes 3145732
  213.3 31.4 %all-to-all-start.5 = ((bf16[16,2,32,512]{3,2,1,0:T(8,128)(2,1)}), bf16[16,2,32,512]{3,2,1,0:T(8,128)(2,1)S(1)}, u32[]{:S(2)}, u32[]{:S(2)}) async-start(bf16[16,2,32,512]{3,2,1,0:T(8,128)(2,1)} %finish.2), calls=%async_computation.5 | async-start | bytes 2097152 | tf_op jit(solution)/shard_map/all_to_all | solution.py:436
  244.7 1.0 copy-start.5

commit v3 on v2

v3 whole, which is shorter than its diff:
```python
import functools

import jax
import jax.numpy as jnp
from jax import lax
from jax.experimental import pallas as pl
from jax.experimental.pallas import tpu as pltpu
from jax.sharding import PartitionSpec as P

HEADDIM = 64
STATE = 128
GROUP = 128
POSITIONS = 512
ROWS = 1024
PAD = 16
BLOCKS = ROWS // GROUP
OWN = 1024
COLS = 256
CHUNKS = 2
CHUNK = OWN // CHUNKS
EPS = 1e-05

Z, X, Y = 8, 4, 8
bf16 = jnp.bfloat16
f32 = jnp.float32


def place(z, x, y, core):
    return (z * X + x) * (2 * Y) + 2 * y + core


def far_groups():
    return [
        [place(2 * k + dz, x, y, c) for k in range(Z // 2)]
        for dz in range(2)
        for x in range(X)
        for y in range(Y)
        for c in range(2)
    ]


def near_groups():
    return [
        [place(2 * zp + dz, x, 2 * yp + dy, c) for dz in range(2) for x in range(X) for dy in range(2)]
        for zp in range(Z // 2)
        for yp in range(Y // 2)
        for c in range(2)
    ]


def spread(block, groups):
    count = len(groups[0])
    return lax.all_to_all(
        jnp.broadcast_to(block[None], (count,) + block.shape),
        ("dp", "seq"), 0, 0, axis_index_groups=groups, tiled=True,
    )


def params():
    return pltpu.CompilerParams(vmem_limit_bytes=58 * 1024 * 1024)


def whole(shape):
    return pl.BlockSpec(shape, lambda *_: (0,) * len(shape))


def project_and_mix(normed, w, taps, bias, w_all, p_all):
    for k in range(4):
        w_all[512 * k : 512 * k + 512, :] = w[:, 32 * k : 32 * k + 32, :].reshape(512, COLS)
    p_all[...] = (
        jnp.dot(normed[...], w_all[...], preferred_element_type=f32).astype(bf16).astype(f32)
    )


def mixed_rows(start, taps, bias, p_all):
    rows = p_all[pl.ds(pl.multiple_of(start + 8, 8), GROUP + 8), :]
    pre = bias[...] + taps[0:1, :] * rows[5 : 5 + GROUP]
    for k in range(1, 4):
        pre = pre + taps[k : k + 1, :] * rows[5 + k : 5 + k + GROUP]
    return (pre / (1.0 + jnp.exp(-pre))).astype(bf16)


def bc_body(normed, w, taps, bias, b_out, c_out, scores, w_all, p_all):
    project_and_mix(normed, w, taps, bias, w_all, p_all)

    def one(j, carry):
        start = pl.multiple_of(j * GROUP, GROUP)
        mixed = mixed_rows(start, taps, bias, p_all)
        b, c = mixed[:, :STATE], mixed[:, STATE:]
        b_out[pl.ds(start, GROUP), :] = b
        c_out[pl.ds(start, GROUP), :] = c
        scores[pl.ds(start, GROUP), :] = lax.dot_general(
            c, b, (((1,), (1,)), ((), ())), preferred_element_type=f32
        )
        return carry

    lax.fori_loop(0, BLOCKS, one, 0)


def bc_kernel(normed, w, taps, bias):
    return pl.pallas_call(
        bc_body,
        out_shape=(
            jax.ShapeDtypeStruct((ROWS, STATE), bf16),
            jax.ShapeDtypeStruct((ROWS, STATE), bf16),
            jax.ShapeDtypeStruct((ROWS, GROUP), f32),
        ),
        grid=(1,),
        in_specs=[
            whole(normed.shape),
            pl.BlockSpec((16, 128, COLS), lambda i: (0, 0, 0)),
            pl.BlockSpec((4, COLS), lambda i: (0, 2 * OWN // COLS)),
            pl.BlockSpec((1, COLS), lambda i: (0, 2 * OWN // COLS)),
        ],
        out_specs=(whole((ROWS, STATE)), whole((ROWS, STATE)), whole((ROWS, GROUP))),
        scratch_shapes=[pltpu.VMEM((2048, COLS), bf16), pltpu.VMEM((PAD + ROWS, COLS), f32)],
        compiler_params=params(),
        name="bc",
    )(normed, w, taps, bias)


def heads_body(
    base, core, normed, w, taps, bias, b_all, c_all, scores_all, cum_r, step_r, cum_c, step_c, skip, fades,
    local, sent, w_all, p_all, state,
):
    project_and_mix(normed, w, taps, bias, w_all, p_all)
    state[...] = jnp.zeros_like(state)
    heads = COLS // HEADDIM
    head = core[0] * (OWN // HEADDIM) + (base + pl.program_id(0)) * heads
    row = lax.broadcasted_iota(jnp.int32, (GROUP, GROUP), 0)
    lane = lax.broadcasted_iota(jnp.int32, (GROUP, GROUP), 1)
    causal = lane <= row
    first = lane < HEADDIM

    def one(j, carry):
        start = pl.multiple_of(j * GROUP, GROUP)
        here = pl.ds(start, GROUP)
        mixed = mixed_rows(start, taps, bias, p_all)
        b = b_all[here, :]
        c = c_all[here, :]
        scores = scores_all[here, :]
        for pair in range(COLS // 128):
            wide = slice(128 * pair, 128 * pair + 128)
            x = mixed[:, wide].astype(f32)
            cums, steps, weights = [], [], []
            for h in (2 * pair, 2 * pair + 1):
                cum = jnp.broadcast_to(cum_c[0, here, h : h + 1], (GROUP, GROUP))
                gap = cum - cum_r[0, h : h + 1, here]
                decay = jnp.exp(jnp.where(causal, gap, -1e30))
                weights.append((scores * decay * step_r[0, h : h + 1, here]).astype(bf16))
                cums.append(cum)
                steps.append(jnp.broadcast_to(step_c[0, here, h : h + 1], (GROUP, GROUP)))
            both = jnp.concatenate(weights, axis=1)
            apart = jnp.concatenate(
                [jnp.where(first, x, 0.0).astype(bf16), jnp.where(first, 0.0, x).astype(bf16)], axis=0
            )
            intra = jnp.dot(both, apart, preferred_element_type=f32)
            cum = jnp.where(first, cums[0], cums[1])
            step = jnp.where(first, steps[0], steps[1])
            closing = cum[GROUP - 1 : GROUP, :]
            scaled = (jnp.exp(closing - cum) * step * x).astype(bf16)
            block_state = lax.dot_general(
                b, scaled, (((0,), (0,)), ((), ())), preferred_element_type=f32
            )
            entering = state[pair]
            inter = jnp.exp(cum) * jnp.dot(c, entering.astype(bf16), preferred_element_type=f32)
            gains = jnp.where(first, skip[head + 2 * pair], skip[head + 2 * pair + 1])
            local[here, wide] = intra + inter + gains * x
            state[pair] = jnp.exp(closing) * entering + block_state
        return carry

    lax.fori_loop(0, BLOCKS, one, 0)
    pairs = COLS // 128
    slab = STATE // Y
    fade_row = sent.shape[1] - PAD
    for y in range(Y):
        for pair in range(pairs):
            at = pl.multiple_of((pl.program_id(0) * pairs + pair) * slab, slab)
            sent[y, pl.ds(at, slab), :] = state[pair, slab * y : slab * y + slab, :].astype(bf16)
        sent[y, fade_row:, :] = fades[...]


def heads_kernel(
    core, g, normed, w, first_step, taps, bias, b_all, c_all, scores, cum_r, step_r, cum_c, step_c, skip, fades
):
    steps = CHUNK // COLS
    heads = COLS // HEADDIM
    base = g * steps
    sent = (Y, CHUNK // 128 * (STATE // Y) + PAD, 128)

    def channels(i, core):
        return (0, core[0] * (OWN // COLS) + base + i)

    def step(i, core):
        return (base + i, 0, 0)

    return pl.pallas_call(
        functools.partial(heads_body, base),
        out_shape=(
            jax.ShapeDtypeStruct((ROWS, CHUNK), f32),
            jax.ShapeDtypeStruct(sent, bf16),
        ),
        grid_spec=pltpu.PrefetchScalarGridSpec(
            num_scalar_prefetch=1,
            grid=(steps,),
            in_specs=[
                whole(normed.shape),
                pl.BlockSpec((16, 128, COLS), lambda i, core: (0, 0, i + first_step)),
                pl.BlockSpec((4, COLS), channels),
                pl.BlockSpec((1, COLS), channels),
                whole(b_all.shape),
                whole(c_all.shape),
                whole(scores.shape),
                pl.BlockSpec((1, heads, ROWS), step),
                pl.BlockSpec((1, heads, ROWS), step),
                pl.BlockSpec((1, ROWS, heads), step),
                pl.BlockSpec((1, ROWS, heads), step),
                pl.BlockSpec(memory_space=pltpu.SMEM),
                pl.BlockSpec((None, PAD, 128), lambda i, core: (g, 0, 0)),
            ],
            out_specs=(
                pl.BlockSpec((ROWS, COLS), lambda i, core: (0, i)),
                whole(sent),
            ),
            scratch_shapes=[
                pltpu.VMEM((2048, COLS), bf16),
                pltpu.VMEM((PAD + ROWS, COLS), f32),
                pltpu.VMEM((COLS // 128, STATE, 128), f32),
            ],
        ),
        compiler_params=params(),
        name="heads",
    )(core, normed, w, taps, bias, b_all, c_all, scores, cum_r, step_r, cum_c, step_c, skip, fades)


def chain_body(parts, out):
    slab = STATE // Y
    pairs = CHUNK // 128
    for g in range(CHUNKS):
        base = g * (pairs * slab + PAD)
        for pair in range(pairs):
            rows = slice(base + pair * slab, base + pair * slab + slab)
            to = slice((g * pairs + pair) * slab, (g * pairs + pair + 1) * slab)
            entering = jnp.zeros((slab, 128), f32)
            for y in range(Y):
                out[y, to, :] = entering.astype(bf16)
                fades = parts[y, base + pairs * slab : base + pairs * slab + PAD, :].astype(f32)
                fade = fades[pair : pair + 1] + fades[pairs + pair : pairs + pair + 1]
                entering = fade * entering + parts[y, rows, :].astype(f32)


def chain_kernel(parts):
    return pl.pallas_call(
        chain_body,
        out_shape=jax.ShapeDtypeStruct((Y, parts.shape[1] - CHUNKS * PAD, 128), bf16),
        compiler_params=params(),
        name="chain",
    )(parts)


def finish_body(core, *refs):
    *locals_, c_all, entering, cum, gain, order, out = refs
    lane = lax.broadcasted_iota(jnp.int32, (GROUP, GROUP), 1)
    row = lax.broadcasted_iota(jnp.int32, (GROUP, GROUP), 0)
    same_head = jnp.where((lane < HEADDIM) == (row < HEADDIM), 1.0 / HEADDIM, 0.0).astype(bf16)
    position = lax.broadcasted_iota(jnp.int32, (POSITIONS, POSITIONS), 1)
    pick = jnp.where(position == order[...], 1.0, 0.0).astype(bf16)
    first = lax.broadcasted_iota(jnp.int32, (1, 128), 1) < HEADDIM
    for frame in range(ROWS // POSITIONS):
        here = slice(frame * POSITIONS, (frame + 1) * POSITIONS)
        parts = []
        step = pl.program_id(0)
        per = CHUNK // COLS
        for pair in range(COLS // 128):
            wide = slice(128 * pair, 128 * pair + 128)
            state = entering[:, pair * (STATE // Y) : (pair + 1) * (STATE // Y), :].reshape(STATE, 128)
            inter = jnp.dot(c_all[here, :], state, preferred_element_type=f32)
            fade = jnp.exp(
                jnp.where(first, cum[0, here, 2 * pair : 2 * pair + 1], cum[0, here, 2 * pair + 1 : 2 * pair + 2])
            )
            local = locals_[0][here, wide]
            for g in range(1, CHUNKS):
                local = jnp.where(step >= g * per, locals_[g][here, wide], local)
            ssm = local + fade * inter
            square = ssm * ssm
            high = square.astype(bf16)
            low = (square - high.astype(f32)).astype(bf16)
            mean = jnp.dot(high, same_head, preferred_element_type=f32) + jnp.dot(
                low, same_head, preferred_element_type=f32
            )
            parts.append((ssm * lax.rsqrt(mean + EPS) * gain[:, wide]).astype(bf16))
        normalized = jnp.concatenate(parts, axis=1)
        picked = jnp.dot(pick, normalized, preferred_element_type=f32).astype(bf16)
        out[:, frame] = picked.reshape(2 * Y, POSITIONS // (2 * Y), COLS)


def finish_kernel(core, locals_, c_all, entering, cum, gain, order):
    steps = OWN // COLS
    per = CHUNK // COLS
    heads = COLS // HEADDIM
    piece = POSITIONS // (2 * Y)

    def chunk_block(g):
        return lambda i, core: (0, jnp.clip(i - g * per, 0, per - 1))

    return pl.pallas_call(
        finish_body,
        out_shape=jax.ShapeDtypeStruct((2 * Y, 2, piece, OWN), bf16),
        grid_spec=pltpu.PrefetchScalarGridSpec(
            num_scalar_prefetch=1,
            grid=(steps,),
            in_specs=[pl.BlockSpec((ROWS, COLS), chunk_block(g)) for g in range(CHUNKS)]
            + [
                whole(c_all.shape),
                pl.BlockSpec((Y, COLS // 128 * (STATE // Y), 128), lambda i, core: (0, i, 0)),
                pl.BlockSpec((1, ROWS, heads), lambda i, core: (i, 0, 0)),
                pl.BlockSpec((1, COLS), lambda i, core: (0, core[0] * steps + i)),
                whole(order.shape),
            ],
            out_specs=pl.BlockSpec((2 * Y, 2, piece, COLS), lambda i, core: (0, 0, 0, i)),
        ),
        compiler_params=params(),
        name="finish",
    )(core, *locals_, c_all, entering, cum, gain, order)


def regroup_body(part, out):
    row = lax.broadcasted_iota(jnp.int32, (POSITIONS, POSITIONS), 0)
    col = lax.broadcasted_iota(jnp.int32, (POSITIONS, POSITIONS), 1)
    piece = POSITIONS // (2 * Y)
    pick = jnp.where(col == (row % (2 * Y)) * piece + row // (2 * Y), 1.0, 0.0).astype(bf16)
    rows = part[...].reshape(POSITIONS, OWN // 2)
    out[...] = jnp.dot(pick, rows, preferred_element_type=f32).astype(bf16)


def regroup_kernel(part):
    half = OWN // 2
    return pl.pallas_call(
        regroup_body,
        out_shape=jax.ShapeDtypeStruct((POSITIONS, 2 * OWN), bf16),
        grid=(4,),
        in_specs=[
            pl.BlockSpec(
                (Y, None, 2, POSITIONS // (2 * Y), half), lambda i: (0, i // 2, 0, 0, i % 2)
            )
        ],
        out_specs=pl.BlockSpec((POSITIONS, half), lambda i: (0, i)),
        compiler_params=params(),
        name="regroup",
    )(part)


def norm_rows(rows, gain):
    widened = rows.astype(f32)
    inverse = lax.rsqrt(jnp.mean(widened * widened, axis=1, keepdims=True) + EPS)
    return (widened * inverse * gain).astype(bf16)


def norm_body(core, own, sibling, gain, out):
    size = 64

    def one(i, carry):
        at = pl.multiple_of(i * size, size)
        mine = pl.multiple_of(PAD + core[0] * POSITIONS + at, PAD)
        other = pl.multiple_of(PAD + (1 - core[0]) * POSITIONS + at, PAD)
        out[pl.ds(mine, size), :] = norm_rows(own[pl.ds(at, size), :], gain[...])
        out[pl.ds(other, size), :] = norm_rows(sibling[pl.ds(at, size), :], gain[...])
        return carry

    out[:PAD, :] = jnp.zeros((PAD, out.shape[1]), bf16)
    lax.fori_loop(0, POSITIONS // size, one, 0)


def norm_kernel(core, own, sibling, gain):
    width = own.shape[1]
    return pl.pallas_call(
        norm_body,
        out_shape=jax.ShapeDtypeStruct((PAD + ROWS, width), bf16),
        in_specs=[pl.BlockSpec(memory_space=pltpu.SMEM)]
        + [pl.BlockSpec(memory_space=pltpu.VMEM) for _ in range(3)],
        compiler_params=params(),
        name="norm",
    )(core, own, sibling, gain)


def tail_body(rows, gain, normed, out):
    out[...] = norm_rows(rows[...], gain[...])


def tail_kernel(rows, gain, normed):
    return pl.pallas_call(
        tail_body,
        out_shape=jax.ShapeDtypeStruct(normed.shape, bf16),
        grid=(1,),
        in_specs=[whole(rows.shape), whole(gain.shape), pl.BlockSpec(memory_space=pl.ANY)],
        out_specs=pl.BlockSpec(rows.shape, lambda i: (0, 0)),
        input_output_aliases={2: 0},
        compiler_params=params(),
        name="tail",
    )(rows, gain, normed)


def decay_body(core, own, other, cum_r, step_r, cum_c, step_c, whole_c, fades):
    count = OWN // HEADDIM
    heads = COLS // HEADDIM
    mine = own[pl.ds(pl.multiple_of(core[0] * count, count), count), :]
    earlier = jnp.where(core[0] == 0, mine, other[...])
    later = jnp.where(core[0] == 0, other[...], mine)
    per = POSITIONS // GROUP
    rows = jnp.concatenate(
        [a[:, GROUP * j : GROUP * j + GROUP] for a in (earlier, later) for j in range(per)], axis=0
    )
    row = lax.broadcasted_iota(jnp.int32, (GROUP, GROUP), 0)
    lane = lax.broadcasted_iota(jnp.int32, (GROUP, GROUP), 1)
    upto = jnp.where(row <= lane, 1.0, 0.0).astype(f32)
    cum = jnp.dot(rows, upto, preferred_element_type=f32, precision=lax.Precision.HIGHEST)
    before = [jnp.zeros((count, 1), f32)]
    for j in range(BLOCKS):
        before.append(before[-1] + cum[count * j : count * j + count, GROUP - 1 : GROUP])
    since = cum + jnp.concatenate(before[:BLOCKS], axis=0)
    turned = [a.T for a in (cum, -rows, since)]
    for i in range(OWN // COLS):
        for j in range(BLOCKS):
            at = slice(GROUP * j, GROUP * j + GROUP)
            some = slice(count * j + heads * i, count * j + heads * i + heads)
            cum_r[i, :, at] = cum[some, :]
            step_r[i, :, at] = -rows[some, :]
            for out, a in zip((cum_c, step_c, whole_c), turned):
                out[i, at, :] = a[:, some]
    fade = jnp.broadcast_to(jnp.exp(before[BLOCKS]), (count, 128))
    first = lax.broadcasted_iota(jnp.int32, (1, 128), 1) < HEADDIM
    pairs = CHUNK // 128
    for g in range(CHUNKS):
        spread_out = jnp.concatenate(
            [
                jnp.where(first, fade[2 * p : 2 * p + 1], fade[2 * p + 1 : 2 * p + 2])
                for p in range(g * pairs, g * pairs + pairs)
            ],
            axis=0,
        )
        high = spread_out.astype(bf16).astype(f32)
        fill = jnp.zeros((PAD - 2 * pairs, 128), f32)
        fades[g] = jnp.concatenate([high, spread_out - high, fill], axis=0).astype(bf16)


def decay_kernel(core, own, other):
    steps = OWN // COLS
    heads = COLS // HEADDIM
    in_rows = jax.ShapeDtypeStruct((steps, heads, ROWS), f32)
    in_columns = jax.ShapeDtypeStruct((steps, ROWS, heads), f32)
    return pl.pallas_call(
        decay_body,
        out_shape=(
            in_rows, in_rows, in_columns, in_columns, in_columns,
            jax.ShapeDtypeStruct((CHUNKS, PAD, 128), bf16),
        ),
        in_specs=[pl.BlockSpec(memory_space=pltpu.SMEM)]
        + [pl.BlockSpec(memory_space=pltpu.VMEM) for _ in range(2)],
        compiler_params=params(),
        name="decay",
    )(core, own, other)


def on_device(
    tokens, in_gain, in_weight, conv_weight, conv_bias, log_decay, skip, out_gain, scan_order
):
    seq = lax.axis_index("seq")
    core = seq % 2
    y = seq // 2
    swap = [(i, i ^ 1) for i in range(2 * Y)]
    onward = [(i, i + 2) for i in range(2 * Y - 2)]
    head_count = OWN // HEADDIM
    which = core.astype(jnp.int32)[None]

    weight = jnp.concatenate(
        [in_weight[:, 2 * OWN :], lax.dynamic_slice_in_dim(in_weight, core * OWN, OWN, 1)], axis=1
    )
    half = lax.dynamic_slice_in_dim(weight, (y % 2) * 32, 32, 0)
    far = spread(half, far_groups()).reshape(128, 2 * STATE + OWN)
    cuts = [0] + [2 * STATE + (g + 1) * CHUNK for g in range(CHUNKS)]
    far_chunks = [far[:, a:b] for a, b in zip(cuts, cuts[1:])]
    chunks = [spread(far_chunks[0], near_groups())]

    own = tokens[0]
    gain = in_gain[None, :]
    sibling = lax.ppermute(own, "seq", swap)
    tail = jnp.where(core == 1, own[POSITIONS - PAD :], sibling[POSITIONS - PAD :])
    tail = lax.ppermute(tail, "seq", onward)
    normed = norm_kernel(which, own, sibling, gain)
    other = lax.dynamic_slice_in_dim(log_decay[0], (1 - core) * head_count, head_count, 0)
    decays = decay_kernel(which, log_decay[0], lax.ppermute(other, "seq", swap))
    bias = conv_bias[None, :]
    last_gain = out_gain[None, :]
    order = scan_order[:, None]

    normed, tail, decays, bias, last_gain, order, far_chunks = lax.optimization_barrier(
        (normed, tail, decays, bias, last_gain, order, far_chunks)
    )
    cum_r, step_r, cum_c, step_c, whole_c, fades = decays
    normed = tail_kernel(tail, gain, normed)
    chunks += [spread(a, near_groups()) for a in far_chunks[1:]]

    b_all, c_all, scores = bc_kernel(normed, chunks[0], conv_weight, bias)
    same_core = [list(range(c, 2 * Y, 2)) for c in range(2)]
    locals_, sents = [], []
    for g in range(CHUNKS):
        local, sent = heads_kernel(
            which, g, normed, chunks[g], 1 if g == 0 else 0, conv_weight, bias,
            b_all, c_all, scores, cum_r, step_r, cum_c, step_c, skip, fades,
        )
        locals_.append(local)
        sents.append(sent)
    parts = lax.all_to_all(
        jnp.concatenate(sents, axis=1), "seq", 0, 0, axis_index_groups=same_core, tiled=True
    )
    entering = lax.all_to_all(
        chain_kernel(parts), "seq", 0, 0, axis_index_groups=same_core, tiled=True
    )
    outgoing = finish_kernel(which, locals_, c_all, entering, whole_c, last_gain, order)
    back = lax.all_to_all(outgoing, "seq", 0, 0, tiled=True)
    return regroup_kernel(back.reshape(Y, 2, 2, POSITIONS // (2 * Y), OWN))[None]


def solution(mesh):
    in_specs = (
        P("dp", "seq", None),
        P(),
        P("dp", None),
        P(),
        P(),
        P("dp", None, "seq"),
        P(),
        P(),
        P(),
    )
    out_specs = P("dp", "seq", None)
    return jax.shard_map(
        on_device, mesh=mesh, in_specs=in_specs, out_specs=out_specs, check_vma=False
    )
```

time: 250 us -> 227 us (0.908)
  blocking collectives: 26.1 us -> 96.7 us
  waiting for transfers between devices: 66 us -> 26.3 us
  local copies, waits for them, and re-layouts: 37.8 us -> 10.1 us
  other arithmetic: 21.3 us -> 1.84 us
  starting transfers between devices: 42.7 us -> 26.5 us
  Pallas kernels: 54.1 us -> 64.7 us
    all_to_all x0 -> x2, blocking collectives: none -> 76.4 us  [the longest x1 60 us: on_device(): back = lax.all_to_all(outgoing, 'seq', 0, 0, tiled=True)]
    all_to_all x3 -> x0, waiting for transfers between devices: 58.1 us -> none  [the longest x2 47.3 us: on_device(): back = lax.all_to_all(outgoing, 'seq', 0, 0, tiled=True)]
    all_to_all x3 -> x0, starting transfers between devices: 16.6 us -> none  [the longest x2 10.7 us: on_device(): back = lax.all_to_all(outgoing, 'seq', 0, 0, tiled=True)]
    slice x22 -> x0, local copies, waits for them, and re-layouts: 14.8 us -> none  [the longest x3 5.9 us: on_device(): step_r[steps]]
    pallas_call x2 -> x5, Pallas kernels: 28.4 us -> 41.7 us  [the longest x2 28.5 us: heads_kernel(): pl.pallas_call(functools.partial(heads_body, base), out_shape=(jax.ShapeD...]
    ppermute x1, waiting for transfers between devices: 0.01 us -> 8.69 us  [on_device(): tail = lax.ppermute(tail, 'seq', onward)]
    all_to_all x1, blocking collectives: 26.1 us -> 20.3 us  [spread(): lax.all_to_all(jnp.broadcast_to(block[None], (count,) + block.shape), ('d...]
    convert_element_type x3 -> x0, other arithmetic: 5.56 us -> none  [the longest x2 5.55 us: norm(): return (widened * inverse * in_gain[None, :]).astype(bf16)]
  transfers between devices with their start and end apart: 9 -> 6, of which waited for: 5 -> 6; matrix products, arithmetic and copies ran while one was open for 19% -> 1% of each run, Pallas kernels for 12% -> 15%
where the time goes in v3:
time: 227 us; the launch traced here: 226 us
  blocking collectives  96.7 us (43%)
  Pallas kernels  64.7 us (29%)
  starting transfers between devices  26.5 us (12%)
  waiting for transfers between devices  26.3 us (12%)
  local copies, waits for them, and re-layouts  10.1 us (4%)
    all_to_all x1, blocking collectives, on_device(): back = lax.all_to_all(outgoing, 'seq', 0, 0, tiled=True)  60 us
    pallas_call x2, Pallas kernels, heads_kernel(): pl.pallas_call(functools.partial(heads_body, base), out_shape=(jax.ShapeD...  28.5 us
    all_to_all x1, blocking collectives, spread(): lax.all_to_all(jnp.broadcast_to(block[None], (count,) + block.shape), ('d...  20.3 us
    all_to_all x1, blocking collectives, on_device(): lax.all_to_all(jnp.concatenate(sents, axis=1), 'seq', 0, 0, axis_index_gr...  16.4 us
    all_to_all x2, starting transfers between devices, spread(): lax.all_to_all(jnp.broadcast_to(block[None], (count,) + block.shape), ('d...  12.9 us
    pallas_call x1, Pallas kernels, finish_kernel(): pl.pallas_call(finish_body, out_shape=jax.ShapeDtypeStruct((2 * Y, 2, pie...  9.82 us
    ppermute x1, waiting for transfers between devices, on_device(): tail = lax.ppermute(tail, 'seq', onward)  8.69 us
    all_to_all x1, waiting for transfers between devices, on_device(): lax.all_to_all(chain_kernel(parts), 'seq', 0, 0, axis_index_groups=same_c...  8.47 us
  transfers between devices with their start and end apart: 6, of which 6 were waited for; matrix products, arithmetic and copies ran while one was open for 1% of the time, Pallas kernels for 15%

profile of v3, /device:TPU:1, one launch (start us, length us, event | category | flops | bytes accessed | tf_op | source)
XLA Modules:
  0.0 226.3 jit_solution(6860318087351160283)
XLA Ops:
  0.0 0.8 slice.21
  0.8 0.9 constant_dynamic-slice_fusion
  1.7 20.3 %all_to_all.30 = bf16[4,32,1280]{2,1,0:T(8,128)(2,1)S(1)} all-to-all(bf16[4,32,1280]{2,1,0:T(8,128)(2,1)S(1)} %broadcast_in_dim.41), channel_id=1, replica_groups={{0,128,256,384},{1,129,257,385},{2,130,258,386},{3,131,259,387},{4,132,..., dimensions={0} | all-to-all | bytes 655360 | tf_op jit(solution)/shard_map/all_to_all | solution.py:53
  22.1 2.0 broadcast_in_dim.42
  24.1 0.0 copy-start.4
  24.1 0.0 copy-start.7
  24.1 8.0 %all-to-all-start.1 = ((bf16[16,128,768]{2,1,0:T(8,128)(2,1)}), bf16[16,128,768]{2,1,0:T(8,128)(2,1)S(1)}, u32[]{:S(2)}, u32[]{:S(2)}) async-start(bf16[16,128,768]{2,1,0:T(8,128)(2,1)} %broadcast_in_dim.42), calls=%async_computation.1 | async-start | bytes 6291456 | tf_op jit(solution)/shard_map/all_to_all | solution.py:53
  32.1 4.0 %collective-permute-start = (bf16[512,2048]{1,0:T(8,128)(2,1)}, bf16[512,2048]{1,0:T(8,128)(2,1)}, u32[]{:S(2)}, u32[]{:S(2)}) collective-permute-start(bf16[512,2048]{1,0:T(8,128)(2,1)} %bitcast.14), channel_id=1, source_target_pairs={{0,1},{1,0},{2,3},{3,2},{4,5},{5,4},{6,7},{7,6},{8,9},{9,8},{10,11... | collective-permute-start | bytes 6291464 | tf_op jit(solution)/shard_map/ppermute | solution.py:486
  36.1 4.1 %collective-permute-done.sibling = bf16[512,2048]{1,0:T(8,128)(2,1)} collective-permute-done((bf16[512,2048]{1,0:T(8,128)(2,1)}, bf16[512,2048]{1,0:T(8,128)(2,1)}, u32[]{:S(2)}, u32[]{:S(2)}) %collective-permute-start) | collective-permute-done | bytes 2097184 | tf_op jit(solution)/shard_map/ppermute | solution.py:486
  40.2 0.9 slice_select_fusion
  41.1 3.5 %collective-permute-start.1 = (bf16[16,2048]{1,0:T(8,128)(2,1)S(1)}, bf16[16,2048]{1,0:T(8,128)(2,1)S(1)}, u32[]{:S(2)}, u32[]{:S(2)}) collective-permute-start(bf16[16,2048]{1,0:T(8,128)(2,1)S(1)} %slice_select_fusion), channel_id=1, source_target_pairs={{0,2},{1,3},{2,4},{3,5},{4,6},{5,7},{6,8},{7,9},{8,10},{9,11},{10,... | collective-permute-start | bytes 196616 | tf_op jit(solution)/shard_map/ppermute | solution.py:488
  44.7 0.0 copy-done.4
  44.7 2.6 %collective-permute-start.2 = (f32[16,512]{1,0:T(8,128)S(1)}, f32[16,512]{1,0:T(8,128)S(1)}, u32[]{:S(2)}, u32[]{:S(2)}) collective-permute-start(f32[16,512]{1,0:T(8,128)S(1)} %dynamic-slice_bitcast_fusion), channel_id=1, source_target_pairs={{0,1},{1,0},{2,3},{3,2},{4,5},{5,4},{6,7},{7,6},{8,9},{9,8},{10,11... | collective-permute-start | bytes 98312 | tf_op jit(solution)/shard_map/ppermute | solution.py:491
  47.3 0.0 copy-done.7
  47.3 0.6 broadcast_in_dim.38.bias
  47.9 0.2 collective-permute-done.2.other
  48.1 0.0 copy-start.6
  48.1 0.6 copy-done.6
  48.7 5.6 %decay.1 = (f32[4,4,1024]{2,1,0:T(4,128)}, f32[4,4,1024]{2,1,0:T(4,128)}, f32[4,1024,4]{2,1,0:T(8,128)}, f32[4,1024,4]{2,1,0:T(8,128)}, f32[4,1024,4]{2,1,0:T(8,128)}, /*index=5*/bf16[2,16,128]{2,1,0:T(8,128)(2,1)}) custom-call(s32[1]{0:T(128)} %bitcast.core, f32[32,512]{1,0:T(8,128)} %bitcast.18, f32[16,512]{1,0:T(8,128)} %copy-done.6), custom_call_target="tpu_custom_call" | custom-call | tf_op jit(solution)/shard_map/decay/pallas_call | solution.py:451
  54.3 0.6 slice.26
  54.9 0.0 copy-start.2
  54.9 6.0 %norm.1.normed = bf16[1040,2048]{1,0:T(8,128)(2,1)} custom-call(s32[1]{0:T(128)} %bitcast.core, bf16[512,2048]{1,0:T(8,128)(2,1)} %bitcast.15, bf16[512,2048]{1,0:T(8,128)(2,1)} %collective-permute-done.sibling, f32[1,2048]{1,0:T(1,128)} %bitcast.19), custom_call_target="tpu_custom_call" | custom-call | tf_op jit(solution)/shard_map/norm/pallas_call | solution.py:376
  61.0 8.7 %collective-permute-done.1.rows = bf16[16,2048]{1,0:T(8,128)(2,1)S(1)} collective-permute-done((bf16[16,2048]{1,0:T(8,128)(2,1)S(1)}, bf16[16,2048]{1,0:T(8,128)(2,1)S(1)}, u32[]{:S(2)}, u32[]{:S(2)}) %collective-permute-start.1) | collective-permute-done | bytes 65568 | tf_op jit(solution)/shard_map/ppermute | solution.py:488
  69.7 0.6 copy-done.5
  70.3 0.6 all-to-all-done.1.w
  70.9 0.0 copy-done.2
  70.9 1.7 broadcast_in_dim.43
  72.5 0.7 copy-done
  73.2 4.9 %all-to-all-start.2 = ((bf16[16,128,512]{2,1,0:T(8,128)(2,1)}), bf16[16,128,512]{2,1,0:T(8,128)(2,1)}, u32[]{:S(2)}, u32[]{:S(2)}) async-start(bf16[16,128,512]{2,1,0:T(8,128)(2,1)} %broadcast_in_dim.43), calls=%async_computation.2 | async-start | bytes 4194304 | tf_op jit(solution)/shard_map/all_to_all | solution.py:53
  78.2 1.6 tail.1.normed
  79.7 6.8 %bc.1 = (bf16[1024,128]{1,0:T(8,128)(2,1)}, bf16[1024,128]{1,0:T(8,128)(2,1)}, f32[1024,128]{1,0:T(8,128)}) custom-call(bf16[1040,2048]{1,0:T(8,128)(2,1)} %tail.1.normed, bf16[16,128,768]{2,1,0:T(8,128)(2,1)} %copy-done, f32[4,2304]{1,0:T(4,128)} %taps.5, f32[1,2304]{1,0:T(1,128)} %broadcast_in_dim.38.bias), custom_call_target="tpu_custom_call" | custom-call | tf_op jit(solution)/shard_map/bc/pallas_call | solution.py:101
  86.6 14.2 %heads.2 = (f32[1024,512]{1,0:T(8,128)}, bf16[8,80,128]{2,1,0:T(8,128)(2,1)}) custom-call(s32[1]{0:T(128)} %bitcast.core, bf16[1040,2048]{1,0:T(8,128)(2,1)} %tail.1.normed, bf16[16,128,768]{2,1,0:T(8,128)(2,1)} %copy-done, f32[4,2304]{1,0:T(4,128)} %taps.5, f32[1,2304]{1,0:T(1,128)} %broadcast_in_dim.38.bias, bf16[1024,128]{1,0:T(8,128)(2,1)} %get-tuple-element.39.b_all, ...), custom_call_target="tpu_custom_call" | custom-call | tf_op jit(solution)/shard_map/heads/pallas_call | solution.py:197
  100.8 0.0 copy-start.3
  100.8 4.3 %all-to-all-done.2.w = bf16[16,128,512]{2,1,0:T(8,128)(2,1)} async-done(((bf16[16,128,512]{2,1,0:T(8,128)(2,1)}), bf16[16,128,512]{2,1,0:T(8,128)(2,1)}, u32[]{:S(2)}, u32[]{:S(2)}) %all-to-all-start.2) | async-done | bytes 2097184 | tf_op jit(solution)/shard_map/all_to_all | solution.py:53
  105.0 14.3 %heads.3 = (f32[1024,512]{1,0:T(8,128)}, bf16[8,80,128]{2,1,0:T(8,128)(2,1)}) custom-call(s32[1]{0:T(128)} %bitcast.core, bf16[1040,2048]{1,0:T(8,128)(2,1)} %tail.1.normed, bf16[16,128,512]{2,1,0:T(8,128)(2,1)} %all-to-all-done.2.w, f32[4,2304]{1,0:T(4,128)} %taps.5, f32[1,2304]{1,0:T(1,128)} %broadcast_in_dim.38.bias, ...), custom_call_target="tpu_custom_call" | custom-call | tf_op jit(solution)/shard_map/heads/pallas_call | solution.py:197
  119.3 0.0 copy-start.8
  119.3 0.0 copy-done.3
  119.3 0.9 pad_maximum_fusion
  120.3 16.4 %all_to_all.31.parts = bf16[8,160,128]{2,1,0:T(8,128)(2,1)} all-to-all(bf16[8,160,128]{2,1,0:T(8,128)(2,1)S(1)} %pad_maximum_fusion), channel_id=1, replica_groups={{0,2,4,6,8,10,12,14},{1,3,5,7,9,11,13,15},{16,18,20,22,24,26,28,30},{17..., dimensions={0} | all-to-all | bytes 655360 | tf_op jit(solution)/shard_map/all_to_all | solution.py:513
  136.7 1.7 chain.1
  138.4 3.4 %all-to-all-start.4 = ((bf16[8,128,128]{2,1,0:T(8,128)(2,1)}), bf16[8,128,128]{2,1,0:T(8,128)(2,1)S(1)}, u32[]{:S(2)}, u32[]{:S(2)}) async-start(bf16[8,128,128]{2,1,0:T(8,128)(2,1)} %chain.1), calls=%async_computation.4 | async-start | bytes 524288 | tf_op jit(solution)/shard_map/all_to_all | solution.py:516
  141.8 0.0 copy-done.8
  141.8 0.9 copy.11.refs_6_
  142.7 8.5 %all-to-all-done.4.refs_3_ = bf16[8,128,128]{2,1,0:T(8,128)(2,1)S(1)} async-done(((bf16[8,128,128]{2,1,0:T(8,128)(2,1)}), bf16[8,128,128]{2,1,0:T(8,128)(2,1)S(1)}, u32[]{:S(2)}, u32[]{:S(2)}) %all-to-all-start.4) | async-done | bytes 262176 | tf_op jit(solution)/shard_map/all_to_all | solution.py:516
  151.2 0.7 copy-done.1
  151.9 9.8 %finish.1 = bf16[16,2,32,1024]{3,2,1,0:T(8,128)(2,1)} custom-call(s32[1]{0:T(128)} %bitcast.core, f32[1024,512]{1,0:T(8,128)} %get-tuple-element.47.refs_0_, f32[1024,512]{1,0:T(8,128)} %get-tuple-element.49.refs_1_, bf16[1024,128]{1,0:T(8,128)(2,1)} %get-tuple-element.40.c_all.refs_2_, bf16[8,128,128]{2,1,0:T(8,128)(2,1)} %copy-done.1, ...), custom_call_target="tpu_custom_call" | custom-call | tf_op jit(solution)/shard_map/finish/pallas_call | solution.py:306
  161.7 60.0 %all_to_all.32 = bf16[16,2,32,1024]{3,2,1,0:T(8,128)(2,1)} all-to-all(bf16[16,2,32,1024]{3,2,1,0:T(8,128)(2,1)} %finish.1), channel_id=1, replica_groups=mesh['dp'=32,'seq'=16] {'seq'}, dimensions={0} | all-to-all | bytes 4194304 | tf_op jit(solution)/shard_map/all_to_all | solution.py:520
  221.7 4.6 %regroup.1 = bf16[512,2048]{1,0:T(8,128)(2,1)} custom-call(bf16[8,2,2,32,1024]{4,3,2,1,0:T(8,128)(2,1)} %bitcast.13), custom_call_target="tpu_custom_call" | custom-call | tf_op jit(solution)/shard_map/regroup/pallas_call | solution.py:338
  (7 shorter events, 0.1 us)
Async XLA Ops:
  24.1 20.6 %copy-start.4 = (f32[1,32,512]{2,1,0:T(8,128)S(1)}, f32[1,32,512]{2,1,0:T(8,128)}, u32[]{:S(2)}) copy-start(f32[1,32,512]{2,1,0:T(8,128)} %param.14) | copy-start | bytes 196612
  24.1 23.2 %copy-start.7 = (f32[2304]{0:T(1024)S(1)}, f32[2304]{0:T(1024)}, u32[]{:S(2)}) copy-start(f32[2304]{0:T(1024)} %param.13) | copy-start | bytes 27652
  24.1 46.8 %all-to-all-start.1 = ((bf16[16,128,768]{2,1,0:T(8,128)(2,1)}), bf16[16,128,768]{2,1,0:T(8,128)(2,1)S(1)}, u32[]{:S(2)}, u32[]{:S(2)}) async-start(bf16[16,128,768]{2,1,0:T(8,128)(2,1)} %broadcast_in_dim.42), calls=%async_computation.1 | async-start | bytes 6291456 | tf_op jit(solution)/shard_map/all_to_all | solution.py:53
  32.1 8.2 %collective-permute-start = (bf16[512,2048]{1,0:T(8,128)(2,1)}, bf16[512,2048]{1,0:T(8,128)(2,1)}, u32[]{:S(2)}, u32[]{:S(2)}) collective-permute-start(bf16[512,2048]{1,0:T(8,128)(2,1)} %bitcast.14), channel_id=1, source_target_pairs={{0,1},{1,0},{2,3},{3,2},{4,5},{5,4},{6,7},{7,6},{8,9},{9,8},{10,11... | collective-permute-start | bytes 6291464 | tf_op jit(solution)/shard_map/ppermute | solution.py:486
  41.1 28.5 %collective-permute-start.1 = (bf16[16,2048]{1,0:T(8,128)(2,1)S(1)}, bf16[16,2048]{1,0:T(8,128)(2,1)S(1)}, u32[]{:S(2)}, u32[]{:S(2)}) collective-permute-start(bf16[16,2048]{1,0:T(8,128)(2,1)S(1)} %slice_select_fusion), channel_id=1, source_target_pairs={{0,2},{1,3},{2,4},{3,5},{4,6},{5,7},{6,8},{7,9},{8,10},{9,11},{10,... | collective-permute-start | bytes 196616 | tf_op jit(solution)/shard_map/ppermute | solution.py:488
  44.7 3.4 %collective-permute-start.2 = (f32[16,512]{1,0:T(8,128)S(1)}, f32[16,512]{1,0:T(8,128)S(1)}, u32[]{:S(2)}, u32[]{:S(2)}) collective-permute-start(f32[16,512]{1,0:T(8,128)S(1)} %dynamic-slice_bitcast_fusion), channel_id=1, source_target_pairs={{0,1},{1,0},{2,3},{3,2},{4,5},{5,4},{6,7},{7,6},{8,9},{9,8},{10,11... | collective-permute-start | bytes 98312 | tf_op jit(solution)/shard_map/ppermute | solution.py:491
  48.1 0.6 copy-start.6
  54.9 15.9 %copy-start.2 = (bf16[128,512]{1,0:T(8,128)(2,1)S(1)}, bf16[128,512]{1,0:T(8,128)(2,1)}, u32[]{:S(2)}) copy-start(bf16[128,512]{1,0:T(8,128)(2,1)} %slice.26) | copy-start | bytes 393220
  69.6 0.6 copy-start.5
  70.9 2.3 %copy-start = (bf16[16,128,768]{2,1,0:T(8,128)(2,1)}, bf16[16,128,768]{2,1,0:T(8,128)(2,1)S(1)}, u32[]{:S(2)}) copy-start(bf16[16,128,768]{2,1,0:T(8,128)(2,1)S(1)} %all-to-all-done.1.w) | copy-start | bytes 9437188
  73.2 31.8 %all-to-all-start.2 = ((bf16[16,128,512]{2,1,0:T(8,128)(2,1)}), bf16[16,128,512]{2,1,0:T(8,128)(2,1)}, u32[]{:S(2)}, u32[]{:S(2)}) async-start(bf16[16,128,512]{2,1,0:T(8,128)(2,1)} %broadcast_in_dim.43), calls=%async_computation.2 | async-start | bytes 4194304 | tf_op jit(solution)/shard_map/all_to_all | solution.py:53
  100.8 18.6 %copy-start.3 = (bf16[8,80,128]{2,1,0:T(8,128)(2,1)S(1)}, bf16[8,80,128]{2,1,0:T(8,128)(2,1)}, u32[]{:S(2)}) copy-start(bf16[8,80,128]{2,1,0:T(8,128)(2,1)} %get-tuple-element.50) | copy-start | bytes 491524
  119.3 22.5 %copy-start.8 = (s32[512]{0:T(512)S(1)}, s32[512]{0:T(512)}, u32[]{:S(2)}) copy-start(s32[512]{0:T(512)} %param.17) | copy-start | bytes 6148
  138.4 12.8 %all-to-all-start.4 = ((bf16[8,128,128]{2,1,0:T(8,128)(2,1)}), bf16[8,128,128]{2,1,0:T(8,128)(2,1)S(1)}, u32[]{:S(2)}, u32[]{:S(2)}) async-start(bf16[8,128,128]{2,1,0:T(8,128)(2,1)} %chain.1), calls=%async_computation.4 | async-start | bytes 524288 | tf_op jit(solution)/shard_map/all_to_all | solution.py:516
  151.2 0.7 copy-start.1

commit v4 on v3

--- a/solution.py
+++ b/solution.py
@@ -16,8 +16,8 @@
 BLOCKS = ROWS // GROUP
 OWN = 1024
 COLS = 256
-CHUNKS = 2
-CHUNK = OWN // CHUNKS
+PARTS = (1, 2, 1)
+LOG2E = 1.4426950408889634
 EPS = 1e-05
 
 Z, X, Y = 8, 4, 8
@@ -73,11 +73,12 @@
 
 
 def mixed_rows(start, taps, bias, p_all):
-    rows = p_all[pl.ds(pl.multiple_of(start + 8, 8), GROUP + 8), :]
-    pre = bias[...] + taps[0:1, :] * rows[5 : 5 + GROUP]
+    rows = p_all.at[pl.ds(pl.multiple_of(start + 8, 8), GROUP + 8), :]
+    pre = bias[...] + taps[0:1, :] * rows[5 : 5 + GROUP, :]
     for k in range(1, 4):
-        pre = pre + taps[k : k + 1, :] * rows[5 + k : 5 + k + GROUP]
-    return (pre / (1.0 + jnp.exp(-pre))).astype(bf16)
+        pre = pre + taps[k : k + 1, :] * rows[5 + k : 5 + k + GROUP, :]
+    half = 0.5 * pre
+    return (half + half * jnp.tanh(half)).astype(bf16)
 
 
 def bc_body(normed, w, taps, bias, b_out, c_out, scores, w_all, p_all):
@@ -120,13 +121,25 @@
 
 
 def heads_body(
-    base, core, normed, w, taps, bias, b_all, c_all, scores_all, cum_r, step_r, cum_c, step_c, skip, fades,
-    local, sent, w_all, p_all, state,
+    base, core, normed, w, taps, bias, b_all, c_all, scores_all, cum_c, cum_r, e_in, e_out, skip, fades,
+    *refs,
 ):
+    local, sent, w_all, p_all, state = refs[-5:]
+    i = pl.program_id(0)
+
+    @pl.when(i == 0)
+    def _():
+        if base:
+            sent[...] = refs[1][...]
+        else:
+            for y in range(Y):
+                sent[y, sent.shape[1] - PAD :, :] = fades[...]
+
     project_and_mix(normed, w, taps, bias, w_all, p_all)
     state[...] = jnp.zeros_like(state)
     heads = COLS // HEADDIM
-    head = core[0] * (OWN // HEADDIM) + (base + pl.program_id(0)) * heads
+    pairs = COLS // 128
+    head = core[0] * (OWN // HEADDIM) + (base + i) * heads
     row = lax.broadcasted_iota(jnp.int32, (GROUP, GROUP), 0)
     lane = lax.broadcasted_iota(jnp.int32, (GROUP, GROUP), 1)
     causal = lane <= row
@@ -139,54 +152,45 @@
         b = b_all[here, :]
         c = c_all[here, :]
         scores = scores_all[here, :]
-        for pair in range(COLS // 128):
+        for pair in range(pairs):
             wide = slice(128 * pair, 128 * pair + 128)
             x = mixed[:, wide].astype(f32)
-            cums, steps, weights = [], [], []
+            weights = []
             for h in (2 * pair, 2 * pair + 1):
                 cum = jnp.broadcast_to(cum_c[0, here, h : h + 1], (GROUP, GROUP))
                 gap = cum - cum_r[0, h : h + 1, here]
-                decay = jnp.exp(jnp.where(causal, gap, -1e30))
-                weights.append((scores * decay * step_r[0, h : h + 1, here]).astype(bf16))
-                cums.append(cum)
-                steps.append(jnp.broadcast_to(step_c[0, here, h : h + 1], (GROUP, GROUP)))
+                weights.append((scores * jnp.exp2(jnp.where(causal, gap, -1e30))).astype(bf16))
             both = jnp.concatenate(weights, axis=1)
             apart = jnp.concatenate(
                 [jnp.where(first, x, 0.0).astype(bf16), jnp.where(first, 0.0, x).astype(bf16)], axis=0
             )
             intra = jnp.dot(both, apart, preferred_element_type=f32)
-            cum = jnp.where(first, cums[0], cums[1])
-            step = jnp.where(first, steps[0], steps[1])
-            closing = cum[GROUP - 1 : GROUP, :]
-            scaled = (jnp.exp(closing - cum) * step * x).astype(bf16)
+            scaled = (e_out[here, wide] * x).astype(bf16)
             block_state = lax.dot_general(
                 b, scaled, (((0,), (0,)), ((), ())), preferred_element_type=f32
             )
             entering = state[pair]
-            inter = jnp.exp(cum) * jnp.dot(c, entering.astype(bf16), preferred_element_type=f32)
+            fade = e_in[here, wide]
+            inter = fade * jnp.dot(c, entering.astype(bf16), preferred_element_type=f32)
             gains = jnp.where(first, skip[head + 2 * pair], skip[head + 2 * pair + 1])
             local[here, wide] = intra + inter + gains * x
-            state[pair] = jnp.exp(closing) * entering + block_state
+            state[pair] = fade[GROUP - 1 :, :] * entering + block_state
         return carry
 
     lax.fori_loop(0, BLOCKS, one, 0)
-    pairs = COLS // 128
     slab = STATE // Y
-    fade_row = sent.shape[1] - PAD
     for y in range(Y):
         for pair in range(pairs):
-            at = pl.multiple_of((pl.program_id(0) * pairs + pair) * slab, slab)
+            at = pl.multiple_of(((base + i) * pairs + pair) * slab, slab)
             sent[y, pl.ds(at, slab), :] = state[pair, slab * y : slab * y + slab, :].astype(bf16)
-        sent[y, fade_row:, :] = fades[...]
 
 
 def heads_kernel(
-    core, g, normed, w, first_step, taps, bias, b_all, c_all, scores, cum_r, step_r, cum_c, step_c, skip, fades
+    core, base, steps, normed, w, first_step, taps, bias, b_all, c_all, scores, cum_c, cum_r, e_in, e_out,
+    skip, fades, earlier,
 ):
-    steps = CHUNK // COLS
     heads = COLS // HEADDIM
-    base = g * steps
-    sent = (Y, CHUNK // 128 * (STATE // Y) + PAD, 128)
+    sent = (Y, OWN // 128 * (STATE // Y) + PAD, 128)
 
     def channels(i, core):
         return (0, core[0] * (OWN // COLS) + base + i)
@@ -194,10 +198,13 @@
     def step(i, core):
         return (base + i, 0, 0)
 
+    def column(i, core):
+        return (0, base + i)
+
     return pl.pallas_call(
         functools.partial(heads_body, base),
         out_shape=(
-            jax.ShapeDtypeStruct((ROWS, CHUNK), f32),
+            jax.ShapeDtypeStruct((ROWS, OWN), f32),
             jax.ShapeDtypeStruct(sent, bf16),
         ),
         grid_spec=pltpu.PrefetchScalarGridSpec(
@@ -211,15 +218,16 @@
                 whole(b_all.shape),
                 whole(c_all.shape),
                 whole(scores.shape),
+                pl.BlockSpec((1, ROWS, heads), step),
                 pl.BlockSpec((1, heads, ROWS), step),
-                pl.BlockSpec((1, heads, ROWS), step),
-                pl.BlockSpec((1, ROWS, heads), step),
-                pl.BlockSpec((1, ROWS, heads), step),
+                pl.BlockSpec((ROWS, COLS), column),
+                pl.BlockSpec((ROWS, COLS), column),
                 pl.BlockSpec(memory_space=pltpu.SMEM),
-                pl.BlockSpec((None, PAD, 128), lambda i, core: (g, 0, 0)),
-            ],
+                whole(fades.shape),
+            ]
+            + ([pl.BlockSpec(memory_space=pl.ANY), whole(sent)] if earlier else []),
             out_specs=(
-                pl.BlockSpec((ROWS, COLS), lambda i, core: (0, i)),
+                pl.BlockSpec((ROWS, COLS), column),
                 whole(sent),
             ),
             scratch_shapes=[
@@ -228,60 +236,52 @@
                 pltpu.VMEM((COLS // 128, STATE, 128), f32),
             ],
         ),
+        input_output_aliases={14: 0, 15: 1} if earlier else {},
         compiler_params=params(),
         name="heads",
-    )(core, normed, w, taps, bias, b_all, c_all, scores, cum_r, step_r, cum_c, step_c, skip, fades)
+    )(
+        core, normed, w, taps, bias, b_all, c_all, scores, cum_c, cum_r, e_in, e_out, skip, fades,
+        *earlier,
+    )
 
 
 def chain_body(parts, out):
     slab = STATE // Y
-    pairs = CHUNK // 128
-    for g in range(CHUNKS):
-        base = g * (pairs * slab + PAD)
-        for pair in range(pairs):
-            rows = slice(base + pair * slab, base + pair * slab + slab)
-            to = slice((g * pairs + pair) * slab, (g * pairs + pair + 1) * slab)
-            entering = jnp.zeros((slab, 128), f32)
-            for y in range(Y):
-                out[y, to, :] = entering.astype(bf16)
-                fades = parts[y, base + pairs * slab : base + pairs * slab + PAD, :].astype(f32)
-                fade = fades[pair : pair + 1] + fades[pairs + pair : pairs + pair + 1]
-                entering = fade * entering + parts[y, rows, :].astype(f32)
+    pairs = OWN // 128
+    base = pairs * slab
+    for pair in range(pairs):
+        rows = slice(pair * slab, pair * slab + slab)
+        entering = jnp.zeros((slab, 128), f32)
+        for y in range(Y):
+            out[y, rows, :] = entering.astype(bf16)
+            fades = parts[y, base:, :].astype(f32)
+            fade = fades[pair : pair + 1] + fades[pairs + pair : pairs + pair + 1]
+            entering = fade * entering + parts[y, rows, :].astype(f32)
 
 
 def chain_kernel(parts):
     return pl.pallas_call(
         chain_body,
-        out_shape=jax.ShapeDtypeStruct((Y, parts.shape[1] - CHUNKS * PAD, 128), bf16),
+        out_shape=jax.ShapeDtypeStruct((Y, parts.shape[1] - PAD, 128), bf16),
         compiler_params=params(),
         name="chain",
     )(parts)
 
 
-def finish_body(core, *refs):
-    *locals_, c_all, entering, cum, gain, order, out = refs
+def finish_body(core, local, c_all, entering, fade, gain, order, out):
     lane = lax.broadcasted_iota(jnp.int32, (GROUP, GROUP), 1)
     row = lax.broadcasted_iota(jnp.int32, (GROUP, GROUP), 0)
     same_head = jnp.where((lane < HEADDIM) == (row < HEADDIM), 1.0 / HEADDIM, 0.0).astype(bf16)
     position = lax.broadcasted_iota(jnp.int32, (POSITIONS, POSITIONS), 1)
     pick = jnp.where(position == order[...], 1.0, 0.0).astype(bf16)
-    first = lax.broadcasted_iota(jnp.int32, (1, 128), 1) < HEADDIM
     for frame in range(ROWS // POSITIONS):
         here = slice(frame * POSITIONS, (frame + 1) * POSITIONS)
         parts = []
-        step = pl.program_id(0)
-        per = CHUNK // COLS
         for pair in range(COLS // 128):
             wide = slice(128 * pair, 128 * pair + 128)
             state = entering[:, pair * (STATE // Y) : (pair + 1) * (STATE // Y), :].reshape(STATE, 128)
             inter = jnp.dot(c_all[here, :], state, preferred_element_type=f32)
-            fade = jnp.exp(
-                jnp.where(first, cum[0, here, 2 * pair : 2 * pair + 1], cum[0, here, 2 * pair + 1 : 2 * pair + 2])
-            )
-            local = locals_[0][here, wide]
-            for g in range(1, CHUNKS):
-                local = jnp.where(step >= g * per, locals_[g][here, wide], local)
-            ssm = local + fade * inter
+            ssm = local[here, wide] + fade[here, wide] * inter
             square = ssm * ssm
             high = square.astype(bf16)
             low = (square - high.astype(f32)).astype(bf16)
@@ -294,14 +294,12 @@
         out[:, frame] = picked.reshape(2 * Y, POSITIONS // (2 * Y), COLS)
 
 
-def finish_kernel(core, locals_, c_all, entering, cum, gain, order):
+def finish_kernel(core, local, c_all, entering, fade, gain, order):
     steps = OWN // COLS
-    per = CHUNK // COLS
-    heads = COLS // HEADDIM
     piece = POSITIONS // (2 * Y)
 
-    def chunk_block(g):
-        return lambda i, core: (0, jnp.clip(i - g * per, 0, per - 1))
+    def column(i, core):
+        return (0, i)
 
     return pl.pallas_call(
         finish_body,
@@ -309,11 +307,11 @@
         grid_spec=pltpu.PrefetchScalarGridSpec(
             num_scalar_prefetch=1,
             grid=(steps,),
-            in_specs=[pl.BlockSpec((ROWS, COLS), chunk_block(g)) for g in range(CHUNKS)]
-            + [
+            in_specs=[
+                pl.BlockSpec((ROWS, COLS), column),
                 whole(c_all.shape),
                 pl.BlockSpec((Y, COLS // 128 * (STATE // Y), 128), lambda i, core: (0, i, 0)),
-                pl.BlockSpec((1, ROWS, heads), lambda i, core: (i, 0, 0)),
+                pl.BlockSpec((ROWS, COLS), column),
                 pl.BlockSpec((1, COLS), lambda i, core: (0, core[0] * steps + i)),
                 whole(order.shape),
             ],
@@ -321,7 +319,7 @@
         ),
         compiler_params=params(),
         name="finish",
-    )(core, *locals_, c_all, entering, cum, gain, order)
+    )(core, local, c_all, entering, fade, gain, order)
 
 
 def regroup_body(part, out):
@@ -400,7 +398,7 @@
     )(rows, gain, normed)
 
 
-def decay_body(core, own, other, cum_r, step_r, cum_c, step_c, whole_c, fades):
+def decay_body(core, own, other, cum_r, cum_two, cum_c, step_c, whole_c, fades):
     count = OWN // HEADDIM
     heads = COLS // HEADDIM
     mine = own[pl.ds(pl.multiple_of(core[0] * count, count), count), :]
@@ -418,47 +416,82 @@
     for j in range(BLOCKS):
         before.append(before[-1] + cum[count * j : count * j + count, GROUP - 1 : GROUP])
     since = cum + jnp.concatenate(before[:BLOCKS], axis=0)
-    turned = [a.T for a in (cum, -rows, since)]
+    step = -rows
+    log_step = jnp.where(step > 0.0, jnp.log(jnp.where(step > 0.0, step, 1.0)), -1e30)
+    two_r = (cum - log_step) * LOG2E
+    turned = [a.T for a in (cum * LOG2E, cum, step, since)]
     for i in range(OWN // COLS):
         for j in range(BLOCKS):
             at = slice(GROUP * j, GROUP * j + GROUP)
             some = slice(count * j + heads * i, count * j + heads * i + heads)
-            cum_r[i, :, at] = cum[some, :]
-            step_r[i, :, at] = -rows[some, :]
-            for out, a in zip((cum_c, step_c, whole_c), turned):
+            cum_r[i, :, at] = two_r[some, :]
+            for out, a in zip((cum_two, cum_c, step_c, whole_c), turned):
                 out[i, at, :] = a[:, some]
     fade = jnp.broadcast_to(jnp.exp(before[BLOCKS]), (count, 128))
     first = lax.broadcasted_iota(jnp.int32, (1, 128), 1) < HEADDIM
-    pairs = CHUNK // 128
-    for g in range(CHUNKS):
-        spread_out = jnp.concatenate(
-            [
-                jnp.where(first, fade[2 * p : 2 * p + 1], fade[2 * p + 1 : 2 * p + 2])
-                for p in range(g * pairs, g * pairs + pairs)
-            ],
-            axis=0,
-        )
-        high = spread_out.astype(bf16).astype(f32)
-        fill = jnp.zeros((PAD - 2 * pairs, 128), f32)
-        fades[g] = jnp.concatenate([high, spread_out - high, fill], axis=0).astype(bf16)
+    pairs = OWN // 128
+    spread_out = jnp.concatenate(
+        [jnp.where(first, fade[2 * p : 2 * p + 1], fade[2 * p + 1 : 2 * p + 2]) for p in range(pairs)],
+        axis=0,
+    )
+    high = spread_out.astype(bf16).astype(f32)
+    fades[...] = jnp.concatenate([high, spread_out - high], axis=0).astype(bf16)
 
 
 def decay_kernel(core, own, other):
     steps = OWN // COLS
     heads = COLS // HEADDIM
-    in_rows = jax.ShapeDtypeStruct((steps, heads, ROWS), f32)
     in_columns = jax.ShapeDtypeStruct((steps, ROWS, heads), f32)
     return pl.pallas_call(
         decay_body,
         out_shape=(
-            in_rows, in_rows, in_columns, in_columns, in_columns,
-            jax.ShapeDtypeStruct((CHUNKS, PAD, 128), bf16),
+            jax.ShapeDtypeStruct((steps, heads, ROWS), f32),
+            in_columns, in_columns, in_columns, in_columns,
+            jax.ShapeDtypeStruct((PAD, 128), bf16),
         ),
         in_specs=[pl.BlockSpec(memory_space=pltpu.SMEM)]
         + [pl.BlockSpec(memory_space=pltpu.VMEM) for _ in range(2)],
         compiler_params=params(),
         name="decay",
     )(core, own, other)
+
+
+def expand_body(cum_c, step_c, whole_c, e_in, e_out, e_all):
+    first = lax.broadcasted_iota(jnp.int32, (GROUP, GROUP), 1) < HEADDIM
+
+    def one(j, carry):
+        here = pl.ds(pl.multiple_of(j * GROUP, GROUP), GROUP)
+        for pair in range(COLS // 128):
+            wide = slice(128 * pair, 128 * pair + 128)
+
+            def by_lane(a):
+                columns = [
+                    jnp.broadcast_to(a[0, here, h : h + 1], (GROUP, GROUP))
+                    for h in (2 * pair, 2 * pair + 1)
+                ]
+                return jnp.where(first, columns[0], columns[1])
+
+            cum = by_lane(cum_c)
+            e_in[here, wide] = jnp.exp(cum)
+            e_out[here, wide] = jnp.exp(cum[GROUP - 1 :, :] - cum) * by_lane(step_c)
+            e_all[here, wide] = jnp.exp(by_lane(whole_c))
+        return carry
+
+    lax.fori_loop(0, BLOCKS, one, 0)
+
+
+def expand_kernel(cum_c, step_c, whole_c):
+    steps = OWN // COLS
+    heads = COLS // HEADDIM
+    return pl.pallas_call(
+        expand_body,
+        out_shape=(jax.ShapeDtypeStruct((ROWS, OWN), f32),) * 3,
+        grid=(steps,),
+        in_specs=[pl.BlockSpec((1, ROWS, heads), lambda i: (i, 0, 0))] * 3,
+        out_specs=(pl.BlockSpec((ROWS, COLS), lambda i: (0, i)),) * 3,
+        compiler_params=params(),
+        name="expand",
+    )(cum_c, step_c, whole_c)
 
 
 def on_device(
@@ -477,7 +510,8 @@
     )
     half = lax.dynamic_slice_in_dim(weight, (y % 2) * 32, 32, 0)
     far = spread(half, far_groups()).reshape(128, 2 * STATE + OWN)
-    cuts = [0] + [2 * STATE + (g + 1) * CHUNK for g in range(CHUNKS)]
+    starts = [sum(PARTS[:g]) for g in range(len(PARTS) + 1)]
+    cuts = [0] + [2 * STATE + COLS * start for start in starts[1:]]
     far_chunks = [far[:, a:b] for a, b in zip(cuts, cuts[1:])]
     chunks = [spread(far_chunks[0], near_groups())]
 
@@ -488,7 +522,10 @@
     tail = lax.ppermute(tail, "seq", onward)
     normed = norm_kernel(which, own, sibling, gain)
     other = lax.dynamic_slice_in_dim(log_decay[0], (1 - core) * head_count, head_count, 0)
-    decays = decay_kernel(which, log_decay[0], lax.ppermute(other, "seq", swap))
+    cum_r, cum_two, cum_c, step_c, whole_c, fades = decay_kernel(
+        which, log_decay[0], lax.ppermute(other, "seq", swap)
+    )
+    decays = (cum_r, cum_two, fades) + tuple(expand_kernel(cum_c, step_c, whole_c))
     bias = conv_bias[None, :]
     last_gain = out_gain[None, :]
     order = scan_order[:, None]
@@ -496,27 +533,28 @@
     normed, tail, decays, bias, last_gain, order, far_chunks = lax.optimization_barrier(
         (normed, tail, decays, bias, last_gain, order, far_chunks)
     )
-    cum_r, step_r, cum_c, step_c, whole_c, fades = decays
+    cum_r, cum_two, fades, e_in, e_out, e_all = decays
     normed = tail_kernel(tail, gain, normed)
-    chunks += [spread(a, near_groups()) for a in far_chunks[1:]]
+    chunks.append(spread(far_chunks[1], near_groups()))
 
     b_all, c_all, scores = bc_kernel(normed, chunks[0], conv_weight, bias)
     same_core = [list(range(c, 2 * Y, 2)) for c in range(2)]
-    locals_, sents = [], []
-    for g in range(CHUNKS):
-        local, sent = heads_kernel(
-            which, g, normed, chunks[g], 1 if g == 0 else 0, conv_weight, bias,
-            b_all, c_all, scores, cum_r, step_r, cum_c, step_c, skip, fades,
+    earlier = ()
+    for g, steps in enumerate(PARTS):
+        earlier = heads_kernel(
+            which, starts[g], steps, normed, chunks[g], 1 if g == 0 else 0, conv_weight, bias,
+            b_all, c_all, scores, cum_two, cum_r, e_in, e_out, skip, fades, earlier,
         )
-        locals_.append(local)
-        sents.append(sent)
-    parts = lax.all_to_all(
-        jnp.concatenate(sents, axis=1), "seq", 0, 0, axis_index_groups=same_core, tiled=True
-    )
+        if g + 2 < len(PARTS):
+            following, sent = lax.optimization_barrier((far_chunks[g + 2], earlier[1]))
+            earlier = (earlier[0], sent)
+            chunks.append(spread(following, near_groups()))
+    local, sent = earlier
+    parts = lax.all_to_all(sent, "seq", 0, 0, axis_index_groups=same_core, tiled=True)
     entering = lax.all_to_all(
         chain_kernel(parts), "seq", 0, 0, axis_index_groups=same_core, tiled=True
     )
-    outgoing = finish_kernel(which, locals_, c_all, entering, whole_c, last_gain, order)
+    outgoing = finish_kernel(which, local, c_all, entering, e_all, last_gain, order)
     back = lax.all_to_all(outgoing, "seq", 0, 0, tiled=True)
     return regroup_kernel(back.reshape(Y, 2, 2, POSITIONS // (2 * Y), OWN))[None]
 

time: 227 us -> 246 us (1.084)
  Pallas kernels: 64.7 us -> 81 us
  starting transfers between devices: 26.5 us -> 33.6 us
    pallas_call x1 -> x2, Pallas kernels: 5.57 us -> 19.3 us  [the longest x1 12.7 us: expand_kernel(): pl.pallas_call(expand_body, out_shape=(jax.ShapeDtypeStruct((ROWS, OWN),...]
    ppermute x1, waiting for transfers between devices: 8.69 us -> 0.01 us  [on_device(): tail = lax.ppermute(tail, 'seq', onward)]
    all_to_all x2 -> x3, starting transfers between devices: 12.9 us -> 20.1 us  [spread(): lax.all_to_all(jnp.broadcast_to(block[None], (count,) + block.shape), ('d...]
    all_to_all x2 -> x3, waiting for transfers between devices: 4.85 us -> 11.5 us  [spread(): lax.all_to_all(jnp.broadcast_to(block[None], (count,) + block.shape), ('d...]
    pallas_call x2 -> x3, Pallas kernels: 28.5 us -> 31.8 us  [heads_kernel(): pl.pallas_call(functools.partial(heads_body, base), out_shape=(jax.ShapeD...]
  transfers between devices with their start and end apart: 6 -> 7, of which waited for: 6 -> 5; matrix products, arithmetic and copies ran while one was open for 1% -> 1% of each run, Pallas kernels for 15% -> 23%
where the time goes in v4:
time: 246 us; the launch traced here: 245 us
  blocking collectives  95 us (39%)
  Pallas kernels  81 us (33%)
  starting transfers between devices  33.6 us (14%)
  waiting for transfers between devices  24.3 us (10%)
  local copies, waits for them, and re-layouts  10.1 us (4%)
    all_to_all x1, blocking collectives, on_device(): back = lax.all_to_all(outgoing, 'seq', 0, 0, tiled=True)  59.4 us
    pallas_call x3, Pallas kernels, heads_kernel(): pl.pallas_call(functools.partial(heads_body, base), out_shape=(jax.ShapeD...  31.8 us
    all_to_all x1, blocking collectives, spread(): lax.all_to_all(jnp.broadcast_to(block[None], (count,) + block.shape), ('d...  20.3 us
    all_to_all x3, starting transfers between devices, spread(): lax.all_to_all(jnp.broadcast_to(block[None], (count,) + block.shape), ('d...  20.1 us
    all_to_all x1, blocking collectives, on_device(): lax.all_to_all(sent, 'seq', 0, 0, axis_index_groups=same_core, tiled=True)  15.3 us
    pallas_call x1, Pallas kernels, expand_kernel(): pl.pallas_call(expand_body, out_shape=(jax.ShapeDtypeStruct((ROWS, OWN),...  12.7 us
    all_to_all x3, waiting for transfers between devices, spread(): lax.all_to_all(jnp.broadcast_to(block[None], (count,) + block.shape), ('d...  11.5 us
    pallas_call x1, Pallas kernels, finish_kernel(): pl.pallas_call(finish_body, out_shape=jax.ShapeDtypeStruct((2 * Y, 2, pie...  9.21 us
  transfers between devices with their start and end apart: 7, of which 5 were waited for; matrix products, arithmetic and copies ran while one was open for 1% of the time, Pallas kernels for 23%

profile of v4, /device:TPU:1, one launch (start us, length us, event | category | flops | bytes accessed | tf_op | source)
XLA Modules:
  0.0 245.1 jit_solution(13048204601845342001)
XLA Ops:
  0.0 0.8 slice.24
  0.8 0.9 constant_dynamic-slice_fusion
  1.7 20.3 %all_to_all.35 = bf16[4,32,1280]{2,1,0:T(8,128)(2,1)S(1)} all-to-all(bf16[4,32,1280]{2,1,0:T(8,128)(2,1)S(1)} %broadcast_in_dim.47), channel_id=1, replica_groups={{0,128,256,384},{1,129,257,385},{2,130,258,386},{3,131,259,387},{4,132,..., dimensions={0} | all-to-all | bytes 655360 | tf_op jit(solution)/shard_map/all_to_all | solution.py:53
  22.1 1.5 broadcast_in_dim.48
  23.6 0.0 copy-start.3
  23.6 0.0 copy-start.6
  23.6 8.0 %all-to-all-start.1 = ((bf16[16,128,512]{2,1,0:T(8,128)(2,1)}), bf16[16,128,512]{2,1,0:T(8,128)(2,1)S(1)}, u32[]{:S(2)}, u32[]{:S(2)}) async-start(bf16[16,128,512]{2,1,0:T(8,128)(2,1)} %broadcast_in_dim.48), calls=%async_computation.1 | async-start | bytes 4194304 | tf_op jit(solution)/shard_map/all_to_all | solution.py:53
  31.6 4.0 %collective-permute-start = (bf16[512,2048]{1,0:T(8,128)(2,1)}, bf16[512,2048]{1,0:T(8,128)(2,1)}, u32[]{:S(2)}, u32[]{:S(2)}) collective-permute-start(bf16[512,2048]{1,0:T(8,128)(2,1)} %bitcast.14), channel_id=1, source_target_pairs={{0,1},{1,0},{2,3},{3,2},{4,5},{5,4},{6,7},{7,6},{8,9},{9,8},{10,11... | collective-permute-start | bytes 6291464 | tf_op jit(solution)/shard_map/ppermute | solution.py:520
  35.7 4.1 %collective-permute-done.sibling = bf16[512,2048]{1,0:T(8,128)(2,1)} collective-permute-done((bf16[512,2048]{1,0:T(8,128)(2,1)}, bf16[512,2048]{1,0:T(8,128)(2,1)}, u32[]{:S(2)}, u32[]{:S(2)}) %collective-permute-start) | collective-permute-done | bytes 2097184 | tf_op jit(solution)/shard_map/ppermute | solution.py:520
  39.8 0.9 slice_select_fusion
  40.7 3.5 %collective-permute-start.1 = (bf16[16,2048]{1,0:T(8,128)(2,1)S(1)}, bf16[16,2048]{1,0:T(8,128)(2,1)S(1)}, u32[]{:S(2)}, u32[]{:S(2)}) collective-permute-start(bf16[16,2048]{1,0:T(8,128)(2,1)S(1)} %slice_select_fusion), channel_id=1, source_target_pairs={{0,2},{1,3},{2,4},{3,5},{4,6},{5,7},{6,8},{7,9},{8,10},{9,11},{10,... | collective-permute-start | bytes 196616 | tf_op jit(solution)/shard_map/ppermute | solution.py:522
  44.2 0.0 copy-done.3
  44.2 2.6 %collective-permute-start.2 = (f32[16,512]{1,0:T(8,128)S(1)}, f32[16,512]{1,0:T(8,128)S(1)}, u32[]{:S(2)}, u32[]{:S(2)}) collective-permute-start(f32[16,512]{1,0:T(8,128)S(1)} %dynamic-slice_bitcast_fusion), channel_id=1, source_target_pairs={{0,1},{1,0},{2,3},{3,2},{4,5},{5,4},{6,7},{7,6},{8,9},{9,8},{10,11... | collective-permute-start | bytes 98312 | tf_op jit(solution)/shard_map/ppermute | solution.py:526
  46.8 0.0 copy-done.6
  46.8 0.6 broadcast_in_dim.44.bias
  47.4 0.2 collective-permute-done.2.other
  47.6 0.0 copy-start.5
  47.6 0.6 copy-done.5
  48.2 6.6 %decay.1 = (f32[4,4,1024]{2,1,0:T(4,128)}, f32[4,1024,4]{2,1,0:T(8,128)}, f32[4,1024,4]{2,1,0:T(8,128)}, f32[4,1024,4]{2,1,0:T(8,128)}, f32[4,1024,4]{2,1,0:T(8,128)}, /*index=5*/bf16[16,128]{1,0:T(8,128)(2,1)}) custom-call(s32[1]{0:T(128)} %bitcast.core, f32[32,512]{1,0:T(8,128)} %bitcast.18, f32[16,512]{1,0:T(8,128)} %copy-done.5), custom_call_target="tpu_custom_call" | custom-call | tf_op jit(solution)/shard_map/decay/pallas_call | solution.py:445
  54.8 12.7 %expand.1 = (f32[1024,1024]{1,0:T(8,128)}, f32[1024,1024]{1,0:T(8,128)}, f32[1024,1024]{1,0:T(8,128)}) custom-call(f32[4,1024,4]{2,1,0:T(8,128)} %get-tuple-element.41.cum_c, f32[4,1024,4]{2,1,0:T(8,128)} %get-tuple-element.42.step_c, f32[4,1024,4]{2,1,0:T(8,128)} %get-tuple-element.43.whole_c), custom_call_target="tpu_custom_call" | custom-call | tf_op jit(solution)/shard_map/expand/pallas_call | solution.py:486
  67.6 6.0 %norm.1.normed = bf16[1040,2048]{1,0:T(8,128)(2,1)} custom-call(s32[1]{0:T(128)} %bitcast.core, bf16[512,2048]{1,0:T(8,128)(2,1)} %bitcast.15, bf16[512,2048]{1,0:T(8,128)(2,1)} %collective-permute-done.sibling, f32[1,2048]{1,0:T(1,128)} %bitcast.19), custom_call_target="tpu_custom_call" | custom-call | tf_op jit(solution)/shard_map/norm/pallas_call | solution.py:374
  73.6 0.0 collective-permute-done.1.rows
  73.6 0.0 all-to-all-done.1.w
  73.6 0.0 copy-start
  73.6 1.7 broadcast_in_dim.50
  75.4 0.0 copy-done.4
  75.4 0.3 copy-done
  75.6 6.1 %all-to-all-start.3 = ((bf16[16,128,512]{2,1,0:T(8,128)(2,1)}), bf16[16,128,512]{2,1,0:T(8,128)(2,1)}, u32[]{:S(2)}, u32[]{:S(2)}) async-start(bf16[16,128,512]{2,1,0:T(8,128)(2,1)} %broadcast_in_dim.50), calls=%async_computation.3 | async-start | bytes 4194304 | tf_op jit(solution)/shard_map/all_to_all | solution.py:53
  81.8 1.6 tail.1.normed
  83.4 6.7 %bc.1 = (bf16[1024,128]{1,0:T(8,128)(2,1)}, bf16[1024,128]{1,0:T(8,128)(2,1)}, f32[1024,128]{1,0:T(8,128)}) custom-call(bf16[1040,2048]{1,0:T(8,128)(2,1)} %tail.1.normed, bf16[16,128,512]{2,1,0:T(8,128)(2,1)} %copy-done, f32[4,2304]{1,0:T(4,128)} %taps.7, f32[1,2304]{1,0:T(1,128)} %broadcast_in_dim.44.bias), custom_call_target="tpu_custom_call" | custom-call | tf_op jit(solution)/shard_map/bc/pallas_call | solution.py:102
  90.1 8.9 %heads.3 = (f32[1024,1024]{1,0:T(8,128)}, bf16[8,144,128]{2,1,0:T(8,128)(2,1)}) custom-call(s32[1]{0:T(128)} %bitcast.core, bf16[1040,2048]{1,0:T(8,128)(2,1)} %tail.1.normed, bf16[16,128,512]{2,1,0:T(8,128)(2,1)} %copy-done, f32[4,2304]{1,0:T(4,128)} %taps.7, f32[1,2304]{1,0:T(1,128)} %broadcast_in_dim.44.bias, bf16[1024,128]{1,0:T(8,128)(2,1)} %get-tuple-element.51.b_all, ...), custom_call_target="tpu_custom_call" | custom-call | tf_op jit(solution)/shard_map/heads/pallas_call | solution.py:204
  99.0 9.8 %all-to-all-done.3.w = bf16[16,128,512]{2,1,0:T(8,128)(2,1)} async-done(((bf16[16,128,512]{2,1,0:T(8,128)(2,1)}), bf16[16,128,512]{2,1,0:T(8,128)(2,1)}, u32[]{:S(2)}, u32[]{:S(2)}) %all-to-all-start.3) | async-done | bytes 2097184 | tf_op jit(solution)/shard_map/all_to_all | solution.py:53
  108.8 1.1 broadcast_in_dim.49
  109.9 5.9 %all-to-all-start.2 = ((bf16[16,128,256]{2,1,0:T(8,128)(2,1)}), bf16[16,128,256]{2,1,0:T(8,128)(2,1)S(1)}, u32[]{:S(2)}, u32[]{:S(2)}) async-start(bf16[16,128,256]{2,1,0:T(8,128)(2,1)} %broadcast_in_dim.49), calls=%async_computation.2 | async-start | bytes 2097152 | tf_op jit(solution)/shard_map/all_to_all | solution.py:53
  115.8 13.9 %heads.4 = (f32[1024,1024]{1,0:T(8,128)}, bf16[8,144,128]{2,1,0:T(8,128)(2,1)}) custom-call(s32[1]{0:T(128)} %bitcast.core, bf16[1040,2048]{1,0:T(8,128)(2,1)} %tail.1.normed, bf16[16,128,512]{2,1,0:T(8,128)(2,1)} %all-to-all-done.3.w, f32[4,2304]{1,0:T(4,128)} %taps.7, ...), custom_call_target="tpu_custom_call", output_to_operand_aliasing={{0}: (14, {}), {1}: (15, {})} | custom-call | tf_op jit(solution)/shard_map/heads/pallas_call | solution.py:204
  129.7 1.7 all-to-all-done.2.w
  131.4 1.0 copy-done.1
  132.3 9.0 %heads.5 = (f32[1024,1024]{1,0:T(8,128)}, bf16[8,144,128]{2,1,0:T(8,128)(2,1)}) custom-call(s32[1]{0:T(128)} %bitcast.core, bf16[1040,2048]{1,0:T(8,128)(2,1)} %tail.1.normed, bf16[16,128,256]{2,1,0:T(8,128)(2,1)} %copy-done.1, f32[4,2304]{1,0:T(4,128)} %taps.7, f32[1,2304]{1,0:T(1,128)} %broadcast_in_dim.44.bias, ...), custom_call_target="tpu_custom_call", output_to_operand_aliasing={{0}: (14, {}), {1}: (15, {})} | custom-call | tf_op jit(solution)/shard_map/heads/pallas_call | solution.py:204
  141.3 15.3 %all_to_all.36.parts = bf16[8,144,128]{2,1,0:T(8,128)(2,1)} all-to-all(bf16[8,144,128]{2,1,0:T(8,128)(2,1)} %get-tuple-element.67), channel_id=1, replica_groups={{0,2,4,6,8,10,12,14},{1,3,5,7,9,11,13,15},{16,18,20,22,24,26,28,30},{17..., dimensions={0} | all-to-all | bytes 589824 | tf_op jit(solution)/shard_map/all_to_all | solution.py:553
  156.7 1.7 chain.1
  158.4 3.4 %all-to-all-start.5 = ((bf16[8,128,128]{2,1,0:T(8,128)(2,1)}), bf16[8,128,128]{2,1,0:T(8,128)(2,1)S(1)}, u32[]{:S(2)}, u32[]{:S(2)}) async-start(bf16[8,128,128]{2,1,0:T(8,128)(2,1)} %chain.1), calls=%async_computation.5 | async-start | bytes 524288 | tf_op jit(solution)/shard_map/all_to_all | solution.py:554
  161.8 0.0 copy-done.7
  161.8 0.9 copy.15.order
  162.7 8.5 %all-to-all-done.5.entering = bf16[8,128,128]{2,1,0:T(8,128)(2,1)S(1)} async-done(((bf16[8,128,128]{2,1,0:T(8,128)(2,1)}), bf16[8,128,128]{2,1,0:T(8,128)(2,1)S(1)}, u32[]{:S(2)}, u32[]{:S(2)}) %all-to-all-start.5) | async-done | bytes 262176 | tf_op jit(solution)/shard_map/all_to_all | solution.py:554
  171.2 0.7 copy-done.2
  171.9 9.2 %finish.1 = bf16[16,2,32,1024]{3,2,1,0:T(8,128)(2,1)} custom-call(s32[1]{0:T(128)} %bitcast.core, f32[1024,1024]{1,0:T(8,128)} %get-tuple-element.66.local, bf16[1024,128]{1,0:T(8,128)(2,1)} %get-tuple-element.52.c_all, bf16[8,128,128]{2,1,0:T(8,128)(2,1)} %copy-done.2, f32[1024,1024]{1,0:T(8,128)} %get-tuple-element.68.fade, f32[1,2048]{1,0:T(1,128)} %bitcast.21, ...), custom_call_target="tpu_custom_call" | custom-call | tf_op jit(solution)/shard_map/finish/pallas_call | solution.py:304
  181.1 59.4 %all_to_all.37 = bf16[16,2,32,1024]{3,2,1,0:T(8,128)(2,1)} all-to-all(bf16[16,2,32,1024]{3,2,1,0:T(8,128)(2,1)} %finish.1), channel_id=1, replica_groups=mesh['dp'=32,'seq'=16] {'seq'}, dimensions={0} | all-to-all | bytes 4194304 | tf_op jit(solution)/shard_map/all_to_all | solution.py:558
  240.5 4.6 %regroup.1 = bf16[512,2048]{1,0:T(8,128)(2,1)} custom-call(bf16[8,2,2,32,1024]{4,3,2,1,0:T(8,128)(2,1)} %bitcast.13), custom_call_target="tpu_custom_call" | custom-call | tf_op jit(solution)/shard_map/regroup/pallas_call | solution.py:336
  (9 shorter events, 0.1 us)
Async XLA Ops:
  23.6 20.6 %copy-start.3 = (f32[1,32,512]{2,1,0:T(8,128)S(1)}, f32[1,32,512]{2,1,0:T(8,128)}, u32[]{:S(2)}) copy-start(f32[1,32,512]{2,1,0:T(8,128)} %param.14) | copy-start | bytes 196612
  23.6 23.2 %copy-start.6 = (f32[2304]{0:T(1024)S(1)}, f32[2304]{0:T(1024)}, u32[]{:S(2)}) copy-start(f32[2304]{0:T(1024)} %param.13) | copy-start | bytes 27652
  23.6 50.0 %all-to-all-start.1 = ((bf16[16,128,512]{2,1,0:T(8,128)(2,1)}), bf16[16,128,512]{2,1,0:T(8,128)(2,1)S(1)}, u32[]{:S(2)}, u32[]{:S(2)}) async-start(bf16[16,128,512]{2,1,0:T(8,128)(2,1)} %broadcast_in_dim.48), calls=%async_computation.1 | async-start | bytes 4194304 | tf_op jit(solution)/shard_map/all_to_all | solution.py:53
  31.6 8.2 %collective-permute-start = (bf16[512,2048]{1,0:T(8,128)(2,1)}, bf16[512,2048]{1,0:T(8,128)(2,1)}, u32[]{:S(2)}, u32[]{:S(2)}) collective-permute-start(bf16[512,2048]{1,0:T(8,128)(2,1)} %bitcast.14), channel_id=1, source_target_pairs={{0,1},{1,0},{2,3},{3,2},{4,5},{5,4},{6,7},{7,6},{8,9},{9,8},{10,11... | collective-permute-start | bytes 6291464 | tf_op jit(solution)/shard_map/ppermute | solution.py:520
  40.7 32.9 %collective-permute-start.1 = (bf16[16,2048]{1,0:T(8,128)(2,1)S(1)}, bf16[16,2048]{1,0:T(8,128)(2,1)S(1)}, u32[]{:S(2)}, u32[]{:S(2)}) collective-permute-start(bf16[16,2048]{1,0:T(8,128)(2,1)S(1)} %slice_select_fusion), channel_id=1, source_target_pairs={{0,2},{1,3},{2,4},{3,5},{4,6},{5,7},{6,8},{7,9},{8,10},{9,11},{10,... | collective-permute-start | bytes 196616 | tf_op jit(solution)/shard_map/ppermute | solution.py:522
  44.2 3.4 %collective-permute-start.2 = (f32[16,512]{1,0:T(8,128)S(1)}, f32[16,512]{1,0:T(8,128)S(1)}, u32[]{:S(2)}, u32[]{:S(2)}) collective-permute-start(f32[16,512]{1,0:T(8,128)S(1)} %dynamic-slice_bitcast_fusion), channel_id=1, source_target_pairs={{0,1},{1,0},{2,3},{3,2},{4,5},{5,4},{6,7},{7,6},{8,9},{9,8},{10,11... | collective-permute-start | bytes 98312 | tf_op jit(solution)/shard_map/ppermute | solution.py:526
  47.6 0.6 copy-start.5
  73.6 1.8 copy-start.4
  73.6 2.0 copy-start
  75.6 33.2 %all-to-all-start.3 = ((bf16[16,128,512]{2,1,0:T(8,128)(2,1)}), bf16[16,128,512]{2,1,0:T(8,128)(2,1)}, u32[]{:S(2)}, u32[]{:S(2)}) async-start(bf16[16,128,512]{2,1,0:T(8,128)(2,1)} %broadcast_in_dim.50), calls=%async_computation.3 | async-start | bytes 4194304 | tf_op jit(solution)/shard_map/all_to_all | solution.py:53
  109.9 21.5 %all-to-all-start.2 = ((bf16[16,128,256]{2,1,0:T(8,128)(2,1)}), bf16[16,128,256]{2,1,0:T(8,128)(2,1)S(1)}, u32[]{:S(2)}, u32[]{:S(2)}) async-start(bf16[16,128,256]{2,1,0:T(8,128)(2,1)} %broadcast_in_dim.49), calls=%async_computation.2 | async-start | bytes 2097152 | tf_op jit(solution)/shard_map/all_to_all | solution.py:53
  131.4 1.0 copy-start.1
  132.3 29.5 %copy-start.7 = (s32[512]{0:T(512)S(1)}, s32[512]{0:T(512)}, u32[]{:S(2)}) copy-start(s32[512]{0:T(512)} %param.17) | copy-start | bytes 6148
  158.4 12.8 %all-to-all-start.5 = ((bf16[8,128,128]{2,1,0:T(8,128)(2,1)}), bf16[8,128,128]{2,1,0:T(8,128)(2,1)S(1)}, u32[]{:S(2)}, u32[]{:S(2)}) async-start(bf16[8,128,128]{2,1,0:T(8,128)(2,1)} %chain.1), calls=%async_computation.5 | async-start | bytes 524288 | tf_op jit(solution)/shard_map/all_to_all | solution.py:554
  171.2 0.7 copy-start.2

commit v5 on v4

--- a/solution.py
+++ b/solution.py
@@ -16,7 +16,7 @@
 BLOCKS = ROWS // GROUP
 OWN = 1024
 COLS = 256
-PARTS = (1, 2, 1)
+PARTS = (2, 2)
 LOG2E = 1.4426950408889634
 EPS = 1e-05
 
@@ -64,9 +64,9 @@
     return pl.BlockSpec(shape, lambda *_: (0,) * len(shape))
 
 
-def project_and_mix(normed, w, taps, bias, w_all, p_all):
+def project(normed, w, w_all, p_all):
     for k in range(4):
-        w_all[512 * k : 512 * k + 512, :] = w[:, 32 * k : 32 * k + 32, :].reshape(512, COLS)
+        w_all[512 * k : 512 * k + 512, :] = w[:, 32 * k : 32 * k + 32, :].reshape(512, w.shape[2])
     p_all[...] = (
         jnp.dot(normed[...], w_all[...], preferred_element_type=f32).astype(bf16).astype(f32)
     )
@@ -81,48 +81,49 @@
     return (half + half * jnp.tanh(half)).astype(bf16)
 
 
-def bc_body(normed, w, taps, bias, b_out, c_out, scores, w_all, p_all):
-    project_and_mix(normed, w, taps, bias, w_all, p_all)
+def bc_body(core, normed, w, taps, bias, out, w_all, p_all):
+    project(normed, w, w_all, p_all)
 
     def one(j, carry):
         start = pl.multiple_of(j * GROUP, GROUP)
-        mixed = mixed_rows(start, taps, bias, p_all)
-        b, c = mixed[:, :STATE], mixed[:, STATE:]
-        b_out[pl.ds(start, GROUP), :] = b
-        c_out[pl.ds(start, GROUP), :] = c
-        scores[pl.ds(start, GROUP), :] = lax.dot_general(
-            c, b, (((1,), (1,)), ((), ())), preferred_element_type=f32
-        )
+        out[pl.ds(start, GROUP), :] = mixed_rows(start, taps, bias, p_all)
         return carry
 
     lax.fori_loop(0, BLOCKS, one, 0)
 
 
-def bc_kernel(normed, w, taps, bias):
+def bc_kernel(core, normed, w, taps, bias):
+    last = w.shape[2] // STATE - 1
+
+    def channels(i, core):
+        return (0, 2 * OWN // STATE + core[0])
+
     return pl.pallas_call(
         bc_body,
-        out_shape=(
-            jax.ShapeDtypeStruct((ROWS, STATE), bf16),
-            jax.ShapeDtypeStruct((ROWS, STATE), bf16),
-            jax.ShapeDtypeStruct((ROWS, GROUP), f32),
+        out_shape=jax.ShapeDtypeStruct((ROWS, STATE), bf16),
+        grid_spec=pltpu.PrefetchScalarGridSpec(
+            num_scalar_prefetch=1,
+            grid=(1,),
+            in_specs=[
+                whole(normed.shape),
+                pl.BlockSpec((16, 128, STATE), lambda i, core: (0, 0, last)),
+                pl.BlockSpec((4, STATE), channels),
+                pl.BlockSpec((1, STATE), channels),
+            ],
+            out_specs=whole((ROWS, STATE)),
+            scratch_shapes=[pltpu.VMEM((2048, STATE), bf16), pltpu.VMEM((PAD + ROWS, STATE), f32)],
         ),
-        grid=(1,),
-        in_specs=[
-            whole(normed.shape),
-            pl.BlockSpec((16, 128, COLS), lambda i: (0, 0, 0)),
-            pl.BlockSpec((4, COLS), lambda i: (0, 2 * OWN // COLS)),
-            pl.BlockSpec((1, COLS), lambda i: (0, 2 * OWN // COLS)),
-        ],
-        out_specs=(whole((ROWS, STATE)), whole((ROWS, STATE)), whole((ROWS, GROUP))),
-        scratch_shapes=[pltpu.VMEM((2048, COLS), bf16), pltpu.VMEM((PAD + ROWS, COLS), f32)],
         compiler_params=params(),
         name="bc",
-    )(normed, w, taps, bias)
+    )(core, normed, w, taps, bias)
+
+
+def turned_to(columns, step):
+    return pltpu.roll(columns, lax.rem(128 - step * (COLS // HEADDIM), 128), 1)
 
 
 def heads_body(
-    base, core, normed, w, taps, bias, b_all, c_all, scores_all, cum_c, cum_r, e_in, e_out, skip, fades,
-    *refs,
+    base, core, normed, w, taps, bias, b_all, c_all, columns, cum_r, skip, fades, *refs,
 ):
     local, sent, w_all, p_all, state = refs[-5:]
     i = pl.program_id(0)
@@ -135,7 +136,7 @@
             for y in range(Y):
                 sent[y, sent.shape[1] - PAD :, :] = fades[...]
 
-    project_and_mix(normed, w, taps, bias, w_all, p_all)
+    project(normed, w, w_all, p_all)
     state[...] = jnp.zeros_like(state)
     heads = COLS // HEADDIM
     pairs = COLS // 128
@@ -151,13 +152,19 @@
         mixed = mixed_rows(start, taps, bias, p_all)
         b = b_all[here, :]
         c = c_all[here, :]
-        scores = scores_all[here, :]
+        scores = lax.dot_general(c, b, (((1,), (1,)), ((), ())), preferred_element_type=f32)
+        cols = turned_to(columns[here, :], base + i)
+
+        def by_row(h):
+            return jnp.broadcast_to(cols[:, h : h + 1], (GROUP, GROUP))
+
         for pair in range(pairs):
             wide = slice(128 * pair, 128 * pair + 128)
             x = mixed[:, wide].astype(f32)
-            weights = []
+            weights, cums = [], []
             for h in (2 * pair, 2 * pair + 1):
-                cum = jnp.broadcast_to(cum_c[0, here, h : h + 1], (GROUP, GROUP))
+                cum = by_row(h)
+                cums.append(cum)
                 gap = cum - cum_r[0, h : h + 1, here]
                 weights.append((scores * jnp.exp2(jnp.where(causal, gap, -1e30))).astype(bf16))
             both = jnp.concatenate(weights, axis=1)
@@ -165,15 +172,17 @@
                 [jnp.where(first, x, 0.0).astype(bf16), jnp.where(first, 0.0, x).astype(bf16)], axis=0
             )
             intra = jnp.dot(both, apart, preferred_element_type=f32)
-            scaled = (e_out[here, wide] * x).astype(bf16)
+            cum = jnp.where(first, cums[0], cums[1])
+            rest = jnp.where(first, by_row(16 + 2 * pair), by_row(17 + 2 * pair))
+            scaled = (jnp.exp2(cum[GROUP - 1 :, :] - rest) * x).astype(bf16)
             block_state = lax.dot_general(
                 b, scaled, (((0,), (0,)), ((), ())), preferred_element_type=f32
             )
             entering = state[pair]
-            fade = e_in[here, wide]
+            fade = jnp.exp2(cum)
             inter = fade * jnp.dot(c, entering.astype(bf16), preferred_element_type=f32)
             gains = jnp.where(first, skip[head + 2 * pair], skip[head + 2 * pair + 1])
-            local[here, wide] = intra + inter + gains * x
+            local[here, wide] = (intra + inter + gains * x).astype(bf16)
             state[pair] = fade[GROUP - 1 :, :] * entering + block_state
         return carry
 
@@ -186,8 +195,7 @@
 
 
 def heads_kernel(
-    core, base, steps, normed, w, first_step, taps, bias, b_all, c_all, scores, cum_c, cum_r, e_in, e_out,
-    skip, fades, earlier,
+    core, base, steps, normed, w, taps, bias, bc, columns, cum_r, skip, fades, earlier,
 ):
     heads = COLS // HEADDIM
     sent = (Y, OWN // 128 * (STATE // Y) + PAD, 128)
@@ -198,13 +206,10 @@
     def step(i, core):
         return (base + i, 0, 0)
 
-    def column(i, core):
-        return (0, base + i)
-
     return pl.pallas_call(
         functools.partial(heads_body, base),
         out_shape=(
-            jax.ShapeDtypeStruct((ROWS, OWN), f32),
+            jax.ShapeDtypeStruct((ROWS, OWN), bf16),
             jax.ShapeDtypeStruct(sent, bf16),
         ),
         grid_spec=pltpu.PrefetchScalarGridSpec(
@@ -212,22 +217,19 @@
             grid=(steps,),
             in_specs=[
                 whole(normed.shape),
-                pl.BlockSpec((16, 128, COLS), lambda i, core: (0, 0, i + first_step)),
+                pl.BlockSpec((16, 128, COLS), lambda i, core: (0, 0, i)),
                 pl.BlockSpec((4, COLS), channels),
                 pl.BlockSpec((1, COLS), channels),
-                whole(b_all.shape),
-                whole(c_all.shape),
-                whole(scores.shape),
-                pl.BlockSpec((1, ROWS, heads), step),
+                pl.BlockSpec((None, ROWS, STATE), lambda i, core: (core[0], 0, 0)),
+                pl.BlockSpec((None, ROWS, STATE), lambda i, core: (1 - core[0], 0, 0)),
+                whole(columns.shape),
                 pl.BlockSpec((1, heads, ROWS), step),
-                pl.BlockSpec((ROWS, COLS), column),
-                pl.BlockSpec((ROWS, COLS), column),
                 pl.BlockSpec(memory_space=pltpu.SMEM),
                 whole(fades.shape),
             ]
             + ([pl.BlockSpec(memory_space=pl.ANY), whole(sent)] if earlier else []),
             out_specs=(
-                pl.BlockSpec((ROWS, COLS), column),
+                pl.BlockSpec((ROWS, COLS), lambda i, core: (0, base + i)),
                 whole(sent),
             ),
             scratch_shapes=[
@@ -236,12 +238,11 @@
                 pltpu.VMEM((COLS // 128, STATE, 128), f32),
             ],
         ),
-        input_output_aliases={14: 0, 15: 1} if earlier else {},
+        input_output_aliases={11: 0, 12: 1} if earlier else {},
         compiler_params=params(),
         name="heads",
     )(
-        core, normed, w, taps, bias, b_all, c_all, scores, cum_c, cum_r, e_in, e_out, skip, fades,
-        *earlier,
+        core, normed, w, taps, bias, bc, bc, columns, cum_r, skip, fades, *earlier,
     )
 
 
@@ -268,20 +269,24 @@
     )(parts)
 
 
-def finish_body(core, local, c_all, entering, fade, gain, order, out):
+def finish_body(core, local, c_all, entering, columns, gain, order, out):
     lane = lax.broadcasted_iota(jnp.int32, (GROUP, GROUP), 1)
     row = lax.broadcasted_iota(jnp.int32, (GROUP, GROUP), 0)
     same_head = jnp.where((lane < HEADDIM) == (row < HEADDIM), 1.0 / HEADDIM, 0.0).astype(bf16)
     position = lax.broadcasted_iota(jnp.int32, (POSITIONS, POSITIONS), 1)
     pick = jnp.where(position == order[...], 1.0, 0.0).astype(bf16)
+    first = lax.broadcasted_iota(jnp.int32, (1, 128), 1) < HEADDIM
     for frame in range(ROWS // POSITIONS):
         here = slice(frame * POSITIONS, (frame + 1) * POSITIONS)
         parts = []
+        cols = jnp.exp2(turned_to(columns[here, :], pl.program_id(0)))
         for pair in range(COLS // 128):
             wide = slice(128 * pair, 128 * pair + 128)
             state = entering[:, pair * (STATE // Y) : (pair + 1) * (STATE // Y), :].reshape(STATE, 128)
             inter = jnp.dot(c_all[here, :], state, preferred_element_type=f32)
-            ssm = local[here, wide] + fade[here, wide] * inter
+            h = 32 + 2 * pair
+            fade = jnp.where(first, cols[:, h : h + 1], cols[:, h + 1 : h + 2])
+            ssm = local[here, wide].astype(f32) + fade * inter
             square = ssm * ssm
             high = square.astype(bf16)
             low = (square - high.astype(f32)).astype(bf16)
@@ -294,7 +299,7 @@
         out[:, frame] = picked.reshape(2 * Y, POSITIONS // (2 * Y), COLS)
 
 
-def finish_kernel(core, local, c_all, entering, fade, gain, order):
+def finish_kernel(core, local, bc, entering, columns, gain, order):
     steps = OWN // COLS
     piece = POSITIONS // (2 * Y)
 
@@ -309,9 +314,9 @@
             grid=(steps,),
             in_specs=[
                 pl.BlockSpec((ROWS, COLS), column),
-                whole(c_all.shape),
+                pl.BlockSpec((None, ROWS, STATE), lambda i, core: (1 - core[0], 0, 0)),
                 pl.BlockSpec((Y, COLS // 128 * (STATE // Y), 128), lambda i, core: (0, i, 0)),
-                pl.BlockSpec((ROWS, COLS), column),
+                whole(columns.shape),
                 pl.BlockSpec((1, COLS), lambda i, core: (0, core[0] * steps + i)),
                 whole(order.shape),
             ],
@@ -319,7 +324,7 @@
         ),
         compiler_params=params(),
         name="finish",
-    )(core, local, c_all, entering, fade, gain, order)
+    )(core, local, bc, entering, columns, gain, order)
 
 
 def regroup_body(part, out):
@@ -398,7 +403,7 @@
     )(rows, gain, normed)
 
 
-def decay_body(core, own, other, cum_r, cum_two, cum_c, step_c, whole_c, fades):
+def decay_body(core, own, other, cum_r, columns, fades):
     count = OWN // HEADDIM
     heads = COLS // HEADDIM
     mine = own[pl.ds(pl.multiple_of(core[0] * count, count), count), :]
@@ -419,14 +424,18 @@
     step = -rows
     log_step = jnp.where(step > 0.0, jnp.log(jnp.where(step > 0.0, step, 1.0)), -1e30)
     two_r = (cum - log_step) * LOG2E
-    turned = [a.T for a in (cum * LOG2E, cum, step, since)]
+    turned = [a.T for a in (cum * LOG2E, two_r, since * LOG2E)]
+    fill = jnp.zeros((GROUP, 128 - 3 * count), f32)
+    for j in range(BLOCKS):
+        some = slice(count * j, count * j + count)
+        columns[GROUP * j : GROUP * j + GROUP, :] = jnp.concatenate(
+            [a[:, some] for a in turned] + [fill], axis=1
+        )
     for i in range(OWN // COLS):
         for j in range(BLOCKS):
             at = slice(GROUP * j, GROUP * j + GROUP)
             some = slice(count * j + heads * i, count * j + heads * i + heads)
             cum_r[i, :, at] = two_r[some, :]
-            for out, a in zip((cum_two, cum_c, step_c, whole_c), turned):
-                out[i, at, :] = a[:, some]
     fade = jnp.broadcast_to(jnp.exp(before[BLOCKS]), (count, 128))
     first = lax.broadcasted_iota(jnp.int32, (1, 128), 1) < HEADDIM
     pairs = OWN // 128
@@ -441,12 +450,11 @@
 def decay_kernel(core, own, other):
     steps = OWN // COLS
     heads = COLS // HEADDIM
-    in_columns = jax.ShapeDtypeStruct((steps, ROWS, heads), f32)
     return pl.pallas_call(
         decay_body,
         out_shape=(
             jax.ShapeDtypeStruct((steps, heads, ROWS), f32),
-            in_columns, in_columns, in_columns, in_columns,
+            jax.ShapeDtypeStruct((ROWS, 128), f32),
             jax.ShapeDtypeStruct((PAD, 128), bf16),
         ),
         in_specs=[pl.BlockSpec(memory_space=pltpu.SMEM)]
@@ -454,44 +462,6 @@
         compiler_params=params(),
         name="decay",
     )(core, own, other)
-
-
-def expand_body(cum_c, step_c, whole_c, e_in, e_out, e_all):
-    first = lax.broadcasted_iota(jnp.int32, (GROUP, GROUP), 1) < HEADDIM
-
-    def one(j, carry):
-        here = pl.ds(pl.multiple_of(j * GROUP, GROUP), GROUP)
-        for pair in range(COLS // 128):
-            wide = slice(128 * pair, 128 * pair + 128)
-
-            def by_lane(a):
-                columns = [
-                    jnp.broadcast_to(a[0, here, h : h + 1], (GROUP, GROUP))
-                    for h in (2 * pair, 2 * pair + 1)
-                ]
-                return jnp.where(first, columns[0], columns[1])
-
-            cum = by_lane(cum_c)
-            e_in[here, wide] = jnp.exp(cum)
-            e_out[here, wide] = jnp.exp(cum[GROUP - 1 :, :] - cum) * by_lane(step_c)
-            e_all[here, wide] = jnp.exp(by_lane(whole_c))
-        return carry
-
-    lax.fori_loop(0, BLOCKS, one, 0)
-
-
-def expand_kernel(cum_c, step_c, whole_c):
-    steps = OWN // COLS
-    heads = COLS // HEADDIM
-    return pl.pallas_call(
-        expand_body,
-        out_shape=(jax.ShapeDtypeStruct((ROWS, OWN), f32),) * 3,
-        grid=(steps,),
-        in_specs=[pl.BlockSpec((1, ROWS, heads), lambda i: (i, 0, 0))] * 3,
-        out_specs=(pl.BlockSpec((ROWS, COLS), lambda i: (0, i)),) * 3,
-        compiler_params=params(),
-        name="expand",
-    )(cum_c, step_c, whole_c)
 
 
 def on_device(
@@ -505,13 +475,23 @@
     head_count = OWN // HEADDIM
     which = core.astype(jnp.int32)[None]
 
+    first_half = sum(PARTS[:1]) * COLS
+
+    def weight_columns(start, count):
+        return lax.dynamic_slice_in_dim(in_weight, start, count, 1)
+
     weight = jnp.concatenate(
-        [in_weight[:, 2 * OWN :], lax.dynamic_slice_in_dim(in_weight, core * OWN, OWN, 1)], axis=1
+        [
+            weight_columns(core * OWN, first_half),
+            weight_columns(2 * OWN + core * STATE, STATE),
+            weight_columns(core * OWN + first_half, OWN - first_half),
+        ],
+        axis=1,
     )
     half = lax.dynamic_slice_in_dim(weight, (y % 2) * 32, 32, 0)
-    far = spread(half, far_groups()).reshape(128, 2 * STATE + OWN)
+    far = spread(half, far_groups()).reshape(128, STATE + OWN)
     starts = [sum(PARTS[:g]) for g in range(len(PARTS) + 1)]
-    cuts = [0] + [2 * STATE + COLS * start for start in starts[1:]]
+    cuts = [0] + [STATE + COLS * start for start in starts[1:]]
     far_chunks = [far[:, a:b] for a, b in zip(cuts, cuts[1:])]
     chunks = [spread(far_chunks[0], near_groups())]
 
@@ -522,10 +502,7 @@
     tail = lax.ppermute(tail, "seq", onward)
     normed = norm_kernel(which, own, sibling, gain)
     other = lax.dynamic_slice_in_dim(log_decay[0], (1 - core) * head_count, head_count, 0)
-    cum_r, cum_two, cum_c, step_c, whole_c, fades = decay_kernel(
-        which, log_decay[0], lax.ppermute(other, "seq", swap)
-    )
-    decays = (cum_r, cum_two, fades) + tuple(expand_kernel(cum_c, step_c, whole_c))
+    decays = decay_kernel(which, log_decay[0], lax.ppermute(other, "seq", swap))
     bias = conv_bias[None, :]
     last_gain = out_gain[None, :]
     order = scan_order[:, None]
@@ -533,17 +510,18 @@
     normed, tail, decays, bias, last_gain, order, far_chunks = lax.optimization_barrier(
         (normed, tail, decays, bias, last_gain, order, far_chunks)
     )
-    cum_r, cum_two, fades, e_in, e_out, e_all = decays
+    cum_r, columns, fades = decays
     normed = tail_kernel(tail, gain, normed)
     chunks.append(spread(far_chunks[1], near_groups()))
 
-    b_all, c_all, scores = bc_kernel(normed, chunks[0], conv_weight, bias)
+    mine = bc_kernel(which, normed, chunks[0], conv_weight, bias)
+    bc = jnp.stack([mine, lax.ppermute(mine, "seq", swap)])
     same_core = [list(range(c, 2 * Y, 2)) for c in range(2)]
     earlier = ()
     for g, steps in enumerate(PARTS):
         earlier = heads_kernel(
-            which, starts[g], steps, normed, chunks[g], 1 if g == 0 else 0, conv_weight, bias,
-            b_all, c_all, scores, cum_two, cum_r, e_in, e_out, skip, fades, earlier,
+            which, starts[g], steps, normed, chunks[g], conv_weight, bias, bc, columns, cum_r, skip,
+            fades, earlier,
         )
         if g + 2 < len(PARTS):
             following, sent = lax.optimization_barrier((far_chunks[g + 2], earlier[1]))
@@ -554,7 +532,7 @@
     entering = lax.all_to_all(
         chain_kernel(parts), "seq", 0, 0, axis_index_groups=same_core, tiled=True
     )
-    outgoing = finish_kernel(which, local, c_all, entering, e_all, last_gain, order)
+    outgoing = finish_kernel(which, local, bc, entering, columns, last_gain, order)
     back = lax.all_to_all(outgoing, "seq", 0, 0, tiled=True)
     return regroup_kernel(back.reshape(Y, 2, 2, POSITIONS // (2 * Y), OWN))[None]
 

time: 246 us -> 222 us (0.902)
  Pallas kernels: 81 us -> 59.8 us
    pallas_call x2 -> x1, Pallas kernels: 19.5 us -> 4.72 us  [bc_kernel(): pl.pallas_call(bc_body, out_shape=jax.ShapeDtypeStruct((ROWS, STATE), bf1...]
    all_to_all x3 -> x2, waiting for transfers between devices: 11.5 us -> 1.88 us  [spread(): lax.all_to_all(jnp.broadcast_to(block[None], (count,) + block.shape), ('d...]
    all_to_all x3 -> x2, starting transfers between devices: 20.1 us -> 12.9 us  [spread(): lax.all_to_all(jnp.broadcast_to(block[None], (count,) + block.shape), ('d...]
    ppermute x1 -> x2, starting transfers between devices: 2.56 us -> 7.78 us  [the longest x1 5.22 us: on_device(): bc = jnp.stack([mine, lax.ppermute(mine, 'seq', swap)])]
    ppermute x1, waiting for transfers between devices: 0.01 us -> 5.07 us  [on_device(): tail = lax.ppermute(tail, 'seq', onward)]
    pallas_call x1, Pallas kernels: 6.58 us -> 2.44 us  [decay_kernel(): pl.pallas_call(decay_body, out_shape=(jax.ShapeDtypeStruct((steps, heads,...]
    all_to_all x1, blocking collectives: 15.3 us -> 18.6 us  [on_device(): lax.all_to_all(sent, 'seq', 0, 0, axis_index_groups=same_core, tiled=True)]
    pallas_call x3 -> x2, Pallas kernels: 31.8 us -> 29.1 us  [heads_kernel(): pl.pallas_call(functools.partial(heads_body, base), out_shape=(jax.ShapeD...]
  transfers between devices with their start and end apart: 7 -> 7, of which waited for: 5 -> 6; matrix products, arithmetic and copies ran while one was open for 1% -> 2% of each run, Pallas kernels for 23% -> 13%
where the time goes in v5:
time: 222 us; the launch traced here: 221 us
  blocking collectives  96.6 us (44%)
  Pallas kernels  59.8 us (27%)
  starting transfers between devices  31.8 us (14%)
  waiting for transfers between devices  21.9 us (10%)
  local copies, waits for them, and re-layouts  8.41 us (4%)
  other arithmetic  2.69 us (1%)
    all_to_all x1, blocking collectives, on_device(): back = lax.all_to_all(outgoing, 'seq', 0, 0, tiled=True)  57.9 us
    pallas_call x2, Pallas kernels, heads_kernel(): pl.pallas_call(functools.partial(heads_body, base), out_shape=(jax.ShapeD...  29.1 us
    all_to_all x1, blocking collectives, spread(): lax.all_to_all(jnp.broadcast_to(block[None], (count,) + block.shape), ('d...  20.1 us
    all_to_all x1, blocking collectives, on_device(): lax.all_to_all(sent, 'seq', 0, 0, axis_index_groups=same_core, tiled=True)  18.6 us
    all_to_all x2, starting transfers between devices, spread(): lax.all_to_all(jnp.broadcast_to(block[None], (count,) + block.shape), ('d...  12.9 us
    pallas_call x1, Pallas kernels, finish_kernel(): pl.pallas_call(finish_body, out_shape=jax.ShapeDtypeStruct((2 * Y, 2, pie...  9.65 us
    all_to_all x1, waiting for transfers between devices, on_device(): lax.all_to_all(chain_kernel(parts), 'seq', 0, 0, axis_index_groups=same_c...  9.25 us
    pallas_call x1, Pallas kernels, norm_kernel(): pl.pallas_call(norm_body, out_shape=jax.ShapeDtypeStruct((PAD + ROWS, wid...  6 us
  transfers between devices with their start and end apart: 7, of which 6 were waited for; matrix products, arithmetic and copies ran while one was open for 2% of the time, Pallas kernels for 13%

profile of v5, /device:TPU:1, one launch (start us, length us, event | category | flops | bytes accessed | tf_op | source)
XLA Modules:
  0.0 221.3 jit_solution(6125355903890099884)
XLA Ops:
  0.0 0.7 constant_dynamic-slice_fusion.1
  0.7 0.9 constant_dynamic-slice_fusion
  1.7 20.1 %all_to_all.30 = bf16[4,32,1152]{2,1,0:T(8,128)(2,1)S(1)} all-to-all(bf16[4,32,1152]{2,1,0:T(8,128)(2,1)S(1)} %broadcast_in_dim.41), channel_id=1, replica_groups={{0,128,256,384},{1,129,257,385},{2,130,258,386},{3,131,259,387},{4,132,..., dimensions={0} | all-to-all | bytes 589824 | tf_op jit(solution)/shard_map/all_to_all | solution.py:53
  21.7 1.8 broadcast_in_dim.43
  23.6 0.0 copy-start.2
  23.6 0.0 copy-start.5
  23.6 7.6 %all-to-all-start.2 = ((bf16[16,128,640]{2,1,0:T(8,128)(2,1)}), bf16[16,128,640]{2,1,0:T(8,128)(2,1)S(1)}, u32[]{:S(2)}, u32[]{:S(2)}) async-start(bf16[16,128,640]{2,1,0:T(8,128)(2,1)} %broadcast_in_dim.43), calls=%async_computation.2 | async-start | bytes 5242880 | tf_op jit(solution)/shard_map/all_to_all | solution.py:53
  31.1 4.1 %collective-permute-start = (bf16[512,2048]{1,0:T(8,128)(2,1)}, bf16[512,2048]{1,0:T(8,128)(2,1)}, u32[]{:S(2)}, u32[]{:S(2)}) collective-permute-start(bf16[512,2048]{1,0:T(8,128)(2,1)} %bitcast.16), channel_id=1, source_target_pairs={{0,1},{1,0},{2,3},{3,2},{4,5},{5,4},{6,7},{7,6},{8,9},{9,8},{10,11... | collective-permute-start | bytes 6291464 | tf_op jit(solution)/shard_map/ppermute | solution.py:500
  35.3 4.1 %collective-permute-done.sibling = bf16[512,2048]{1,0:T(8,128)(2,1)} collective-permute-done((bf16[512,2048]{1,0:T(8,128)(2,1)}, bf16[512,2048]{1,0:T(8,128)(2,1)}, u32[]{:S(2)}, u32[]{:S(2)}) %collective-permute-start) | collective-permute-done | bytes 2097184 | tf_op jit(solution)/shard_map/ppermute | solution.py:500
  39.4 0.9 slice_select_fusion
  40.3 3.5 %collective-permute-start.1 = (bf16[16,2048]{1,0:T(8,128)(2,1)S(1)}, bf16[16,2048]{1,0:T(8,128)(2,1)S(1)}, u32[]{:S(2)}, u32[]{:S(2)}) collective-permute-start(bf16[16,2048]{1,0:T(8,128)(2,1)S(1)} %slice_select_fusion), channel_id=1, source_target_pairs={{0,2},{1,3},{2,4},{3,5},{4,6},{5,7},{6,8},{7,9},{8,10},{9,11},{10,... | collective-permute-start | bytes 196616 | tf_op jit(solution)/shard_map/ppermute | solution.py:502
  43.8 0.0 copy-done.2
  43.8 2.6 %collective-permute-start.2 = (f32[16,512]{1,0:T(8,128)S(1)}, f32[16,512]{1,0:T(8,128)S(1)}, u32[]{:S(2)}, u32[]{:S(2)}) collective-permute-start(f32[16,512]{1,0:T(8,128)S(1)} %dynamic-slice_bitcast_fusion), channel_id=1, source_target_pairs={{0,1},{1,0},{2,3},{3,2},{4,5},{5,4},{6,7},{7,6},{8,9},{9,8},{10,11... | collective-permute-start | bytes 98312 | tf_op jit(solution)/shard_map/ppermute | solution.py:505
  46.4 0.0 copy-done.5
  46.4 0.6 broadcast_in_dim.38.bias
  47.0 0.2 collective-permute-done.2.other
  47.3 0.0 copy-start.4
  47.3 0.6 copy-done.4
  47.9 2.4 %decay.1 = (f32[4,4,1024]{2,1,0:T(4,128)}, f32[1024,128]{1,0:T(8,128)}, bf16[16,128]{1,0:T(8,128)(2,1)}) custom-call(s32[1]{0:T(128)} %bitcast.core, f32[32,512]{1,0:T(8,128)} %bitcast.22, f32[16,512]{1,0:T(8,128)} %copy-done.4), custom_call_target="tpu_custom_call" | custom-call | tf_op jit(solution)/shard_map/decay/pallas_call | solution.py:453
  50.3 6.0 %norm.1.normed = bf16[1040,2048]{1,0:T(8,128)(2,1)} custom-call(s32[1]{0:T(128)} %bitcast.core, bf16[512,2048]{1,0:T(8,128)(2,1)} %bitcast.17, bf16[512,2048]{1,0:T(8,128)(2,1)} %collective-permute-done.sibling, f32[1,2048]{1,0:T(1,128)} %bitcast.23), custom_call_target="tpu_custom_call" | custom-call | tf_op jit(solution)/shard_map/norm/pallas_call | solution.py:379
  56.3 5.1 %collective-permute-done.1.rows = bf16[16,2048]{1,0:T(8,128)(2,1)S(1)} collective-permute-done((bf16[16,2048]{1,0:T(8,128)(2,1)S(1)}, bf16[16,2048]{1,0:T(8,128)(2,1)S(1)}, u32[]{:S(2)}, u32[]{:S(2)}) %collective-permute-start.1) | collective-permute-done | bytes 65568 | tf_op jit(solution)/shard_map/ppermute | solution.py:502
  61.4 0.0 copy-start.3
  61.4 1.9 all-to-all-done.2.w
  63.3 0.0 copy-start
  63.3 1.7 broadcast_in_dim.42
  64.9 0.0 copy-done.3
  64.9 0.5 copy-done
  65.4 5.3 %all-to-all-start.1 = ((bf16[16,128,512]{2,1,0:T(8,128)(2,1)}), bf16[16,128,512]{2,1,0:T(8,128)(2,1)}, u32[]{:S(2)}, u32[]{:S(2)}) async-start(bf16[16,128,512]{2,1,0:T(8,128)(2,1)} %broadcast_in_dim.42), calls=%async_computation.1 | async-start | bytes 4194304 | tf_op jit(solution)/shard_map/all_to_all | solution.py:53
  70.8 1.6 tail.1.normed
  72.3 4.7 %bc.1 = bf16[1024,128]{1,0:T(8,128)(2,1)} custom-call(s32[1]{0:T(128)} %bitcast.core, bf16[1040,2048]{1,0:T(8,128)(2,1)} %tail.1.normed, bf16[16,128,640]{2,1,0:T(8,128)(2,1)} %copy-done, f32[4,2304]{1,0:T(4,128)} %taps.5, f32[1,2304]{1,0:T(1,128)} %broadcast_in_dim.38.bias), custom_call_target="tpu_custom_call" | custom-call | tf_op jit(solution)/shard_map/bc/pallas_call | solution.py:101
  77.1 5.2 %collective-permute-start.3 = (bf16[1024,128]{1,0:T(8,128)(2,1)}, bf16[1024,128]{1,0:T(8,128)(2,1)S(1)}, u32[]{:S(2)}, u32[]{:S(2)}) collective-permute-start(bf16[1024,128]{1,0:T(8,128)(2,1)} %bc.1), channel_id=1, source_target_pairs={{0,1},{1,0},{2,3},{3,2},{4,5},{5,4},{6,7},{7,6},{8,9},{9,8},{10,11... | collective-permute-start | bytes 786440 | tf_op jit(solution)/shard_map/ppermute | solution.py:518
  82.3 1.4 collective-permute-done.3
  83.6 1.8 pad_maximum_fusion.b_all.c_all
  85.4 14.5 %heads.2 = (bf16[1024,1024]{1,0:T(8,128)(2,1)}, bf16[8,144,128]{2,1,0:T(8,128)(2,1)}) custom-call(s32[1]{0:T(128)} %bitcast.core, bf16[1040,2048]{1,0:T(8,128)(2,1)} %tail.1.normed, bf16[16,128,640]{2,1,0:T(8,128)(2,1)} %copy-done, f32[4,2304]{1,0:T(4,128)} %taps.5, f32[1,2304]{1,0:T(1,128)} %broadcast_in_dim.38.bias, ...), custom_call_target="tpu_custom_call" | custom-call | tf_op jit(solution)/shard_map/heads/pallas_call | solution.py:209
  100.0 0.0 all-to-all-done.1.w
  100.0 0.0 copy-start.6
  100.0 14.6 %heads.3 = (bf16[1024,1024]{1,0:T(8,128)(2,1)}, bf16[8,144,128]{2,1,0:T(8,128)(2,1)}) custom-call(s32[1]{0:T(128)} %bitcast.core, bf16[1040,2048]{1,0:T(8,128)(2,1)} %tail.1.normed, bf16[16,128,512]{2,1,0:T(8,128)(2,1)} %all-to-all-done.1.w, f32[4,2304]{1,0:T(4,128)} %taps.5, ...), custom_call_target="tpu_custom_call", output_to_operand_aliasing={{0}: (11, {}), {1}: (12, {})} | custom-call | tf_op jit(solution)/shard_map/heads/pallas_call | solution.py:209
  114.6 18.6 %all_to_all.31.parts = bf16[8,144,128]{2,1,0:T(8,128)(2,1)} all-to-all(bf16[8,144,128]{2,1,0:T(8,128)(2,1)} %get-tuple-element.34), channel_id=1, replica_groups={{0,2,4,6,8,10,12,14},{1,3,5,7,9,11,13,15},{16,18,20,22,24,26,28,30},{17..., dimensions={0} | all-to-all | bytes 589824 | tf_op jit(solution)/shard_map/all_to_all | solution.py:531
  133.2 1.7 chain.1
  134.9 3.4 %all-to-all-start.4 = ((bf16[8,128,128]{2,1,0:T(8,128)(2,1)}), bf16[8,128,128]{2,1,0:T(8,128)(2,1)S(1)}, u32[]{:S(2)}, u32[]{:S(2)}) async-start(bf16[8,128,128]{2,1,0:T(8,128)(2,1)} %chain.1), calls=%async_computation.4 | async-start | bytes 524288 | tf_op jit(solution)/shard_map/all_to_all | solution.py:532
  138.3 0.0 copy-done.6
  138.4 0.9 copy.13.order
  139.2 9.2 %all-to-all-done.4.entering = bf16[8,128,128]{2,1,0:T(8,128)(2,1)S(1)} async-done(((bf16[8,128,128]{2,1,0:T(8,128)(2,1)}), bf16[8,128,128]{2,1,0:T(8,128)(2,1)S(1)}, u32[]{:S(2)}, u32[]{:S(2)}) %all-to-all-start.4) | async-done | bytes 262176 | tf_op jit(solution)/shard_map/all_to_all | solution.py:532
  148.5 0.0 copy-start.1
  148.5 0.7 copy-done.1
  149.2 9.7 %finish.1 = bf16[16,2,32,1024]{3,2,1,0:T(8,128)(2,1)} custom-call(s32[1]{0:T(128)} %bitcast.core, bf16[1024,1024]{1,0:T(8,128)(2,1)} %get-tuple-element.33.local, bf16[2,1024,128]{2,1,0:T(8,128)(2,1)} %pad_maximum_fusion.b_all.c_all, bf16[8,128,128]{2,1,0:T(8,128)(2,1)} %copy-done.1, f32[1024,128]{1,0:T(8,128)} %get-tuple-element.28.columns, ...), custom_call_target="tpu_custom_call" | custom-call | tf_op jit(solution)/shard_map/finish/pallas_call | solution.py:309
  158.8 57.9 %all_to_all.32 = bf16[16,2,32,1024]{3,2,1,0:T(8,128)(2,1)} all-to-all(bf16[16,2,32,1024]{3,2,1,0:T(8,128)(2,1)} %finish.1), channel_id=1, replica_groups=mesh['dp'=32,'seq'=16] {'seq'}, dimensions={0} | all-to-all | bytes 4194304 | tf_op jit(solution)/shard_map/all_to_all | solution.py:536
  216.7 4.6 %regroup.1 = bf16[512,2048]{1,0:T(8,128)(2,1)} custom-call(bf16[8,2,2,32,1024]{4,3,2,1,0:T(8,128)(2,1)} %bitcast.15), custom_call_target="tpu_custom_call" | custom-call | tf_op jit(solution)/shard_map/regroup/pallas_call | solution.py:341
  (5 shorter events, 0.1 us)
Async XLA Ops:
  23.6 20.2 %copy-start.2 = (f32[1,32,512]{2,1,0:T(8,128)S(1)}, f32[1,32,512]{2,1,0:T(8,128)}, u32[]{:S(2)}) copy-start(f32[1,32,512]{2,1,0:T(8,128)} %param.14) | copy-start | bytes 196612
  23.6 22.8 %copy-start.5 = (f32[2304]{0:T(1024)S(1)}, f32[2304]{0:T(1024)}, u32[]{:S(2)}) copy-start(f32[2304]{0:T(1024)} %param.13) | copy-start | bytes 27652
  23.6 39.7 %all-to-all-start.2 = ((bf16[16,128,640]{2,1,0:T(8,128)(2,1)}), bf16[16,128,640]{2,1,0:T(8,128)(2,1)S(1)}, u32[]{:S(2)}, u32[]{:S(2)}) async-start(bf16[16,128,640]{2,1,0:T(8,128)(2,1)} %broadcast_in_dim.43), calls=%async_computation.2 | async-start | bytes 5242880 | tf_op jit(solution)/shard_map/all_to_all | solution.py:53
  31.1 8.2 %collective-permute-start = (bf16[512,2048]{1,0:T(8,128)(2,1)}, bf16[512,2048]{1,0:T(8,128)(2,1)}, u32[]{:S(2)}, u32[]{:S(2)}) collective-permute-start(bf16[512,2048]{1,0:T(8,128)(2,1)} %bitcast.16), channel_id=1, source_target_pairs={{0,1},{1,0},{2,3},{3,2},{4,5},{5,4},{6,7},{7,6},{8,9},{9,8},{10,11... | collective-permute-start | bytes 6291464 | tf_op jit(solution)/shard_map/ppermute | solution.py:500
  40.3 21.1 %collective-permute-start.1 = (bf16[16,2048]{1,0:T(8,128)(2,1)S(1)}, bf16[16,2048]{1,0:T(8,128)(2,1)S(1)}, u32[]{:S(2)}, u32[]{:S(2)}) collective-permute-start(bf16[16,2048]{1,0:T(8,128)(2,1)S(1)} %slice_select_fusion), channel_id=1, source_target_pairs={{0,2},{1,3},{2,4},{3,5},{4,6},{5,7},{6,8},{7,9},{8,10},{9,11},{10,... | collective-permute-start | bytes 196616 | tf_op jit(solution)/shard_map/ppermute | solution.py:502
  43.8 3.4 %collective-permute-start.2 = (f32[16,512]{1,0:T(8,128)S(1)}, f32[16,512]{1,0:T(8,128)S(1)}, u32[]{:S(2)}, u32[]{:S(2)}) collective-permute-start(f32[16,512]{1,0:T(8,128)S(1)} %dynamic-slice_bitcast_fusion), channel_id=1, source_target_pairs={{0,1},{1,0},{2,3},{3,2},{4,5},{5,4},{6,7},{7,6},{8,9},{9,8},{10,11... | collective-permute-start | bytes 98312 | tf_op jit(solution)/shard_map/ppermute | solution.py:505
  47.3 0.6 copy-start.4
  61.4 3.6 %copy-start.3 = (bf16[16,2048]{1,0:T(8,128)(2,1)}, bf16[16,2048]{1,0:T(8,128)(2,1)S(1)}, u32[]{:S(2)}) copy-start(bf16[16,2048]{1,0:T(8,128)(2,1)S(1)} %collective-permute-done.1.rows) | copy-start | bytes 196612
  63.3 2.1 copy-start
  65.4 34.5 %all-to-all-start.1 = ((bf16[16,128,512]{2,1,0:T(8,128)(2,1)}), bf16[16,128,512]{2,1,0:T(8,128)(2,1)}, u32[]{:S(2)}, u32[]{:S(2)}) async-start(bf16[16,128,512]{2,1,0:T(8,128)(2,1)} %broadcast_in_dim.42), calls=%async_computation.1 | async-start | bytes 4194304 | tf_op jit(solution)/shard_map/all_to_all | solution.py:53
  77.1 6.6 %collective-permute-start.3 = (bf16[1024,128]{1,0:T(8,128)(2,1)}, bf16[1024,128]{1,0:T(8,128)(2,1)S(1)}, u32[]{:S(2)}, u32[]{:S(2)}) collective-permute-start(bf16[1024,128]{1,0:T(8,128)(2,1)} %bc.1), channel_id=1, source_target_pairs={{0,1},{1,0},{2,3},{3,2},{4,5},{5,4},{6,7},{7,6},{8,9},{9,8},{10,11... | collective-permute-start | bytes 786440 | tf_op jit(solution)/shard_map/ppermute | solution.py:518
  100.0 38.4 %copy-start.6 = (s32[512]{0:T(512)S(1)}, s32[512]{0:T(512)}, u32[]{:S(2)}) copy-start(s32[512]{0:T(512)} %param.17) | copy-start | bytes 6148
  134.9 13.5 %all-to-all-start.4 = ((bf16[8,128,128]{2,1,0:T(8,128)(2,1)}), bf16[8,128,128]{2,1,0:T(8,128)(2,1)S(1)}, u32[]{:S(2)}, u32[]{:S(2)}) async-start(bf16[8,128,128]{2,1,0:T(8,128)(2,1)} %chain.1), calls=%async_computation.4 | async-start | bytes 524288 | tf_op jit(solution)/shard_map/all_to_all | solution.py:532
  148.5 0.7 copy-start.1

commit v6 on v5

--- a/solution.py
+++ b/solution.py
@@ -123,7 +123,7 @@
 
 
 def heads_body(
-    base, core, normed, w, taps, bias, b_all, c_all, columns, cum_r, skip, fades, *refs,
+    base, core, normed, w, taps, bias, mine, other, columns, cum_r, skip, fades, *refs,
 ):
     local, sent, w_all, p_all, state = refs[-5:]
     i = pl.program_id(0)
@@ -150,8 +150,9 @@
         start = pl.multiple_of(j * GROUP, GROUP)
         here = pl.ds(start, GROUP)
         mixed = mixed_rows(start, taps, bias, p_all)
-        b = b_all[here, :]
-        c = c_all[here, :]
+        ours, theirs = mine[here, :], other[here, :]
+        b = jnp.where(core[0] == 0, ours, theirs)
+        c = jnp.where(core[0] == 0, theirs, ours)
         scores = lax.dot_general(c, b, (((1,), (1,)), ((), ())), preferred_element_type=f32)
         cols = turned_to(columns[here, :], base + i)
 
@@ -186,7 +187,7 @@
             state[pair] = fade[GROUP - 1 :, :] * entering + block_state
         return carry
 
-    lax.fori_loop(0, BLOCKS, one, 0)
+    lax.fori_loop(0, BLOCKS, one, 0, unroll=2)
     slab = STATE // Y
     for y in range(Y):
         for pair in range(pairs):
@@ -195,7 +196,7 @@
 
 
 def heads_kernel(
-    core, base, steps, normed, w, taps, bias, bc, columns, cum_r, skip, fades, earlier,
+    core, base, steps, normed, w, taps, bias, mine, other, columns, cum_r, skip, fades, earlier,
 ):
     heads = COLS // HEADDIM
     sent = (Y, OWN // 128 * (STATE // Y) + PAD, 128)
@@ -220,8 +221,8 @@
                 pl.BlockSpec((16, 128, COLS), lambda i, core: (0, 0, i)),
                 pl.BlockSpec((4, COLS), channels),
                 pl.BlockSpec((1, COLS), channels),
-                pl.BlockSpec((None, ROWS, STATE), lambda i, core: (core[0], 0, 0)),
-                pl.BlockSpec((None, ROWS, STATE), lambda i, core: (1 - core[0], 0, 0)),
+                whole(mine.shape),
+                whole(other.shape),
                 whole(columns.shape),
                 pl.BlockSpec((1, heads, ROWS), step),
                 pl.BlockSpec(memory_space=pltpu.SMEM),
@@ -242,7 +243,7 @@
         compiler_params=params(),
         name="heads",
     )(
-        core, normed, w, taps, bias, bc, bc, columns, cum_r, skip, fades, *earlier,
+        core, normed, w, taps, bias, mine, other, columns, cum_r, skip, fades, *earlier,
     )
 
 
@@ -269,37 +270,58 @@
     )(parts)
 
 
-def finish_body(core, local, c_all, entering, columns, gain, order, out):
+def finish_body(core, local, mine, other, entering, columns, gain, order, out, normalized, pick):
+    @pl.when(pl.program_id(0) == 0)
+    def _():
+        position = lax.broadcasted_iota(jnp.int32, (POSITIONS, POSITIONS), 1)
+        pick[...] = jnp.where(position == order[...], 1.0, 0.0).astype(bf16)
+
+    heads = COLS // HEADDIM
     lane = lax.broadcasted_iota(jnp.int32, (GROUP, GROUP), 1)
     row = lax.broadcasted_iota(jnp.int32, (GROUP, GROUP), 0)
     same_head = jnp.where((lane < HEADDIM) == (row < HEADDIM), 1.0 / HEADDIM, 0.0).astype(bf16)
-    position = lax.broadcasted_iota(jnp.int32, (POSITIONS, POSITIONS), 1)
-    pick = jnp.where(position == order[...], 1.0, 0.0).astype(bf16)
-    first = lax.broadcasted_iota(jnp.int32, (1, 128), 1) < HEADDIM
+    wanted = 2 * (OWN // HEADDIM) + pl.program_id(0) * heads
+    source = lax.broadcasted_iota(jnp.int32, (GROUP, COLS), 0)
+    channel = lax.broadcasted_iota(jnp.int32, (GROUP, COLS), 1)
+    by_head = jnp.where(source == wanted + channel // HEADDIM, 1.0, 0.0).astype(bf16)
+    kept = lane >= 2 * (OWN // HEADDIM)
+    states = [
+        entering[:, p * (STATE // Y) : (p + 1) * (STATE // Y), :].reshape(STATE, 128)
+        for p in range(COLS // 128)
+    ]
+    state = jnp.concatenate(states, axis=1)
+
+    def one(j, carry):
+        here = pl.ds(pl.multiple_of(j * GROUP, GROUP), GROUP)
+        fades = jnp.exp2(jnp.where(kept, columns[here, :], 0.0))
+        high = fades.astype(bf16)
+        low = (fades - high.astype(f32)).astype(bf16)
+        fade = jnp.dot(high, by_head, preferred_element_type=f32) + jnp.dot(
+            low, by_head, preferred_element_type=f32
+        )
+        c = jnp.where(core[0] == 0, other[here, :], mine[here, :])
+        inter = jnp.dot(c, state, preferred_element_type=f32)
+        ssm = local[here, :].astype(f32) + fade * inter
+        square = ssm * ssm
+        high = square.astype(bf16)
+        low = (square - high.astype(f32)).astype(bf16)
+        for pair in range(COLS // 128):
+            wide = slice(128 * pair, 128 * pair + 128)
+            mean = jnp.dot(high[:, wide], same_head, preferred_element_type=f32) + jnp.dot(
+                low[:, wide], same_head, preferred_element_type=f32
+            )
+            scale = lax.rsqrt(mean + EPS) * gain[:, wide]
+            normalized[here, wide] = (ssm[:, wide] * scale).astype(bf16)
+        return carry
+
+    lax.fori_loop(0, BLOCKS, one, 0, unroll=2)
     for frame in range(ROWS // POSITIONS):
         here = slice(frame * POSITIONS, (frame + 1) * POSITIONS)
-        parts = []
-        cols = jnp.exp2(turned_to(columns[here, :], pl.program_id(0)))
-        for pair in range(COLS // 128):
-            wide = slice(128 * pair, 128 * pair + 128)
-            state = entering[:, pair * (STATE // Y) : (pair + 1) * (STATE // Y), :].reshape(STATE, 128)
-            inter = jnp.dot(c_all[here, :], state, preferred_element_type=f32)
-            h = 32 + 2 * pair
-            fade = jnp.where(first, cols[:, h : h + 1], cols[:, h + 1 : h + 2])
-            ssm = local[here, wide].astype(f32) + fade * inter
-            square = ssm * ssm
-            high = square.astype(bf16)
-            low = (square - high.astype(f32)).astype(bf16)
-            mean = jnp.dot(high, same_head, preferred_element_type=f32) + jnp.dot(
-                low, same_head, preferred_element_type=f32
-            )
-            parts.append((ssm * lax.rsqrt(mean + EPS) * gain[:, wide]).astype(bf16))
-        normalized = jnp.concatenate(parts, axis=1)
-        picked = jnp.dot(pick, normalized, preferred_element_type=f32).astype(bf16)
+        picked = jnp.dot(pick[...], normalized[here, :], preferred_element_type=f32).astype(bf16)
         out[:, frame] = picked.reshape(2 * Y, POSITIONS // (2 * Y), COLS)
 
 
-def finish_kernel(core, local, bc, entering, columns, gain, order):
+def finish_kernel(core, local, mine, other, entering, columns, gain, order):
     steps = OWN // COLS
     piece = POSITIONS // (2 * Y)
 
@@ -314,26 +336,32 @@
             grid=(steps,),
             in_specs=[
                 pl.BlockSpec((ROWS, COLS), column),
-                pl.BlockSpec((None, ROWS, STATE), lambda i, core: (1 - core[0], 0, 0)),
+                whole(mine.shape),
+                whole(other.shape),
                 pl.BlockSpec((Y, COLS // 128 * (STATE // Y), 128), lambda i, core: (0, i, 0)),
                 whole(columns.shape),
                 pl.BlockSpec((1, COLS), lambda i, core: (0, core[0] * steps + i)),
                 whole(order.shape),
             ],
             out_specs=pl.BlockSpec((2 * Y, 2, piece, COLS), lambda i, core: (0, 0, 0, i)),
+            scratch_shapes=[pltpu.VMEM((ROWS, COLS), bf16), pltpu.VMEM((POSITIONS, POSITIONS), bf16)],
         ),
         compiler_params=params(),
         name="finish",
-    )(core, local, bc, entering, columns, gain, order)
-
-
-def regroup_body(part, out):
-    row = lax.broadcasted_iota(jnp.int32, (POSITIONS, POSITIONS), 0)
-    col = lax.broadcasted_iota(jnp.int32, (POSITIONS, POSITIONS), 1)
-    piece = POSITIONS // (2 * Y)
-    pick = jnp.where(col == (row % (2 * Y)) * piece + row // (2 * Y), 1.0, 0.0).astype(bf16)
+    )(core, local, mine, other, entering, columns, gain, order)
+
+
+def regroup_body(part, out, pick):
+    @pl.when(pl.program_id(0) == 0)
+    def _():
+        row = lax.broadcasted_iota(jnp.int32, (POSITIONS, POSITIONS), 0)
+        col = lax.broadcasted_iota(jnp.int32, (POSITIONS, POSITIONS), 1)
+        piece = POSITIONS // (2 * Y)
+        chosen = col == (row % (2 * Y)) * piece + row // (2 * Y)
+        pick[...] = jnp.where(chosen, 1.0, 0.0).astype(bf16)
+
     rows = part[...].reshape(POSITIONS, OWN // 2)
-    out[...] = jnp.dot(pick, rows, preferred_element_type=f32).astype(bf16)
+    out[...] = jnp.dot(pick[...], rows, preferred_element_type=f32).astype(bf16)
 
 
 def regroup_kernel(part):
@@ -348,6 +376,7 @@
             )
         ],
         out_specs=pl.BlockSpec((POSITIONS, half), lambda i: (0, i)),
+        scratch_shapes=[pltpu.VMEM((POSITIONS, POSITIONS), bf16)],
         compiler_params=params(),
         name="regroup",
     )(part)
@@ -515,13 +544,13 @@
     chunks.append(spread(far_chunks[1], near_groups()))
 
     mine = bc_kernel(which, normed, chunks[0], conv_weight, bias)
-    bc = jnp.stack([mine, lax.ppermute(mine, "seq", swap)])
+    theirs = lax.ppermute(mine, "seq", swap)
     same_core = [list(range(c, 2 * Y, 2)) for c in range(2)]
     earlier = ()
     for g, steps in enumerate(PARTS):
         earlier = heads_kernel(
-            which, starts[g], steps, normed, chunks[g], conv_weight, bias, bc, columns, cum_r, skip,
-            fades, earlier,
+            which, starts[g], steps, normed, chunks[g], conv_weight, bias, mine, theirs, columns, cum_r,
+            skip, fades, earlier,
         )
         if g + 2 < len(PARTS):
             following, sent = lax.optimization_barrier((far_chunks[g + 2], earlier[1]))
@@ -532,7 +561,7 @@
     entering = lax.all_to_all(
         chain_kernel(parts), "seq", 0, 0, axis_index_groups=same_core, tiled=True
     )
-    outgoing = finish_kernel(which, local, bc, entering, columns, last_gain, order)
+    outgoing = finish_kernel(which, local, mine, theirs, entering, columns, last_gain, order)
     back = lax.all_to_all(outgoing, "seq", 0, 0, tiled=True)
     return regroup_kernel(back.reshape(Y, 2, 2, POSITIONS // (2 * Y), OWN))[None]
 

time: 222 us -> 222 us (level)
    pallas_call x1, Pallas kernels: 9.65 us -> 14.2 us  [finish_kernel(): pl.pallas_call(finish_body, out_shape=jax.ShapeDtypeStruct((2 * Y, 2, pie...]
    pallas_call x2, Pallas kernels: 29.1 us -> 26.1 us  [heads_kernel(): pl.pallas_call(functools.partial(heads_body, base), out_shape=(jax.ShapeD...]
  transfers between devices with their start and end apart: 7 -> 7, of which waited for: 6 -> 6; matrix products, arithmetic and copies ran while one was open for 2% -> 1% of each run, Pallas kernels for 13% -> 13%
where the time goes in v6:
time: 222 us; the launch traced here: 221 us
  blocking collectives  96.4 us (43%)
  Pallas kernels  61.6 us (28%)
  starting transfers between devices  31.8 us (14%)
  waiting for transfers between devices  21.1 us (10%)
  local copies, waits for them, and re-layouts  9.1 us (4%)
    all_to_all x1, blocking collectives, on_device(): back = lax.all_to_all(outgoing, 'seq', 0, 0, tiled=True)  59.5 us
    pallas_call x2, Pallas kernels, heads_kernel(): pl.pallas_call(functools.partial(heads_body, base), out_shape=(jax.ShapeD...  26.1 us
    all_to_all x1, blocking collectives, spread(): lax.all_to_all(jnp.broadcast_to(block[None], (count,) + block.shape), ('d...  20.1 us
    all_to_all x1, blocking collectives, on_device(): lax.all_to_all(sent, 'seq', 0, 0, axis_index_groups=same_core, tiled=True)  16.8 us
    pallas_call x1, Pallas kernels, finish_kernel(): pl.pallas_call(finish_body, out_shape=jax.ShapeDtypeStruct((2 * Y, 2, pie...  14.2 us
    all_to_all x2, starting transfers between devices, spread(): lax.all_to_all(jnp.broadcast_to(block[None], (count,) + block.shape), ('d...  12.9 us
    all_to_all x1, waiting for transfers between devices, on_device(): lax.all_to_all(chain_kernel(parts), 'seq', 0, 0, axis_index_groups=same_c...  8.49 us
    pallas_call x1, Pallas kernels, norm_kernel(): pl.pallas_call(norm_body, out_shape=jax.ShapeDtypeStruct((PAD + ROWS, wid...  5.99 us
  transfers between devices with their start and end apart: 7, of which 6 were waited for; matrix products, arithmetic and copies ran while one was open for 1% of the time, Pallas kernels for 13%

profile of v6, /device:TPU:1, one launch (start us, length us, event | category | flops | bytes accessed | tf_op | source)
XLA Modules:
  0.0 221.0 jit_solution(13122895732904803914)
XLA Ops:
  0.0 0.7 constant_dynamic-slice_fusion.1
  0.7 0.9 constant_dynamic-slice_fusion
  1.7 20.1 %all_to_all.30 = bf16[4,32,1152]{2,1,0:T(8,128)(2,1)S(1)} all-to-all(bf16[4,32,1152]{2,1,0:T(8,128)(2,1)S(1)} %broadcast_in_dim.41), channel_id=1, replica_groups={{0,128,256,384},{1,129,257,385},{2,130,258,386},{3,131,259,387},{4,132,..., dimensions={0} | all-to-all | bytes 589824 | tf_op jit(solution)/shard_map/all_to_all | solution.py:53
  21.7 1.8 broadcast_in_dim.43
  23.6 0.0 copy-start.3
  23.6 0.0 copy-start.6
  23.6 7.6 %all-to-all-start.2 = ((bf16[16,128,640]{2,1,0:T(8,128)(2,1)}), bf16[16,128,640]{2,1,0:T(8,128)(2,1)S(1)}, u32[]{:S(2)}, u32[]{:S(2)}) async-start(bf16[16,128,640]{2,1,0:T(8,128)(2,1)} %broadcast_in_dim.43), calls=%async_computation.2 | async-start | bytes 5242880 | tf_op jit(solution)/shard_map/all_to_all | solution.py:53
  31.1 4.1 %collective-permute-start = (bf16[512,2048]{1,0:T(8,128)(2,1)}, bf16[512,2048]{1,0:T(8,128)(2,1)}, u32[]{:S(2)}, u32[]{:S(2)}) collective-permute-start(bf16[512,2048]{1,0:T(8,128)(2,1)} %bitcast.14), channel_id=1, source_target_pairs={{0,1},{1,0},{2,3},{3,2},{4,5},{5,4},{6,7},{7,6},{8,9},{9,8},{10,11... | collective-permute-start | bytes 6291464 | tf_op jit(solution)/shard_map/ppermute | solution.py:529
  35.3 4.1 %collective-permute-done.sibling = bf16[512,2048]{1,0:T(8,128)(2,1)} collective-permute-done((bf16[512,2048]{1,0:T(8,128)(2,1)}, bf16[512,2048]{1,0:T(8,128)(2,1)}, u32[]{:S(2)}, u32[]{:S(2)}) %collective-permute-start) | collective-permute-done | bytes 2097184 | tf_op jit(solution)/shard_map/ppermute | solution.py:529
  39.4 0.9 slice_select_fusion
  40.3 3.5 %collective-permute-start.1 = (bf16[16,2048]{1,0:T(8,128)(2,1)S(1)}, bf16[16,2048]{1,0:T(8,128)(2,1)S(1)}, u32[]{:S(2)}, u32[]{:S(2)}) collective-permute-start(bf16[16,2048]{1,0:T(8,128)(2,1)S(1)} %slice_select_fusion), channel_id=1, source_target_pairs={{0,2},{1,3},{2,4},{3,5},{4,6},{5,7},{6,8},{7,9},{8,10},{9,11},{10,... | collective-permute-start | bytes 196616 | tf_op jit(solution)/shard_map/ppermute | solution.py:531
  43.8 0.0 copy-done.3
  43.8 2.6 %collective-permute-start.2 = (f32[16,512]{1,0:T(8,128)S(1)}, f32[16,512]{1,0:T(8,128)S(1)}, u32[]{:S(2)}, u32[]{:S(2)}) collective-permute-start(f32[16,512]{1,0:T(8,128)S(1)} %dynamic-slice_bitcast_fusion), channel_id=1, source_target_pairs={{0,1},{1,0},{2,3},{3,2},{4,5},{5,4},{6,7},{7,6},{8,9},{9,8},{10,11... | collective-permute-start | bytes 98312 | tf_op jit(solution)/shard_map/ppermute | solution.py:534
  46.4 0.0 copy-done.6
  46.4 0.6 broadcast_in_dim.38.bias
  47.0 0.2 collective-permute-done.2.other
  47.3 0.0 copy-start.5
  47.3 0.6 copy-done.5
  47.9 2.4 %decay.1 = (f32[4,4,1024]{2,1,0:T(4,128)}, f32[1024,128]{1,0:T(8,128)}, bf16[16,128]{1,0:T(8,128)(2,1)}) custom-call(s32[1]{0:T(128)} %bitcast.core, f32[32,512]{1,0:T(8,128)} %bitcast.18, f32[16,512]{1,0:T(8,128)} %copy-done.5), custom_call_target="tpu_custom_call" | custom-call | tf_op jit(solution)/shard_map/decay/pallas_call | solution.py:482
  50.3 6.0 %norm.1.normed = bf16[1040,2048]{1,0:T(8,128)(2,1)} custom-call(s32[1]{0:T(128)} %bitcast.core, bf16[512,2048]{1,0:T(8,128)(2,1)} %bitcast.15, bf16[512,2048]{1,0:T(8,128)(2,1)} %collective-permute-done.sibling, f32[1,2048]{1,0:T(1,128)} %bitcast.19), custom_call_target="tpu_custom_call" | custom-call | tf_op jit(solution)/shard_map/norm/pallas_call | solution.py:408
  56.3 5.1 %collective-permute-done.1.rows = bf16[16,2048]{1,0:T(8,128)(2,1)S(1)} collective-permute-done((bf16[16,2048]{1,0:T(8,128)(2,1)S(1)}, bf16[16,2048]{1,0:T(8,128)(2,1)S(1)}, u32[]{:S(2)}, u32[]{:S(2)}) %collective-permute-start.1) | collective-permute-done | bytes 65568 | tf_op jit(solution)/shard_map/ppermute | solution.py:531
  61.4 0.0 copy-start.4
  61.4 1.9 all-to-all-done.2.w
  63.3 0.0 copy-start
  63.3 1.7 broadcast_in_dim.42
  64.9 0.0 copy-done.4
  64.9 0.5 copy-done
  65.4 5.3 %all-to-all-start.1 = ((bf16[16,128,512]{2,1,0:T(8,128)(2,1)}), bf16[16,128,512]{2,1,0:T(8,128)(2,1)}, u32[]{:S(2)}, u32[]{:S(2)}) async-start(bf16[16,128,512]{2,1,0:T(8,128)(2,1)} %broadcast_in_dim.42), calls=%async_computation.1 | async-start | bytes 4194304 | tf_op jit(solution)/shard_map/all_to_all | solution.py:53
  70.8 1.6 tail.1.normed
  72.3 4.7 %bc.1.mine = bf16[1024,128]{1,0:T(8,128)(2,1)} custom-call(s32[1]{0:T(128)} %bitcast.core, bf16[1040,2048]{1,0:T(8,128)(2,1)} %tail.1.normed, bf16[16,128,640]{2,1,0:T(8,128)(2,1)} %copy-done, f32[4,2304]{1,0:T(4,128)} %taps.5, f32[1,2304]{1,0:T(1,128)} %broadcast_in_dim.38.bias), custom_call_target="tpu_custom_call" | custom-call | tf_op jit(solution)/shard_map/bc/pallas_call | solution.py:101
  77.1 5.2 %collective-permute-start.3 = (bf16[1024,128]{1,0:T(8,128)(2,1)}, bf16[1024,128]{1,0:T(8,128)(2,1)S(1)}, u32[]{:S(2)}, u32[]{:S(2)}) collective-permute-start(bf16[1024,128]{1,0:T(8,128)(2,1)} %bc.1.mine), channel_id=1, source_target_pairs={{0,1},{1,0},{2,3},{3,2},{4,5},{5,4},{6,7},{7,6},{8,9},{9,8},{10,11... | collective-permute-start | bytes 786440 | tf_op jit(solution)/shard_map/ppermute | solution.py:547
  82.3 1.4 collective-permute-done.3.other
  83.6 0.0 copy-start.1
  83.6 0.7 copy-done.1
  84.3 13.0 %heads.2 = (bf16[1024,1024]{1,0:T(8,128)(2,1)}, bf16[8,144,128]{2,1,0:T(8,128)(2,1)}) custom-call(s32[1]{0:T(128)} %bitcast.core, bf16[1040,2048]{1,0:T(8,128)(2,1)} %tail.1.normed, bf16[16,128,640]{2,1,0:T(8,128)(2,1)} %copy-done, f32[4,2304]{1,0:T(4,128)} %taps.5, f32[1,2304]{1,0:T(1,128)} %broadcast_in_dim.38.bias, bf16[1024,128]{1,0:T(8,128)(2,1)} %bc.1.mine, ...), custom_call_target="tpu_custom_call" | custom-call | tf_op jit(solution)/shard_map/heads/pallas_call | solution.py:210
  97.4 0.0 all-to-all-done.1.w
  97.4 0.0 copy-start.7
  97.4 13.1 %heads.3 = (bf16[1024,1024]{1,0:T(8,128)(2,1)}, bf16[8,144,128]{2,1,0:T(8,128)(2,1)}) custom-call(s32[1]{0:T(128)} %bitcast.core, bf16[1040,2048]{1,0:T(8,128)(2,1)} %tail.1.normed, bf16[16,128,512]{2,1,0:T(8,128)(2,1)} %all-to-all-done.1.w, f32[4,2304]{1,0:T(4,128)} %taps.5, ...), custom_call_target="tpu_custom_call", output_to_operand_aliasing={{0}: (11, {}), {1}: (12, {})} | custom-call | tf_op jit(solution)/shard_map/heads/pallas_call | solution.py:210
  110.5 16.8 %all_to_all.31.parts = bf16[8,144,128]{2,1,0:T(8,128)(2,1)} all-to-all(bf16[8,144,128]{2,1,0:T(8,128)(2,1)} %get-tuple-element.34), channel_id=1, replica_groups={{0,2,4,6,8,10,12,14},{1,3,5,7,9,11,13,15},{16,18,20,22,24,26,28,30},{17..., dimensions={0} | all-to-all | bytes 589824 | tf_op jit(solution)/shard_map/all_to_all | solution.py:560
  127.3 1.7 chain.1
  129.0 3.4 %all-to-all-start.4 = ((bf16[8,128,128]{2,1,0:T(8,128)(2,1)}), bf16[8,128,128]{2,1,0:T(8,128)(2,1)S(1)}, u32[]{:S(2)}, u32[]{:S(2)}) async-start(bf16[8,128,128]{2,1,0:T(8,128)(2,1)} %chain.1), calls=%async_computation.4 | async-start | bytes 524288 | tf_op jit(solution)/shard_map/all_to_all | solution.py:561
  132.4 0.0 copy-done.7
  132.5 0.9 copy.13.order
  133.3 8.5 %all-to-all-done.4.entering = bf16[8,128,128]{2,1,0:T(8,128)(2,1)S(1)} async-done(((bf16[8,128,128]{2,1,0:T(8,128)(2,1)}), bf16[8,128,128]{2,1,0:T(8,128)(2,1)S(1)}, u32[]{:S(2)}, u32[]{:S(2)}) %all-to-all-start.4) | async-done | bytes 262176 | tf_op jit(solution)/shard_map/all_to_all | solution.py:561
  141.8 0.7 copy-done.2
  142.5 14.2 %finish.1 = bf16[16,2,32,1024]{3,2,1,0:T(8,128)(2,1)} custom-call(s32[1]{0:T(128)} %bitcast.core, bf16[1024,1024]{1,0:T(8,128)(2,1)} %get-tuple-element.33.local, bf16[1024,128]{1,0:T(8,128)(2,1)} %bc.1.mine, bf16[1024,128]{1,0:T(8,128)(2,1)} %copy-done.1, bf16[8,128,128]{2,1,0:T(8,128)(2,1)} %copy-done.2, f32[1024,128]{1,0:T(8,128)} %get-tuple-element.28.columns, ...), custom_call_target="tpu_custom_call" | custom-call | tf_op jit(solution)/shard_map/finish/pallas_call | solution.py:331
  156.7 59.5 %all_to_all.32 = bf16[16,2,32,1024]{3,2,1,0:T(8,128)(2,1)} all-to-all(bf16[16,2,32,1024]{3,2,1,0:T(8,128)(2,1)} %finish.1), channel_id=1, replica_groups=mesh['dp'=32,'seq'=16] {'seq'}, dimensions={0} | all-to-all | bytes 4194304 | tf_op jit(solution)/shard_map/all_to_all | solution.py:565
  216.2 4.7 %regroup.1 = bf16[512,2048]{1,0:T(8,128)(2,1)} custom-call(bf16[8,2,2,32,1024]{4,3,2,1,0:T(8,128)(2,1)} %bitcast.13), custom_call_target="tpu_custom_call" | custom-call | tf_op jit(solution)/shard_map/regroup/pallas_call | solution.py:369
  (6 shorter events, 0.1 us)
Async XLA Ops:
  23.6 20.2 %copy-start.3 = (f32[1,32,512]{2,1,0:T(8,128)S(1)}, f32[1,32,512]{2,1,0:T(8,128)}, u32[]{:S(2)}) copy-start(f32[1,32,512]{2,1,0:T(8,128)} %param.14) | copy-start | bytes 196612
  23.6 22.8 %copy-start.6 = (f32[2304]{0:T(1024)S(1)}, f32[2304]{0:T(1024)}, u32[]{:S(2)}) copy-start(f32[2304]{0:T(1024)} %param.13) | copy-start | bytes 27652
  23.6 39.7 %all-to-all-start.2 = ((bf16[16,128,640]{2,1,0:T(8,128)(2,1)}), bf16[16,128,640]{2,1,0:T(8,128)(2,1)S(1)}, u32[]{:S(2)}, u32[]{:S(2)}) async-start(bf16[16,128,640]{2,1,0:T(8,128)(2,1)} %broadcast_in_dim.43), calls=%async_computation.2 | async-start | bytes 5242880 | tf_op jit(solution)/shard_map/all_to_all | solution.py:53
  31.1 8.2 %collective-permute-start = (bf16[512,2048]{1,0:T(8,128)(2,1)}, bf16[512,2048]{1,0:T(8,128)(2,1)}, u32[]{:S(2)}, u32[]{:S(2)}) collective-permute-start(bf16[512,2048]{1,0:T(8,128)(2,1)} %bitcast.14), channel_id=1, source_target_pairs={{0,1},{1,0},{2,3},{3,2},{4,5},{5,4},{6,7},{7,6},{8,9},{9,8},{10,11... | collective-permute-start | bytes 6291464 | tf_op jit(solution)/shard_map/ppermute | solution.py:529
  40.3 21.1 %collective-permute-start.1 = (bf16[16,2048]{1,0:T(8,128)(2,1)S(1)}, bf16[16,2048]{1,0:T(8,128)(2,1)S(1)}, u32[]{:S(2)}, u32[]{:S(2)}) collective-permute-start(bf16[16,2048]{1,0:T(8,128)(2,1)S(1)} %slice_select_fusion), channel_id=1, source_target_pairs={{0,2},{1,3},{2,4},{3,5},{4,6},{5,7},{6,8},{7,9},{8,10},{9,11},{10,... | collective-permute-start | bytes 196616 | tf_op jit(solution)/shard_map/ppermute | solution.py:531
  43.8 3.4 %collective-permute-start.2 = (f32[16,512]{1,0:T(8,128)S(1)}, f32[16,512]{1,0:T(8,128)S(1)}, u32[]{:S(2)}, u32[]{:S(2)}) collective-permute-start(f32[16,512]{1,0:T(8,128)S(1)} %dynamic-slice_bitcast_fusion), channel_id=1, source_target_pairs={{0,1},{1,0},{2,3},{3,2},{4,5},{5,4},{6,7},{7,6},{8,9},{9,8},{10,11... | collective-permute-start | bytes 98312 | tf_op jit(solution)/shard_map/ppermute | solution.py:534
  47.3 0.6 copy-start.5
  61.4 3.5 %copy-start.4 = (bf16[16,2048]{1,0:T(8,128)(2,1)}, bf16[16,2048]{1,0:T(8,128)(2,1)S(1)}, u32[]{:S(2)}) copy-start(bf16[16,2048]{1,0:T(8,128)(2,1)S(1)} %collective-permute-done.1.rows) | copy-start | bytes 196612
  63.3 2.1 copy-start
  65.4 32.0 %all-to-all-start.1 = ((bf16[16,128,512]{2,1,0:T(8,128)(2,1)}), bf16[16,128,512]{2,1,0:T(8,128)(2,1)}, u32[]{:S(2)}, u32[]{:S(2)}) async-start(bf16[16,128,512]{2,1,0:T(8,128)(2,1)} %broadcast_in_dim.42), calls=%async_computation.1 | async-start | bytes 4194304 | tf_op jit(solution)/shard_map/all_to_all | solution.py:53
  77.1 6.6 %collective-permute-start.3 = (bf16[1024,128]{1,0:T(8,128)(2,1)}, bf16[1024,128]{1,0:T(8,128)(2,1)S(1)}, u32[]{:S(2)}, u32[]{:S(2)}) collective-permute-start(bf16[1024,128]{1,0:T(8,128)(2,1)} %bc.1.mine), channel_id=1, source_target_pairs={{0,1},{1,0},{2,3},{3,2},{4,5},{5,4},{6,7},{7,6},{8,9},{9,8},{10,11... | collective-permute-start | bytes 786440 | tf_op jit(solution)/shard_map/ppermute | solution.py:547
  83.6 0.7 copy-start.1
  97.4 35.1 %copy-start.7 = (s32[512]{0:T(512)S(1)}, s32[512]{0:T(512)}, u32[]{:S(2)}) copy-start(s32[512]{0:T(512)} %param.17) | copy-start | bytes 6148
  129.0 12.8 %all-to-all-start.4 = ((bf16[8,128,128]{2,1,0:T(8,128)(2,1)}), bf16[8,128,128]{2,1,0:T(8,128)(2,1)S(1)}, u32[]{:S(2)}, u32[]{:S(2)}) async-start(bf16[8,128,128]{2,1,0:T(8,128)(2,1)} %chain.1), calls=%async_computation.4 | async-start | bytes 524288 | tf_op jit(solution)/shard_map/all_to_all | solution.py:561
  141.8 0.7 copy-start.2

commit v7 on v6

--- a/solution.py
+++ b/solution.py
@@ -48,12 +48,12 @@
     ]
 
 
-def spread(block, groups):
-    count = len(groups[0])
-    return lax.all_to_all(
-        jnp.broadcast_to(block[None], (count,) + block.shape),
-        ("dp", "seq"), 0, 0, axis_index_groups=groups, tiled=True,
-    )
+def copies(block, groups):
+    return jnp.broadcast_to(block[None], (len(groups[0]),) + block.shape)
+
+
+def spread(sent, groups):
+    return lax.all_to_all(sent, ("dp", "seq"), 0, 0, axis_index_groups=groups, tiled=True)
 
 
 def params():
@@ -187,7 +187,7 @@
             state[pair] = fade[GROUP - 1 :, :] * entering + block_state
         return carry
 
-    lax.fori_loop(0, BLOCKS, one, 0, unroll=2)
+    lax.fori_loop(0, BLOCKS, one, 0, unroll=4)
     slab = STATE // Y
     for y in range(Y):
         for pair in range(pairs):
@@ -270,29 +270,29 @@
     )(parts)
 
 
-def finish_body(core, local, mine, other, entering, columns, gain, order, out, normalized, pick):
+def finish_body(core, local, mine, other, entering, columns, gain, order, out, pick):
     @pl.when(pl.program_id(0) == 0)
     def _():
         position = lax.broadcasted_iota(jnp.int32, (POSITIONS, POSITIONS), 1)
         pick[...] = jnp.where(position == order[...], 1.0, 0.0).astype(bf16)
 
     heads = COLS // HEADDIM
-    lane = lax.broadcasted_iota(jnp.int32, (GROUP, GROUP), 1)
-    row = lax.broadcasted_iota(jnp.int32, (GROUP, GROUP), 0)
-    same_head = jnp.where((lane < HEADDIM) == (row < HEADDIM), 1.0 / HEADDIM, 0.0).astype(bf16)
+    row = lax.broadcasted_iota(jnp.int32, (COLS, COLS), 0)
+    lane = lax.broadcasted_iota(jnp.int32, (COLS, COLS), 1)
+    same_head = jnp.where(row // HEADDIM == lane // HEADDIM, 1.0 / HEADDIM, 0.0).astype(bf16)
     wanted = 2 * (OWN // HEADDIM) + pl.program_id(0) * heads
     source = lax.broadcasted_iota(jnp.int32, (GROUP, COLS), 0)
     channel = lax.broadcasted_iota(jnp.int32, (GROUP, COLS), 1)
     by_head = jnp.where(source == wanted + channel // HEADDIM, 1.0, 0.0).astype(bf16)
-    kept = lane >= 2 * (OWN // HEADDIM)
+    kept = lax.broadcasted_iota(jnp.int32, (1, GROUP), 1) >= 2 * (OWN // HEADDIM)
     states = [
         entering[:, p * (STATE // Y) : (p + 1) * (STATE // Y), :].reshape(STATE, 128)
         for p in range(COLS // 128)
     ]
     state = jnp.concatenate(states, axis=1)
 
-    def one(j, carry):
-        here = pl.ds(pl.multiple_of(j * GROUP, GROUP), GROUP)
+    for frame in range(ROWS // POSITIONS):
+        here = slice(frame * POSITIONS, (frame + 1) * POSITIONS)
         fades = jnp.exp2(jnp.where(kept, columns[here, :], 0.0))
         high = fades.astype(bf16)
         low = (fades - high.astype(f32)).astype(bf16)
@@ -302,22 +302,9 @@
         c = jnp.where(core[0] == 0, other[here, :], mine[here, :])
         inter = jnp.dot(c, state, preferred_element_type=f32)
         ssm = local[here, :].astype(f32) + fade * inter
-        square = ssm * ssm
-        high = square.astype(bf16)
-        low = (square - high.astype(f32)).astype(bf16)
-        for pair in range(COLS // 128):
-            wide = slice(128 * pair, 128 * pair + 128)
-            mean = jnp.dot(high[:, wide], same_head, preferred_element_type=f32) + jnp.dot(
-                low[:, wide], same_head, preferred_element_type=f32
-            )
-            scale = lax.rsqrt(mean + EPS) * gain[:, wide]
-            normalized[here, wide] = (ssm[:, wide] * scale).astype(bf16)
-        return carry
-
-    lax.fori_loop(0, BLOCKS, one, 0, unroll=2)
-    for frame in range(ROWS // POSITIONS):
-        here = slice(frame * POSITIONS, (frame + 1) * POSITIONS)
-        picked = jnp.dot(pick[...], normalized[here, :], preferred_element_type=f32).astype(bf16)
+        mean = jnp.dot((ssm * ssm).astype(bf16), same_head, preferred_element_type=f32)
+        normalized = (ssm * lax.rsqrt(mean + EPS) * gain[...]).astype(bf16)
+        picked = jnp.dot(pick[...], normalized, preferred_element_type=f32).astype(bf16)
         out[:, frame] = picked.reshape(2 * Y, POSITIONS // (2 * Y), COLS)
 
 
@@ -344,7 +331,7 @@
                 whole(order.shape),
             ],
             out_specs=pl.BlockSpec((2 * Y, 2, piece, COLS), lambda i, core: (0, 0, 0, i)),
-            scratch_shapes=[pltpu.VMEM((ROWS, COLS), bf16), pltpu.VMEM((POSITIONS, POSITIONS), bf16)],
+            scratch_shapes=[pltpu.VMEM((POSITIONS, POSITIONS), bf16)],
         ),
         compiler_params=params(),
         name="finish",
@@ -352,31 +339,29 @@
 
 
 def regroup_body(part, out, pick):
+    frames = 2 * Y
+
     @pl.when(pl.program_id(0) == 0)
     def _():
-        row = lax.broadcasted_iota(jnp.int32, (POSITIONS, POSITIONS), 0)
-        col = lax.broadcasted_iota(jnp.int32, (POSITIONS, POSITIONS), 1)
-        piece = POSITIONS // (2 * Y)
-        chosen = col == (row % (2 * Y)) * piece + row // (2 * Y)
-        pick[...] = jnp.where(chosen, 1.0, 0.0).astype(bf16)
-
-    rows = part[...].reshape(POSITIONS, OWN // 2)
+        row = lax.broadcasted_iota(jnp.int32, pick.shape, 0)
+        col = lax.broadcasted_iota(jnp.int32, pick.shape, 1)
+        each = pick.shape[0] // frames
+        pick[...] = jnp.where(col == (row % frames) * each + row // frames, 1.0, 0.0).astype(bf16)
+
+    rows = part[...].reshape(pick.shape[0], OWN)
     out[...] = jnp.dot(pick[...], rows, preferred_element_type=f32).astype(bf16)
 
 
 def regroup_kernel(part):
-    half = OWN // 2
+    each = POSITIONS // (2 * Y) // 2
+    rows = POSITIONS // 2
     return pl.pallas_call(
         regroup_body,
         out_shape=jax.ShapeDtypeStruct((POSITIONS, 2 * OWN), bf16),
         grid=(4,),
-        in_specs=[
-            pl.BlockSpec(
-                (Y, None, 2, POSITIONS // (2 * Y), half), lambda i: (0, i // 2, 0, 0, i % 2)
-            )
-        ],
-        out_specs=pl.BlockSpec((POSITIONS, half), lambda i: (0, i)),
-        scratch_shapes=[pltpu.VMEM((POSITIONS, POSITIONS), bf16)],
+        in_specs=[pl.BlockSpec((Y, None, 2, each, OWN), lambda i: (0, i % 2, 0, i // 2, 0))],
+        out_specs=pl.BlockSpec((rows, OWN), lambda i: (i // 2, i % 2)),
+        scratch_shapes=[pltpu.VMEM((rows, rows), bf16)],
         compiler_params=params(),
         name="regroup",
     )(part)
@@ -518,10 +503,10 @@
         axis=1,
     )
     half = lax.dynamic_slice_in_dim(weight, (y % 2) * 32, 32, 0)
-    far = spread(half, far_groups()).reshape(128, STATE + OWN)
+    far = spread(copies(half, far_groups()), far_groups()).reshape(128, STATE + OWN)
     starts = [sum(PARTS[:g]) for g in range(len(PARTS) + 1)]
     cuts = [0] + [STATE + COLS * start for start in starts[1:]]
-    far_chunks = [far[:, a:b] for a, b in zip(cuts, cuts[1:])]
+    far_chunks = [copies(far[:, a:b], near_groups()) for a, b in zip(cuts, cuts[1:])]
     chunks = [spread(far_chunks[0], near_groups())]
 
     own = tokens[0]

time: 222 us -> 213 us (0.959)
  Pallas kernels: 61.6 us -> 54.7 us
    pallas_call x1, Pallas kernels: 14.2 us -> 8.57 us  [finish_kernel(): pl.pallas_call(finish_body, out_shape=jax.ShapeDtypeStruct((2 * Y, 2, pie...]
  transfers between devices with their start and end apart: 7 -> 7, of which waited for: 6 -> 7; matrix products, arithmetic and copies ran while one was open for 1% -> 2% of each run, Pallas kernels for 13% -> 13%
where the time goes in v7:
time: 213 us; the launch traced here: 212 us
  blocking collectives  96.1 us (45%)
  Pallas kernels  54.7 us (26%)
  starting transfers between devices  32 us (15%)
  waiting for transfers between devices  19.7 us (9%)
  local copies, waits for them, and re-layouts  8.48 us (4%)
    all_to_all x1, blocking collectives, on_device(): back = lax.all_to_all(outgoing, 'seq', 0, 0, tiled=True)  60.3 us
    pallas_call x2, Pallas kernels, heads_kernel(): pl.pallas_call(functools.partial(heads_body, base), out_shape=(jax.ShapeD...  25.3 us
    all_to_all x1, blocking collectives, spread(): lax.all_to_all(sent, ('dp', 'seq'), 0, 0, axis_index_groups=groups, tiled...  20.1 us
    all_to_all x1, blocking collectives, on_device(): lax.all_to_all(sent, 'seq', 0, 0, axis_index_groups=same_core, tiled=True)  15.7 us
    all_to_all x2, starting transfers between devices, spread(): lax.all_to_all(sent, ('dp', 'seq'), 0, 0, axis_index_groups=groups, tiled...  12.9 us
    pallas_call x1, Pallas kernels, finish_kernel(): pl.pallas_call(finish_body, out_shape=jax.ShapeDtypeStruct((2 * Y, 2, pie...  8.57 us
    all_to_all x1, waiting for transfers between devices, on_device(): lax.all_to_all(chain_kernel(parts), 'seq', 0, 0, axis_index_groups=same_c...  8.5 us
    pallas_call x1, Pallas kernels, norm_kernel(): pl.pallas_call(norm_body, out_shape=jax.ShapeDtypeStruct((PAD + ROWS, wid...  5.99 us
  transfers between devices with their start and end apart: 7, of which 7 were waited for; matrix products, arithmetic and copies ran while one was open for 2% of the time, Pallas kernels for 13%

profile of v7, /device:TPU:1, one launch (start us, length us, event | category | flops | bytes accessed | tf_op | source)
XLA Modules:
  0.0 212.0 jit_solution(523256317255292470)
XLA Ops:
  0.0 0.7 constant_dynamic-slice_fusion.1
  0.7 0.9 constant_dynamic-slice_fusion
  1.7 20.1 %all_to_all.30 = bf16[4,32,1152]{2,1,0:T(8,128)(2,1)S(1)} all-to-all(bf16[4,32,1152]{2,1,0:T(8,128)(2,1)S(1)} %broadcast_in_dim.41), channel_id=1, replica_groups={{0,128,256,384},{1,129,257,385},{2,130,258,386},{3,131,259,387},{4,132,..., dimensions={0} | all-to-all | bytes 589824 | tf_op jit(solution)/shard_map/all_to_all | solution.py:56
  21.7 1.8 broadcast_in_dim.42
  23.6 0.0 copy-start.3
  23.6 0.0 copy-start.6
  23.6 7.6 %all-to-all-start.2 = ((bf16[16,128,640]{2,1,0:T(8,128)(2,1)}), bf16[16,128,640]{2,1,0:T(8,128)(2,1)S(1)}, u32[]{:S(2)}, u32[]{:S(2)}) async-start(bf16[16,128,640]{2,1,0:T(8,128)(2,1)} %broadcast_in_dim.42), calls=%async_computation.2 | async-start | bytes 5242880 | tf_op jit(solution)/shard_map/all_to_all | solution.py:56
  31.1 4.1 %collective-permute-start = (bf16[512,2048]{1,0:T(8,128)(2,1)}, bf16[512,2048]{1,0:T(8,128)(2,1)}, u32[]{:S(2)}, u32[]{:S(2)}) collective-permute-start(bf16[512,2048]{1,0:T(8,128)(2,1)} %bitcast.14), channel_id=1, source_target_pairs={{0,1},{1,0},{2,3},{3,2},{4,5},{5,4},{6,7},{7,6},{8,9},{9,8},{10,11... | collective-permute-start | bytes 6291464 | tf_op jit(solution)/shard_map/ppermute | solution.py:514
  35.3 4.1 %collective-permute-done.sibling = bf16[512,2048]{1,0:T(8,128)(2,1)} collective-permute-done((bf16[512,2048]{1,0:T(8,128)(2,1)}, bf16[512,2048]{1,0:T(8,128)(2,1)}, u32[]{:S(2)}, u32[]{:S(2)}) %collective-permute-start) | collective-permute-done | bytes 2097184 | tf_op jit(solution)/shard_map/ppermute | solution.py:514
  39.4 0.9 slice_select_fusion
  40.3 3.5 %collective-permute-start.1 = (bf16[16,2048]{1,0:T(8,128)(2,1)S(1)}, bf16[16,2048]{1,0:T(8,128)(2,1)S(1)}, u32[]{:S(2)}, u32[]{:S(2)}) collective-permute-start(bf16[16,2048]{1,0:T(8,128)(2,1)S(1)} %slice_select_fusion), channel_id=1, source_target_pairs={{0,2},{1,3},{2,4},{3,5},{4,6},{5,7},{6,8},{7,9},{8,10},{9,11},{10,... | collective-permute-start | bytes 196616 | tf_op jit(solution)/shard_map/ppermute | solution.py:516
  43.8 0.0 copy-done.3
  43.8 2.6 %collective-permute-start.2 = (f32[16,512]{1,0:T(8,128)S(1)}, f32[16,512]{1,0:T(8,128)S(1)}, u32[]{:S(2)}, u32[]{:S(2)}) collective-permute-start(f32[16,512]{1,0:T(8,128)S(1)} %dynamic-slice_bitcast_fusion), channel_id=1, source_target_pairs={{0,1},{1,0},{2,3},{3,2},{4,5},{5,4},{6,7},{7,6},{8,9},{9,8},{10,11... | collective-permute-start | bytes 98312 | tf_op jit(solution)/shard_map/ppermute | solution.py:519
  46.4 0.0 copy-done.6
  46.4 0.6 broadcast_in_dim.38.bias
  47.0 0.2 collective-permute-done.2.other
  47.3 0.0 copy-start.5
  47.3 0.6 copy-done.5
  47.9 2.4 %decay.1 = (f32[4,4,1024]{2,1,0:T(4,128)}, f32[1024,128]{1,0:T(8,128)}, bf16[16,128]{1,0:T(8,128)(2,1)}) custom-call(s32[1]{0:T(128)} %bitcast.core, f32[32,512]{1,0:T(8,128)} %bitcast.18, f32[16,512]{1,0:T(8,128)} %copy-done.5), custom_call_target="tpu_custom_call" | custom-call | tf_op jit(solution)/shard_map/decay/pallas_call | solution.py:467
  50.3 6.0 %norm.1.normed = bf16[1040,2048]{1,0:T(8,128)(2,1)} custom-call(s32[1]{0:T(128)} %bitcast.core, bf16[512,2048]{1,0:T(8,128)(2,1)} %bitcast.15, bf16[512,2048]{1,0:T(8,128)(2,1)} %collective-permute-done.sibling, f32[1,2048]{1,0:T(1,128)} %bitcast.19), custom_call_target="tpu_custom_call" | custom-call | tf_op jit(solution)/shard_map/norm/pallas_call | solution.py:393
  56.3 5.1 %collective-permute-done.1.rows = bf16[16,2048]{1,0:T(8,128)(2,1)S(1)} collective-permute-done((bf16[16,2048]{1,0:T(8,128)(2,1)S(1)}, bf16[16,2048]{1,0:T(8,128)(2,1)S(1)}, u32[]{:S(2)}, u32[]{:S(2)}) %collective-permute-start.1) | collective-permute-done | bytes 65568 | tf_op jit(solution)/shard_map/ppermute | solution.py:516
  61.4 0.0 copy-start.4
  61.4 1.5 broadcast_in_dim.43
  62.9 0.4 all-to-all-done.2.w
  63.3 0.0 copy-start
  63.3 0.0 copy-done.4
  63.3 5.3 %all-to-all-start.1 = ((bf16[16,128,512]{2,1,0:T(8,128)(2,1)}), bf16[16,128,512]{2,1,0:T(8,128)(2,1)}, u32[]{:S(2)}, u32[]{:S(2)}) async-start(bf16[16,128,512]{2,1,0:T(8,128)(2,1)} %broadcast_in_dim.43), calls=%async_computation.1 | async-start | bytes 4194304 | tf_op jit(solution)/shard_map/all_to_all | solution.py:56
  68.6 1.6 tail.1.normed
  70.2 0.0 copy-done
  70.2 4.7 %bc.1.mine = bf16[1024,128]{1,0:T(8,128)(2,1)} custom-call(s32[1]{0:T(128)} %bitcast.core, bf16[1040,2048]{1,0:T(8,128)(2,1)} %tail.1.normed, bf16[16,128,640]{2,1,0:T(8,128)(2,1)} %copy-done, f32[4,2304]{1,0:T(4,128)} %taps.5, f32[1,2304]{1,0:T(1,128)} %broadcast_in_dim.38.bias), custom_call_target="tpu_custom_call" | custom-call | tf_op jit(solution)/shard_map/bc/pallas_call | solution.py:101
  74.9 5.2 %collective-permute-start.3 = (bf16[1024,128]{1,0:T(8,128)(2,1)}, bf16[1024,128]{1,0:T(8,128)(2,1)S(1)}, u32[]{:S(2)}, u32[]{:S(2)}) collective-permute-start(bf16[1024,128]{1,0:T(8,128)(2,1)} %bc.1.mine), channel_id=1, source_target_pairs={{0,1},{1,0},{2,3},{3,2},{4,5},{5,4},{6,7},{7,6},{8,9},{9,8},{10,11... | collective-permute-start | bytes 786440 | tf_op jit(solution)/shard_map/ppermute | solution.py:532
  80.2 1.4 collective-permute-done.3.other
  81.5 0.0 copy-start.1
  81.5 0.7 copy-done.1
  82.2 12.6 %heads.2 = (bf16[1024,1024]{1,0:T(8,128)(2,1)}, bf16[8,144,128]{2,1,0:T(8,128)(2,1)}) custom-call(s32[1]{0:T(128)} %bitcast.core, bf16[1040,2048]{1,0:T(8,128)(2,1)} %tail.1.normed, bf16[16,128,640]{2,1,0:T(8,128)(2,1)} %copy-done, f32[4,2304]{1,0:T(4,128)} %taps.5, f32[1,2304]{1,0:T(1,128)} %broadcast_in_dim.38.bias, bf16[1024,128]{1,0:T(8,128)(2,1)} %bc.1.mine, ...), custom_call_target="tpu_custom_call" | custom-call | tf_op jit(solution)/shard_map/heads/pallas_call | solution.py:210
  94.9 0.1 all-to-all-done.1.w
  94.9 0.0 copy-start.7
  94.9 12.7 %heads.3 = (bf16[1024,1024]{1,0:T(8,128)(2,1)}, bf16[8,144,128]{2,1,0:T(8,128)(2,1)}) custom-call(s32[1]{0:T(128)} %bitcast.core, bf16[1040,2048]{1,0:T(8,128)(2,1)} %tail.1.normed, bf16[16,128,512]{2,1,0:T(8,128)(2,1)} %all-to-all-done.1.w, f32[4,2304]{1,0:T(4,128)} %taps.5, ...), custom_call_target="tpu_custom_call", output_to_operand_aliasing={{0}: (11, {}), {1}: (12, {})} | custom-call | tf_op jit(solution)/shard_map/heads/pallas_call | solution.py:210
  107.7 15.7 %all_to_all.31.parts = bf16[8,144,128]{2,1,0:T(8,128)(2,1)} all-to-all(bf16[8,144,128]{2,1,0:T(8,128)(2,1)} %get-tuple-element.34), channel_id=1, replica_groups={{0,2,4,6,8,10,12,14},{1,3,5,7,9,11,13,15},{16,18,20,22,24,26,28,30},{17..., dimensions={0} | all-to-all | bytes 589824 | tf_op jit(solution)/shard_map/all_to_all | solution.py:545
  123.4 1.7 chain.1
  125.1 3.6 %all-to-all-start.4 = ((bf16[8,128,128]{2,1,0:T(8,128)(2,1)}), bf16[8,128,128]{2,1,0:T(8,128)(2,1)S(1)}, u32[]{:S(2)}, u32[]{:S(2)}) async-start(bf16[8,128,128]{2,1,0:T(8,128)(2,1)} %chain.1), calls=%async_computation.4 | async-start | bytes 524288 | tf_op jit(solution)/shard_map/all_to_all | solution.py:546
  128.8 0.0 copy-done.7
  128.8 0.9 copy.13.order
  129.6 8.5 %all-to-all-done.4.entering = bf16[8,128,128]{2,1,0:T(8,128)(2,1)S(1)} async-done(((bf16[8,128,128]{2,1,0:T(8,128)(2,1)}), bf16[8,128,128]{2,1,0:T(8,128)(2,1)S(1)}, u32[]{:S(2)}, u32[]{:S(2)}) %all-to-all-start.4) | async-done | bytes 262176 | tf_op jit(solution)/shard_map/all_to_all | solution.py:546
  138.1 0.7 copy-done.2
  138.8 8.6 %finish.1 = bf16[16,2,32,1024]{3,2,1,0:T(8,128)(2,1)} custom-call(s32[1]{0:T(128)} %bitcast.core, bf16[1024,1024]{1,0:T(8,128)(2,1)} %get-tuple-element.33.local, bf16[1024,128]{1,0:T(8,128)(2,1)} %bc.1.mine, bf16[1024,128]{1,0:T(8,128)(2,1)} %copy-done.1, bf16[8,128,128]{2,1,0:T(8,128)(2,1)} %copy-done.2, f32[1024,128]{1,0:T(8,128)} %get-tuple-element.28.columns, ...), custom_call_target="tpu_custom_call" | custom-call | tf_op jit(solution)/shard_map/finish/pallas_call | solution.py:318
  147.4 60.3 %all_to_all.32 = bf16[16,2,32,1024]{3,2,1,0:T(8,128)(2,1)} all-to-all(bf16[16,2,32,1024]{3,2,1,0:T(8,128)(2,1)} %finish.1), channel_id=1, replica_groups=mesh['dp'=32,'seq'=16] {'seq'}, dimensions={0} | all-to-all | bytes 4194304 | tf_op jit(solution)/shard_map/all_to_all | solution.py:550
  207.6 4.4 %regroup.1 = bf16[512,2048]{1,0:T(8,128)(2,1)} custom-call(bf16[8,2,2,32,1024]{4,3,2,1,0:T(8,128)(2,1)} %bitcast.13), custom_call_target="tpu_custom_call" | custom-call | tf_op jit(solution)/shard_map/regroup/pallas_call | solution.py:358
  (6 shorter events, 0.1 us)
Async XLA Ops:
  23.6 20.2 %copy-start.3 = (f32[1,32,512]{2,1,0:T(8,128)S(1)}, f32[1,32,512]{2,1,0:T(8,128)}, u32[]{:S(2)}) copy-start(f32[1,32,512]{2,1,0:T(8,128)} %param.14) | copy-start | bytes 196612
  23.6 22.8 %copy-start.6 = (f32[2304]{0:T(1024)S(1)}, f32[2304]{0:T(1024)}, u32[]{:S(2)}) copy-start(f32[2304]{0:T(1024)} %param.13) | copy-start | bytes 27652
  23.6 39.7 %all-to-all-start.2 = ((bf16[16,128,640]{2,1,0:T(8,128)(2,1)}), bf16[16,128,640]{2,1,0:T(8,128)(2,1)S(1)}, u32[]{:S(2)}, u32[]{:S(2)}) async-start(bf16[16,128,640]{2,1,0:T(8,128)(2,1)} %broadcast_in_dim.42), calls=%async_computation.2 | async-start | bytes 5242880 | tf_op jit(solution)/shard_map/all_to_all | solution.py:56
  31.1 8.2 %collective-permute-start = (bf16[512,2048]{1,0:T(8,128)(2,1)}, bf16[512,2048]{1,0:T(8,128)(2,1)}, u32[]{:S(2)}, u32[]{:S(2)}) collective-permute-start(bf16[512,2048]{1,0:T(8,128)(2,1)} %bitcast.14), channel_id=1, source_target_pairs={{0,1},{1,0},{2,3},{3,2},{4,5},{5,4},{6,7},{7,6},{8,9},{9,8},{10,11... | collective-permute-start | bytes 6291464 | tf_op jit(solution)/shard_map/ppermute | solution.py:514
  40.3 21.1 %collective-permute-start.1 = (bf16[16,2048]{1,0:T(8,128)(2,1)S(1)}, bf16[16,2048]{1,0:T(8,128)(2,1)S(1)}, u32[]{:S(2)}, u32[]{:S(2)}) collective-permute-start(bf16[16,2048]{1,0:T(8,128)(2,1)S(1)} %slice_select_fusion), channel_id=1, source_target_pairs={{0,2},{1,3},{2,4},{3,5},{4,6},{5,7},{6,8},{7,9},{8,10},{9,11},{10,... | collective-permute-start | bytes 196616 | tf_op jit(solution)/shard_map/ppermute | solution.py:516
  43.8 3.4 %collective-permute-start.2 = (f32[16,512]{1,0:T(8,128)S(1)}, f32[16,512]{1,0:T(8,128)S(1)}, u32[]{:S(2)}, u32[]{:S(2)}) collective-permute-start(f32[16,512]{1,0:T(8,128)S(1)} %dynamic-slice_bitcast_fusion), channel_id=1, source_target_pairs={{0,1},{1,0},{2,3},{3,2},{4,5},{5,4},{6,7},{7,6},{8,9},{9,8},{10,11... | collective-permute-start | bytes 98312 | tf_op jit(solution)/shard_map/ppermute | solution.py:519
  47.3 0.6 copy-start.5
  61.4 1.9 copy-start.4
  63.3 6.9 %copy-start = (bf16[16,128,640]{2,1,0:T(8,128)(2,1)}, bf16[16,128,640]{2,1,0:T(8,128)(2,1)S(1)}, u32[]{:S(2)}) copy-start(bf16[16,128,640]{2,1,0:T(8,128)(2,1)S(1)} %all-to-all-done.2.w) | copy-start | bytes 7864324
  63.3 31.7 %all-to-all-start.1 = ((bf16[16,128,512]{2,1,0:T(8,128)(2,1)}), bf16[16,128,512]{2,1,0:T(8,128)(2,1)}, u32[]{:S(2)}, u32[]{:S(2)}) async-start(bf16[16,128,512]{2,1,0:T(8,128)(2,1)} %broadcast_in_dim.43), calls=%async_computation.1 | async-start | bytes 4194304 | tf_op jit(solution)/shard_map/all_to_all | solution.py:56
  74.9 6.6 %collective-permute-start.3 = (bf16[1024,128]{1,0:T(8,128)(2,1)}, bf16[1024,128]{1,0:T(8,128)(2,1)S(1)}, u32[]{:S(2)}, u32[]{:S(2)}) collective-permute-start(bf16[1024,128]{1,0:T(8,128)(2,1)} %bc.1.mine), channel_id=1, source_target_pairs={{0,1},{1,0},{2,3},{3,2},{4,5},{5,4},{6,7},{7,6},{8,9},{9,8},{10,11... | collective-permute-start | bytes 786440 | tf_op jit(solution)/shard_map/ppermute | solution.py:532
  81.5 0.7 copy-start.1
  94.9 33.8 %copy-start.7 = (s32[512]{0:T(512)S(1)}, s32[512]{0:T(512)}, u32[]{:S(2)}) copy-start(s32[512]{0:T(512)} %param.17) | copy-start | bytes 6148
  125.1 13.0 %all-to-all-start.4 = ((bf16[8,128,128]{2,1,0:T(8,128)(2,1)}), bf16[8,128,128]{2,1,0:T(8,128)(2,1)S(1)}, u32[]{:S(2)}, u32[]{:S(2)}) async-start(bf16[8,128,128]{2,1,0:T(8,128)(2,1)} %chain.1), calls=%async_computation.4 | async-start | bytes 524288 | tf_op jit(solution)/shard_map/all_to_all | solution.py:546
  138.1 0.7 copy-start.2

commit v8 on v7

--- a/solution.py
+++ b/solution.py
@@ -89,7 +89,7 @@
         out[pl.ds(start, GROUP), :] = mixed_rows(start, taps, bias, p_all)
         return carry
 
-    lax.fori_loop(0, BLOCKS, one, 0)
+    lax.fori_loop(0, BLOCKS, one, 0, unroll=2)
 
 
 def bc_kernel(core, normed, w, taps, bias):
@@ -145,6 +145,8 @@
     lane = lax.broadcasted_iota(jnp.int32, (GROUP, GROUP), 1)
     causal = lane <= row
     first = lane < HEADDIM
+    of_first = jnp.where(first, 1.0, 0.0).astype(bf16)
+    of_second = jnp.where(first, 0.0, 1.0).astype(bf16)
 
     def one(j, carry):
         start = pl.multiple_of(j * GROUP, GROUP)
@@ -170,7 +172,7 @@
                 weights.append((scores * jnp.exp2(jnp.where(causal, gap, -1e30))).astype(bf16))
             both = jnp.concatenate(weights, axis=1)
             apart = jnp.concatenate(
-                [jnp.where(first, x, 0.0).astype(bf16), jnp.where(first, 0.0, x).astype(bf16)], axis=0
+                [mixed[:, wide] * of_first, mixed[:, wide] * of_second], axis=0
             )
             intra = jnp.dot(both, apart, preferred_element_type=f32)
             cum = jnp.where(first, cums[0], cums[1])
@@ -514,6 +516,7 @@
     sibling = lax.ppermute(own, "seq", swap)
     tail = jnp.where(core == 1, own[POSITIONS - PAD :], sibling[POSITIONS - PAD :])
     tail = lax.ppermute(tail, "seq", onward)
+    sibling, far_chunks = lax.optimization_barrier((sibling, far_chunks))
     normed = norm_kernel(which, own, sibling, gain)
     other = lax.dynamic_slice_in_dim(log_decay[0], (1 - core) * head_count, head_count, 0)
     decays = decay_kernel(which, log_decay[0], lax.ppermute(other, "seq", swap))

time: 213 us -> 213 us (level)
  no operation moved by 1% of the time
where the time goes in v8:
time: 213 us; the launch traced here: 212 us
  blocking collectives  96.2 us (45%)
  Pallas kernels  54.6 us (26%)
  starting transfers between devices  31.8 us (15%)
  waiting for transfers between devices  19.7 us (9%)
  local copies, waits for them, and re-layouts  8.49 us (4%)
    all_to_all x1, blocking collectives, on_device(): back = lax.all_to_all(outgoing, 'seq', 0, 0, tiled=True)  60.1 us
    pallas_call x2, Pallas kernels, heads_kernel(): pl.pallas_call(functools.partial(heads_body, base), out_shape=(jax.ShapeD...  25.3 us
    all_to_all x1, blocking collectives, spread(): lax.all_to_all(sent, ('dp', 'seq'), 0, 0, axis_index_groups=groups, tiled...  20.1 us
    all_to_all x1, blocking collectives, on_device(): lax.all_to_all(sent, 'seq', 0, 0, axis_index_groups=same_core, tiled=True)  16.1 us
    all_to_all x2, starting transfers between devices, spread(): lax.all_to_all(sent, ('dp', 'seq'), 0, 0, axis_index_groups=groups, tiled...  12.9 us
    pallas_call x1, Pallas kernels, finish_kernel(): pl.pallas_call(finish_body, out_shape=jax.ShapeDtypeStruct((2 * Y, 2, pie...  8.56 us
    all_to_all x1, waiting for transfers between devices, on_device(): lax.all_to_all(chain_kernel(parts), 'seq', 0, 0, axis_index_groups=same_c...  8.49 us
    pallas_call x1, Pallas kernels, norm_kernel(): pl.pallas_call(norm_body, out_shape=jax.ShapeDtypeStruct((PAD + ROWS, wid...  5.99 us
  transfers between devices with their start and end apart: 7, of which 7 were waited for; matrix products, arithmetic and copies ran while one was open for 2% of the time, Pallas kernels for 13%

profile of v8, /device:TPU:1, one launch (start us, length us, event | category | flops | bytes accessed | tf_op | source)
XLA Modules:
  0.0 211.9 jit_solution(9212285238831446186)
XLA Ops:
  0.0 0.7 constant_dynamic-slice_fusion.1
  0.7 0.9 constant_dynamic-slice_fusion
  1.7 20.1 %all_to_all.30 = bf16[4,32,1152]{2,1,0:T(8,128)(2,1)S(1)} all-to-all(bf16[4,32,1152]{2,1,0:T(8,128)(2,1)S(1)} %broadcast_in_dim.37), channel_id=1, replica_groups={{0,128,256,384},{1,129,257,385},{2,130,258,386},{3,131,259,387},{4,132,..., dimensions={0} | all-to-all | bytes 589824 | tf_op jit(solution)/shard_map/all_to_all | solution.py:56
  21.7 1.8 broadcast_in_dim.38
  23.6 0.0 copy-start.3
  23.6 0.0 copy-start.6
  23.6 7.6 %all-to-all-start.2 = ((bf16[16,128,640]{2,1,0:T(8,128)(2,1)}), bf16[16,128,640]{2,1,0:T(8,128)(2,1)S(1)}, u32[]{:S(2)}, u32[]{:S(2)}) async-start(bf16[16,128,640]{2,1,0:T(8,128)(2,1)} %broadcast_in_dim.38), calls=%async_computation.2 | async-start | bytes 5242880 | tf_op jit(solution)/shard_map/all_to_all | solution.py:56
  31.1 4.1 %collective-permute-start = (bf16[512,2048]{1,0:T(8,128)(2,1)}, bf16[512,2048]{1,0:T(8,128)(2,1)}, u32[]{:S(2)}, u32[]{:S(2)}) collective-permute-start(bf16[512,2048]{1,0:T(8,128)(2,1)} %bitcast.14), channel_id=1, source_target_pairs={{0,1},{1,0},{2,3},{3,2},{4,5},{5,4},{6,7},{7,6},{8,9},{9,8},{10,11... | collective-permute-start | bytes 6291464 | tf_op jit(solution)/shard_map/ppermute | solution.py:516
  35.3 4.1 %collective-permute-done.sibling = bf16[512,2048]{1,0:T(8,128)(2,1)} collective-permute-done((bf16[512,2048]{1,0:T(8,128)(2,1)}, bf16[512,2048]{1,0:T(8,128)(2,1)}, u32[]{:S(2)}, u32[]{:S(2)}) %collective-permute-start) | collective-permute-done | bytes 2097184 | tf_op jit(solution)/shard_map/ppermute | solution.py:516
  39.4 0.9 slice_select_fusion
  40.3 3.5 %collective-permute-start.1 = (bf16[16,2048]{1,0:T(8,128)(2,1)S(1)}, bf16[16,2048]{1,0:T(8,128)(2,1)S(1)}, u32[]{:S(2)}, u32[]{:S(2)}) collective-permute-start(bf16[16,2048]{1,0:T(8,128)(2,1)S(1)} %slice_select_fusion), channel_id=1, source_target_pairs={{0,2},{1,3},{2,4},{3,5},{4,6},{5,7},{6,8},{7,9},{8,10},{9,11},{10,... | collective-permute-start | bytes 196616 | tf_op jit(solution)/shard_map/ppermute | solution.py:518
  43.8 0.0 copy-done.3
  43.8 2.6 %collective-permute-start.2 = (f32[16,512]{1,0:T(8,128)S(1)}, f32[16,512]{1,0:T(8,128)S(1)}, u32[]{:S(2)}, u32[]{:S(2)}) collective-permute-start(f32[16,512]{1,0:T(8,128)S(1)} %dynamic-slice_bitcast_fusion), channel_id=1, source_target_pairs={{0,1},{1,0},{2,3},{3,2},{4,5},{5,4},{6,7},{7,6},{8,9},{9,8},{10,11... | collective-permute-start | bytes 98312 | tf_op jit(solution)/shard_map/ppermute | solution.py:522
  46.4 0.0 copy-done.6
  46.4 0.6 broadcast_in_dim.41.bias
  47.0 0.2 collective-permute-done.2.other
  47.3 0.6 copy-done.5
  47.9 2.4 %decay.1 = (f32[4,4,1024]{2,1,0:T(4,128)}, f32[1024,128]{1,0:T(8,128)}, bf16[16,128]{1,0:T(8,128)(2,1)}) custom-call(s32[1]{0:T(128)} %bitcast.core, f32[32,512]{1,0:T(8,128)} %bitcast.18, f32[16,512]{1,0:T(8,128)} %copy-done.5), custom_call_target="tpu_custom_call" | custom-call | tf_op jit(solution)/shard_map/decay/pallas_call | solution.py:469
  50.3 1.5 broadcast_in_dim.39
  51.9 6.0 %norm.1.normed = bf16[1040,2048]{1,0:T(8,128)(2,1)} custom-call(s32[1]{0:T(128)} %bitcast.core, bf16[512,2048]{1,0:T(8,128)(2,1)} %bitcast.15, bf16[512,2048]{1,0:T(8,128)(2,1)} %collective-permute-done.sibling, f32[1,2048]{1,0:T(1,128)} %bitcast.19), custom_call_target="tpu_custom_call" | custom-call | tf_op jit(solution)/shard_map/norm/pallas_call | solution.py:395
  57.8 3.5 %collective-permute-done.1.rows = bf16[16,2048]{1,0:T(8,128)(2,1)S(1)} collective-permute-done((bf16[16,2048]{1,0:T(8,128)(2,1)S(1)}, bf16[16,2048]{1,0:T(8,128)(2,1)S(1)}, u32[]{:S(2)}, u32[]{:S(2)}) %collective-permute-start.1) | collective-permute-done | bytes 65568 | tf_op jit(solution)/shard_map/ppermute | solution.py:518
  61.4 0.0 copy-start.4
  61.4 1.9 all-to-all-done.2.w
  63.3 0.0 copy-start
  63.3 0.0 copy-done.4
  63.3 5.3 %all-to-all-start.1 = ((bf16[16,128,512]{2,1,0:T(8,128)(2,1)}), bf16[16,128,512]{2,1,0:T(8,128)(2,1)}, u32[]{:S(2)}, u32[]{:S(2)}) async-start(bf16[16,128,512]{2,1,0:T(8,128)(2,1)} %broadcast_in_dim.39), calls=%async_computation.1 | async-start | bytes 4194304 | tf_op jit(solution)/shard_map/all_to_all | solution.py:56
  68.6 1.6 tail.1.normed
  70.2 0.0 copy-done
  70.2 4.7 %bc.1.mine = bf16[1024,128]{1,0:T(8,128)(2,1)} custom-call(s32[1]{0:T(128)} %bitcast.core, bf16[1040,2048]{1,0:T(8,128)(2,1)} %tail.1.normed, bf16[16,128,640]{2,1,0:T(8,128)(2,1)} %copy-done, f32[4,2304]{1,0:T(4,128)} %taps.5, f32[1,2304]{1,0:T(1,128)} %broadcast_in_dim.41.bias), custom_call_target="tpu_custom_call" | custom-call | tf_op jit(solution)/shard_map/bc/pallas_call | solution.py:101
  74.9 5.2 %collective-permute-start.3 = (bf16[1024,128]{1,0:T(8,128)(2,1)}, bf16[1024,128]{1,0:T(8,128)(2,1)S(1)}, u32[]{:S(2)}, u32[]{:S(2)}) collective-permute-start(bf16[1024,128]{1,0:T(8,128)(2,1)} %bc.1.mine), channel_id=1, source_target_pairs={{0,1},{1,0},{2,3},{3,2},{4,5},{5,4},{6,7},{7,6},{8,9},{9,8},{10,11... | collective-permute-start | bytes 786440 | tf_op jit(solution)/shard_map/ppermute | solution.py:535
  80.1 1.4 collective-permute-done.3.other
  81.5 0.0 copy-start.1
  81.5 0.7 copy-done.1
  82.2 12.6 %heads.2 = (bf16[1024,1024]{1,0:T(8,128)(2,1)}, bf16[8,144,128]{2,1,0:T(8,128)(2,1)}) custom-call(s32[1]{0:T(128)} %bitcast.core, bf16[1040,2048]{1,0:T(8,128)(2,1)} %tail.1.normed, bf16[16,128,640]{2,1,0:T(8,128)(2,1)} %copy-done, f32[4,2304]{1,0:T(4,128)} %taps.5, f32[1,2304]{1,0:T(1,128)} %broadcast_in_dim.41.bias, bf16[1024,128]{1,0:T(8,128)(2,1)} %bc.1.mine, ...), custom_call_target="tpu_custom_call" | custom-call | tf_op jit(solution)/shard_map/heads/pallas_call | solution.py:212
  94.8 0.2 all-to-all-done.1.w
  94.9 0.0 copy-start.7
  94.9 12.7 %heads.3 = (bf16[1024,1024]{1,0:T(8,128)(2,1)}, bf16[8,144,128]{2,1,0:T(8,128)(2,1)}) custom-call(s32[1]{0:T(128)} %bitcast.core, bf16[1040,2048]{1,0:T(8,128)(2,1)} %tail.1.normed, bf16[16,128,512]{2,1,0:T(8,128)(2,1)} %all-to-all-done.1.w, f32[4,2304]{1,0:T(4,128)} %taps.5, ...), custom_call_target="tpu_custom_call", output_to_operand_aliasing={{0}: (11, {}), {1}: (12, {})} | custom-call | tf_op jit(solution)/shard_map/heads/pallas_call | solution.py:212
  107.6 16.1 %all_to_all.31.parts = bf16[8,144,128]{2,1,0:T(8,128)(2,1)} all-to-all(bf16[8,144,128]{2,1,0:T(8,128)(2,1)} %get-tuple-element.38), channel_id=1, replica_groups={{0,2,4,6,8,10,12,14},{1,3,5,7,9,11,13,15},{16,18,20,22,24,26,28,30},{17..., dimensions={0} | all-to-all | bytes 589824 | tf_op jit(solution)/shard_map/all_to_all | solution.py:548
  123.7 1.7 chain.1
  125.4 3.4 %all-to-all-start.4 = ((bf16[8,128,128]{2,1,0:T(8,128)(2,1)}), bf16[8,128,128]{2,1,0:T(8,128)(2,1)S(1)}, u32[]{:S(2)}, u32[]{:S(2)}) async-start(bf16[8,128,128]{2,1,0:T(8,128)(2,1)} %chain.1), calls=%async_computation.4 | async-start | bytes 524288 | tf_op jit(solution)/shard_map/all_to_all | solution.py:549
  128.9 0.0 copy-done.7
  128.9 0.9 copy.13.order
  129.7 8.5 %all-to-all-done.4.entering = bf16[8,128,128]{2,1,0:T(8,128)(2,1)S(1)} async-done(((bf16[8,128,128]{2,1,0:T(8,128)(2,1)}), bf16[8,128,128]{2,1,0:T(8,128)(2,1)S(1)}, u32[]{:S(2)}, u32[]{:S(2)}) %all-to-all-start.4) | async-done | bytes 262176 | tf_op jit(solution)/shard_map/all_to_all | solution.py:549
  138.2 0.0 copy-start.2
  138.2 0.7 copy-done.2
  138.9 8.6 %finish.1 = bf16[16,2,32,1024]{3,2,1,0:T(8,128)(2,1)} custom-call(s32[1]{0:T(128)} %bitcast.core, bf16[1024,1024]{1,0:T(8,128)(2,1)} %get-tuple-element.37.local, bf16[1024,128]{1,0:T(8,128)(2,1)} %bc.1.mine, bf16[1024,128]{1,0:T(8,128)(2,1)} %copy-done.1, bf16[8,128,128]{2,1,0:T(8,128)(2,1)} %copy-done.2, f32[1024,128]{1,0:T(8,128)} %get-tuple-element.32.columns, ...), custom_call_target="tpu_custom_call" | custom-call | tf_op jit(solution)/shard_map/finish/pallas_call | solution.py:320
  147.5 60.1 %all_to_all.32 = bf16[16,2,32,1024]{3,2,1,0:T(8,128)(2,1)} all-to-all(bf16[16,2,32,1024]{3,2,1,0:T(8,128)(2,1)} %finish.1), channel_id=1, replica_groups=mesh['dp'=32,'seq'=16] {'seq'}, dimensions={0} | all-to-all | bytes 4194304 | tf_op jit(solution)/shard_map/all_to_all | solution.py:553
  207.6 4.4 %regroup.1 = bf16[512,2048]{1,0:T(8,128)(2,1)} custom-call(bf16[8,2,2,32,1024]{4,3,2,1,0:T(8,128)(2,1)} %bitcast.13), custom_call_target="tpu_custom_call" | custom-call | tf_op jit(solution)/shard_map/regroup/pallas_call | solution.py:360
  (6 shorter events, 0.1 us)
Async XLA Ops:
  23.6 20.2 %copy-start.3 = (f32[1,32,512]{2,1,0:T(8,128)S(1)}, f32[1,32,512]{2,1,0:T(8,128)}, u32[]{:S(2)}) copy-start(f32[1,32,512]{2,1,0:T(8,128)} %param.14) | copy-start | bytes 196612
  23.6 22.8 %copy-start.6 = (f32[2304]{0:T(1024)S(1)}, f32[2304]{0:T(1024)}, u32[]{:S(2)}) copy-start(f32[2304]{0:T(1024)} %param.13) | copy-start | bytes 27652
  23.6 39.7 %all-to-all-start.2 = ((bf16[16,128,640]{2,1,0:T(8,128)(2,1)}), bf16[16,128,640]{2,1,0:T(8,128)(2,1)S(1)}, u32[]{:S(2)}, u32[]{:S(2)}) async-start(bf16[16,128,640]{2,1,0:T(8,128)(2,1)} %broadcast_in_dim.38), calls=%async_computation.2 | async-start | bytes 5242880 | tf_op jit(solution)/shard_map/all_to_all | solution.py:56
  31.1 8.2 %collective-permute-start = (bf16[512,2048]{1,0:T(8,128)(2,1)}, bf16[512,2048]{1,0:T(8,128)(2,1)}, u32[]{:S(2)}, u32[]{:S(2)}) collective-permute-start(bf16[512,2048]{1,0:T(8,128)(2,1)} %bitcast.14), channel_id=1, source_target_pairs={{0,1},{1,0},{2,3},{3,2},{4,5},{5,4},{6,7},{7,6},{8,9},{9,8},{10,11... | collective-permute-start | bytes 6291464 | tf_op jit(solution)/shard_map/ppermute | solution.py:516
  40.3 21.1 %collective-permute-start.1 = (bf16[16,2048]{1,0:T(8,128)(2,1)S(1)}, bf16[16,2048]{1,0:T(8,128)(2,1)S(1)}, u32[]{:S(2)}, u32[]{:S(2)}) collective-permute-start(bf16[16,2048]{1,0:T(8,128)(2,1)S(1)} %slice_select_fusion), channel_id=1, source_target_pairs={{0,2},{1,3},{2,4},{3,5},{4,6},{5,7},{6,8},{7,9},{8,10},{9,11},{10,... | collective-permute-start | bytes 196616 | tf_op jit(solution)/shard_map/ppermute | solution.py:518
  43.8 3.4 %collective-permute-start.2 = (f32[16,512]{1,0:T(8,128)S(1)}, f32[16,512]{1,0:T(8,128)S(1)}, u32[]{:S(2)}, u32[]{:S(2)}) collective-permute-start(f32[16,512]{1,0:T(8,128)S(1)} %dynamic-slice_bitcast_fusion), channel_id=1, source_target_pairs={{0,1},{1,0},{2,3},{3,2},{4,5},{5,4},{6,7},{7,6},{8,9},{9,8},{10,11... | collective-permute-start | bytes 98312 | tf_op jit(solution)/shard_map/ppermute | solution.py:522
  47.3 0.6 copy-start.5
  61.4 1.9 copy-start.4
  63.3 6.9 %copy-start = (bf16[16,128,640]{2,1,0:T(8,128)(2,1)}, bf16[16,128,640]{2,1,0:T(8,128)(2,1)S(1)}, u32[]{:S(2)}) copy-start(bf16[16,128,640]{2,1,0:T(8,128)(2,1)S(1)} %all-to-all-done.2.w) | copy-start | bytes 7864324
  63.3 31.7 %all-to-all-start.1 = ((bf16[16,128,512]{2,1,0:T(8,128)(2,1)}), bf16[16,128,512]{2,1,0:T(8,128)(2,1)}, u32[]{:S(2)}, u32[]{:S(2)}) async-start(bf16[16,128,512]{2,1,0:T(8,128)(2,1)} %broadcast_in_dim.39), calls=%async_computation.1 | async-start | bytes 4194304 | tf_op jit(solution)/shard_map/all_to_all | solution.py:56
  74.9 6.6 %collective-permute-start.3 = (bf16[1024,128]{1,0:T(8,128)(2,1)}, bf16[1024,128]{1,0:T(8,128)(2,1)S(1)}, u32[]{:S(2)}, u32[]{:S(2)}) collective-permute-start(bf16[1024,128]{1,0:T(8,128)(2,1)} %bc.1.mine), channel_id=1, source_target_pairs={{0,1},{1,0},{2,3},{3,2},{4,5},{5,4},{6,7},{7,6},{8,9},{9,8},{10,11... | collective-permute-start | bytes 786440 | tf_op jit(solution)/shard_map/ppermute | solution.py:535
  81.5 0.7 copy-start.1
  94.9 33.9 %copy-start.7 = (s32[512]{0:T(512)S(1)}, s32[512]{0:T(512)}, u32[]{:S(2)}) copy-start(s32[512]{0:T(512)} %param.17) | copy-start | bytes 6148
  125.4 12.8 %all-to-all-start.4 = ((bf16[8,128,128]{2,1,0:T(8,128)(2,1)}), bf16[8,128,128]{2,1,0:T(8,128)(2,1)S(1)}, u32[]{:S(2)}, u32[]{:S(2)}) async-start(bf16[8,128,128]{2,1,0:T(8,128)(2,1)} %chain.1), calls=%async_computation.4 | async-start | bytes 524288 | tf_op jit(solution)/shard_map/all_to_all | solution.py:549
  138.2 0.7 copy-start.2
